TPU v7x, 512 devices: a whole 4x4x16 slice. The times are simulated.
512 devices in a mesh: dp: 2 (over z_hi), row: 8 (over y, core), col: 32 (over x, z_lo).
Axes of the slice: x: 4, y: 4, z: 16 (z_hi: 2, z_lo: 8; z = z_hi * 8 + z_lo), core: 2. Of those that a mesh axis runs over, the one named last changes fastest.
Arguments:
- activations: bfloat16 [2048, 16384], P(('dp', 'row'), 'col'), may hold values from -6 to 6
- cotangent: bfloat16 [2048, 16384], P(('dp', 'row'), 'col'), may hold values from -6 to 6
- gate_saved: bfloat16 [2048, 6656], P(('dp', 'col'), 'row'), may hold values from -6 to 6
- up_saved: bfloat16 [2048, 6656], P(('dp', 'col'), 'row'), may hold values from -6 to 6
- w_gate: bfloat16 [16384, 6656], P('col', 'row'), may hold values from -0.046875 to 0.046875
- w_up: bfloat16 [16384, 6656], P('col', 'row'), may hold values from -0.046875 to 0.046875
- w_down: bfloat16 [6656, 16384], P('row', 'col'), may hold values from -0.078125 to 0.078125
- assignment: int32 [4], replicated, may hold values from 0 to 3, each once
- pair_lengths: int32 [8], replicated, may hold values from 1 to 256, 1536 in all
Outputs:
- input_grad: bfloat16 [2048, 16384], P(('dp', 'row'), 'col')
- gate_grad: bfloat16 [16384, 6656], P(('col', 'dp'), 'row')
- up_grad: bfloat16 [16384, 6656], P(('col', 'dp'), 'row')
- down_grad: bfloat16 [6656, 16384], P(('row', 'dp'), 'col')
Inputs may be any that keep to these rules, and one draw needn't show every extreme that they name: `assignment`: each of the 4 pairs stands in exactly one pair slot; pair slot s belongs to batch s // 2. `pair_lengths`: entry 2 p is the live length of pair p's chosen sequence and entry 2 p + 1 that of its rejected one; the largest entry is exactly 256.
All inputs are finite; a program needn't handle non-finite values.
Results may differ from a plain program's by a relative error of at most 0.019.
Values may be sent and summed in bfloat16 or wider, within the bound.
No kernel may reach another device: no remote copies, remote signals or barrier semaphores. Data moves between devices by JAX's collectives and lax.ppermute only.
A program may use at most 64 MiB of HBM per device.

v0:
```python
import jax
import jax.numpy as jnp
from jax import lax
from jax.sharding import PartitionSpec as P

SEQ = 256


def contract_last(left, right):
    return lax.dot_general(
        left, right, (((1,), (1,)), ((), ())), preferred_element_type=jnp.float32
    )


def contract_first(left, right):
    return lax.dot_general(
        left, right, (((0,), (0,)), ((), ())), preferred_element_type=jnp.float32
    )


def live_mask(assignment, pair_lengths, batch_id, row_count):
    seq_count = row_count // SEQ
    seq_index = jnp.arange(seq_count, dtype=jnp.int32)
    slot_ids = batch_id * (seq_count // 2) + seq_index // 2
    slot_table = jnp.arange(assignment.shape[0], dtype=jnp.int32)
    pair_ids = jnp.sum(
        jnp.where(slot_table[None, :] == slot_ids[:, None], assignment[None, :], 0), axis=1
    )
    entry_ids = 2 * pair_ids + seq_index % 2
    entry_table = jnp.arange(pair_lengths.shape[0], dtype=jnp.int32)
    live_len = jnp.sum(
        jnp.where(entry_table[None, :] == entry_ids[:, None], pair_lengths[None, :], 0), axis=1
    )
    position = jnp.arange(row_count, dtype=jnp.int32)
    return position % SEQ < jnp.repeat(live_len, SEQ, total_repeat_length=row_count)


def swiglu_grads(head_grad, gate_vals, up_vals):
    gate_float = gate_vals.astype(jnp.float32)
    up_float = up_vals.astype(jnp.float32)
    sigmoid_gate = jax.nn.sigmoid(gate_float)
    silu_gate = gate_float * sigmoid_gate
    hidden = (silu_gate * up_float).astype(jnp.bfloat16)
    grad_gate = (
        head_grad * up_float * sigmoid_gate * (1.0 + gate_float * (1.0 - sigmoid_gate))
    ).astype(jnp.bfloat16)
    grad_up = (head_grad * silu_gate).astype(jnp.bfloat16)
    return (grad_gate, grad_up, hidden)


def on_device(
    activations, cotangent, gate_saved, up_saved, w_gate, w_up, w_down, assignment, pair_lengths
):
    input_rows, output_grads = (
        lax.all_gather(activations, "row", axis=0, tiled=True),
        lax.all_gather(cotangent, "row", axis=0, tiled=True),
    )
    row_count = input_rows.shape[0]
    batch_id = lax.axis_index("dp")
    live_tokens = live_mask(assignment, pair_lengths, batch_id, row_count)
    masked = jnp.where(live_tokens[:, None], output_grads, jnp.zeros_like(output_grads))
    col_count = lax.axis_size("col")
    head_count = row_count // col_count
    block_term = contract_last(masked, w_down).astype(jnp.bfloat16)
    received = lax.all_to_all(block_term, "col", split_axis=0, concat_axis=0, tiled=True)
    stacked = received.reshape(col_count, head_count, received.shape[1])
    head_grad = jnp.sum(stacked, axis=0, dtype=jnp.float32)
    part_gate, part_up, part_hidden = swiglu_grads(head_grad, gate_saved, up_saved)
    grad_gate, grad_up, hidden = (
        lax.all_gather(part_gate, "col", axis=0, tiled=True),
        lax.all_gather(part_up, "col", axis=0, tiled=True),
        lax.all_gather(part_hidden, "col", axis=0, tiled=True),
    )
    input_grad = lax.psum_scatter(
        (contract_last(grad_gate, w_gate) + contract_last(grad_up, w_up)).astype(jnp.bfloat16),
        "row",
        scatter_dimension=0,
        tiled=True,
    )
    grad_scale = 1.0 / jnp.sqrt(jnp.float32(row_count * lax.axis_size("dp")))
    gate_term = contract_first(input_rows, grad_gate) * grad_scale
    up_term = contract_first(input_rows, grad_up) * grad_scale
    down_term = contract_first(hidden, masked) * grad_scale
    gate_total, up_total, down_total = (
        lax.psum_scatter(
            gate_term.astype(jnp.bfloat16), "dp", scatter_dimension=0, tiled=True
        ).astype(jnp.float32),
        lax.psum_scatter(
            up_term.astype(jnp.bfloat16), "dp", scatter_dimension=0, tiled=True
        ).astype(jnp.float32),
        lax.psum_scatter(
            down_term.astype(jnp.bfloat16), "dp", scatter_dimension=0, tiled=True
        ).astype(jnp.float32),
    )
    return (
        input_grad,
        gate_total.astype(jnp.bfloat16),
        up_total.astype(jnp.bfloat16),
        down_total.astype(jnp.bfloat16),
    )


def solution(mesh):
    return jax.shard_map(
        on_device,
        mesh=mesh,
        in_specs=(
            P(("dp", "row"), "col"),
            P(("dp", "row"), "col"),
            P(("dp", "col"), "row"),
            P(("dp", "col"), "row"),
            P("col", "row"),
            P("col", "row"),
            P("row", "col"),
            P(),
            P(),
        ),
        out_specs=(
            P(("dp", "row"), "col"),
            P(("col", "dp"), "row"),
            P(("col", "dp"), "row"),
            P(("row", "dp"), "col"),
        ),
        check_vma=False,
    )
```

profile of v0, /device:TPU:2, one launch (start us, length us, event | category | flops | bytes accessed | tf_op | source)
XLA Modules:
  0.0 1084.4 jit_solution(2719218604420227594)
XLA Ops:
  7.2 0.7 all-gather.6.cloned.1.call-update
  8.0 0.8 select_reduce_fusion.1
  8.8 0.8 select_reduce_fusion
  9.7 0.6 fusion.18
  10.3 3.3 fusion.10
  13.6 32.0 %all-gather.6.cloned.1.call-done = bf16[1024,512]{1,0:T(8,128)(2,1)} async-done(((bf16[128,512]{1,0:T(8,128)(2,1)}), bf16[1024,512]{1,0:T(8,128)(2,1)}) %all-gather.6.cloned.1.call-update) | async-done | bytes 1048592 | tf_op jit(solution)/shard_map/all_gather | solution.py:56
  45.6 3.6 convolution_convert_fusion
  49.1 3.0 copy.14
  52.2 95.9 %all_to_all.9 = bf16[32,32,832]{2,1,0:T(8,128)(2,1)S(1)} all-to-all(bf16[32,32,832]{2,1,0:T(8,128)(2,1)S(1)} %bitcast.19), channel_id=1, replica_groups=mesh['dp'=2,'row'=8,'col'=32] {'col'}, dimensions={0} | all-to-all | bytes 3407872 | tf_op jit(solution)/shard_map/all_to_all | solution.py:65
  148.9 0.7 multiply_convert_fusion.3
  149.7 0.7 all-gather.12.cloned.1.call-update
  151.6 199.6 %all-gather.14.cloned.1.call-done = bf16[1024,832]{1,0:T(8,128)(2,1)} async-done(((bf16[32,832]{1,0:T(8,128)(2,1)}), bf16[1024,832]{1,0:T(8,128)(2,1)}) %all-gather.14.cloned.1.call-update) | async-done | bytes 1703952 | tf_op jit(solution)/shard_map/all_gather | solution.py:72
  351.2 3.5 multiply_convert_fusion
  354.8 45.7 %all-gather.12.cloned.1.call-done = bf16[1024,512]{1,0:T(8,128)(2,1)} async-done(((bf16[128,512]{1,0:T(8,128)(2,1)}), bf16[1024,512]{1,0:T(8,128)(2,1)}) %all-gather.12.cloned.1.call-update) | async-done | bytes 1048592 | tf_op jit(solution)/shard_map/all_gather | solution.py:55
  400.5 210.0 %all-gather.8.cloned.1.call-done = bf16[1024,832]{1,0:T(8,128)(2,1)} async-done(((bf16[32,832]{1,0:T(8,128)(2,1)}), bf16[1024,832]{1,0:T(8,128)(2,1)}) %all-gather.8.cloned.1.call-update) | async-done | bytes 1703952 | tf_op jit(solution)/shard_map/all_gather | solution.py:70
  610.6 3.8 fusion
  614.4 222.3 %all-gather.10.cloned.1.call-done = bf16[1024,832]{1,0:T(8,128)(2,1)} async-done(((bf16[32,832]{1,0:T(8,128)(2,1)}), bf16[1024,832]{1,0:T(8,128)(2,1)}) %all-gather.10.cloned.1.call-update) | async-done | bytes 1703952 | tf_op jit(solution)/shard_map/all_gather | solution.py:71
  836.7 3.8 fusion.1
  840.6 1.2 fusion.19
  842.3 2.2 add_convert_fusion
  844.6 76.8 %reduce-scatter.11.cloned.1.call-done = bf16[416,512]{1,0:T(8,128)(2,1)} async-done(((bf16[832,512]{1,0:T(8,128)(2,1)}), bf16[416,512]{1,0:T(8,128)(2,1)}) %reduce-scatter.11.cloned.1.call-update) | async-done | bytes 426000 | tf_op jit(solution)/shard_map/reduce_scatter | solution.py:91
  921.4 60.5 %reduce-scatter.7.cloned.1.call-done = bf16[256,832]{0,1:T(8,128)(2,1)} async-done(((bf16[512,832]{0,1:T(8,128)(2,1)}), bf16[256,832]{0,1:T(8,128)(2,1)}) %reduce-scatter.7.cloned.1.call-update) | async-done | bytes 426000 | tf_op jit(solution)/shard_map/reduce_scatter | solution.py:85
  981.9 60.6 %reduce-scatter.9.cloned.1.call-done = bf16[256,832]{0,1:T(8,128)(2,1)} async-done(((bf16[512,832]{0,1:T(8,128)(2,1)}), bf16[256,832]{0,1:T(8,128)(2,1)}) %reduce-scatter.9.cloned.1.call-update) | async-done | bytes 426000 | tf_op jit(solution)/shard_map/reduce_scatter | solution.py:88
  1042.5 35.4 %reduce-scatter.5.cloned.1.call-done = bf16[128,512]{1,0:T(8,128)(2,1)} async-done(((bf16[1024,512]{1,0:T(8,128)(2,1)}), bf16[128,512]{1,0:T(8,128)(2,1)}) %reduce-scatter.5.cloned.1.call-update) | async-done | bytes 131088 | tf_op jit(solution)/shard_map/reduce_scatter | solution.py:74
  (35 shorter events, 2.8 us)
Async XLA Ops:
  7.2 38.4 %copy-start = (bf16[832,512]{1,0:T(8,128)(2,1)S(1)}, bf16[832,512]{1,0:T(8,128)(2,1)}, u32[]{:S(2)}) copy-start(bf16[832,512]{1,0:T(8,128)(2,1)} %param.17) | copy-start | bytes 2555908
  7.2 38.4 %all-gather.6.cloned.1.call-start = ((), (), s32[]{:S(2)}) async-start(), calls=%async_computation.5 | async-start | bytes 1179648 | tf_op jit(solution)/shard_map/all_gather | solution.py:56
  7.9 343.3 %all-gather.14.cloned.1.call-start = ((), (), s32[]{:S(2)}) async-start(), calls=%async_computation.12 | async-start | bytes 1892352 | tf_op jit(solution)/shard_map/all_gather | solution.py:72
  148.1 0.8 copy-start.1
  148.1 0.8 copy-start.2
  148.1 203.1 %copy-start.5 = (bf16[1024,512]{1,0:T(8,128)(2,1)S(1)}, bf16[1024,512]{1,0:T(8,128)(2,1)}, u32[]{:S(2)}) copy-start(bf16[1024,512]{1,0:T(8,128)(2,1)} %all-gather.6.cloned.1.call-done) | copy-start | bytes 3145732
  149.7 250.9 %all-gather.12.cloned.1.call-start = ((), (), s32[]{:S(2)}) async-start(), calls=%async_computation.9 | async-start | bytes 1179648 | tf_op jit(solution)/shard_map/all_gather | solution.py:55
  150.4 460.2 %all-gather.8.cloned.1.call-start = ((), (), s32[]{:S(2)}) async-start(), calls=%async_computation.6 | async-start | bytes 1892352 | tf_op jit(solution)/shard_map/all_gather | solution.py:70
  151.0 685.7 %all-gather.10.cloned.1.call-start = ((), (), s32[]{:S(2)}) async-start(), calls=%async_computation.7 | async-start | bytes 1892352 | tf_op jit(solution)/shard_map/all_gather | solution.py:71
  151.6 769.8 %reduce-scatter.11.cloned.1.call-start = ((), (), s32[]{:S(2)}) async-start(), calls=%async_computation.13 | async-start | bytes 1277952 | tf_op jit(solution)/shard_map/reduce_scatter | solution.py:91
  354.8 627.1 %reduce-scatter.7.cloned.1.call-start = ((), (), s32[]{:S(2)}) async-start(), calls=%async_computation.10 | async-start | bytes 1277952 | tf_op jit(solution)/shard_map/reduce_scatter | solution.py:85
  614.4 226.2 %copy-start.3 = (bf16[1024,832]{1,0:T(8,128)(2,1)S(1)}, bf16[1024,832]{1,0:T(8,128)(2,1)}, u32[]{:S(2)}) copy-start(bf16[1024,832]{1,0:T(8,128)(2,1)} %all-gather.8.cloned.1.call-done) | copy-start | bytes 5111812
  614.4 226.2 %copy-start.6 = (bf16[512,832]{0,1:T(8,128)(2,1)S(1)}, bf16[512,832]{0,1:T(8,128)(2,1)}, u32[]{:S(2)}) copy-start(bf16[512,832]{0,1:T(8,128)(2,1)} %param.15) | copy-start | bytes 2555908
  614.4 428.1 %reduce-scatter.9.cloned.1.call-start = ((), (), s32[]{:S(2)}) async-start(), calls=%async_computation.11 | async-start | bytes 1277952 | tf_op jit(solution)/shard_map/reduce_scatter | solution.py:88
  840.6 237.3 %reduce-scatter.5.cloned.1.call-start = ((), (), s32[]{:S(2)}) async-start(), calls=%async_computation.8 | async-start | bytes 1179648 | tf_op jit(solution)/shard_map/reduce_scatter | solution.py:74
  840.6 1.5 copy-start.4
  840.6 1.7 copy-start.7
Sparse Core Ops, SparseCore 0:
  10.1 35.3 all-gather.5
  149.8 201.3 all-gather.13
  353.4 47.0 all-gather.11
  403.0 207.4 all-gather.7
  613.1 223.6 all-gather.9
  840.0 81.3 reduce-scatter.10
  924.8 57.0 reduce-scatter.6
  985.3 57.1 reduce-scatter.8
  1045.9 31.9 reduce-scatter.4
where the time goes:
time: 1080 us
  waiting for transfers between devices  945 us (88%)
  blocking collectives  95.9 us (9%)
  matrix products  18.2 us (2%)
  between operations  13.9 us (1%)
    all_gather x1, waiting for transfers between devices, on_device(): lax.all_gather(part_up, 'col', axis=0, tiled=True)  222 us
    all_gather x1, waiting for transfers between devices, on_device(): lax.all_gather(part_gate, 'col', axis=0, tiled=True)  210 us
    all_gather x1, waiting for transfers between devices, on_device(): lax.all_gather(part_hidden, 'col', axis=0, tiled=True)  200 us
    all_to_all x1, blocking collectives, on_device(): lax.all_to_all(block_term, 'col', split_axis=0, concat_axis=0, tiled=True)  95.9 us
    reduce_scatter x1, waiting for transfers between devices, on_device(): lax.psum_scatter(down_term.astype(jnp.bfloat16), 'dp', scatter_dimension=...  76.8 us
    reduce_scatter x1, waiting for transfers between devices, on_device(): lax.psum_scatter(up_term.astype(jnp.bfloat16), 'dp', scatter_dimension=0,...  60.6 us
    reduce_scatter x1, waiting for transfers between devices, on_device(): lax.psum_scatter(gate_term.astype(jnp.bfloat16), 'dp', scatter_dimension=...  60.5 us
    all_gather x1, waiting for transfers between devices, on_device(): lax.all_gather(activations, 'row', axis=0, tiled=True)  45.7 us
  transfers between devices with their start and end apart: 9, of which 9 were waited for; matrix products, arithmetic and copies ran while one was open for 2% of the time, Pallas kernels for 0%

commit v1 on v0

v1 whole, which is shorter than its diff:
```python
import jax
import jax.numpy as jnp
from jax import lax
from jax.sharding import Mesh, PartitionSpec as P

SEQ = 256
N_Y, N_CORE, N_X, N_Z = 4, 2, 4, 8


def contract_last(left, right):
    return lax.dot_general(
        left, right, (((1,), (1,)), ((), ())), preferred_element_type=jnp.float32
    )


def contract_first(left, right):
    return lax.dot_general(
        left, right, (((0,), (0,)), ((), ())), preferred_element_type=jnp.float32
    )


def live_mask(assignment, pair_lengths, row_count):
    seq_count = row_count // SEQ
    seq_index = jnp.arange(seq_count, dtype=jnp.int32)
    slot_table = jnp.arange(assignment.shape[0], dtype=jnp.int32)
    pair_ids = jnp.sum(
        jnp.where(slot_table[None, :] == seq_index[:, None] // 2, assignment[None, :], 0), axis=1
    )
    entry_ids = 2 * pair_ids + seq_index % 2
    entry_table = jnp.arange(pair_lengths.shape[0], dtype=jnp.int32)
    live_len = jnp.sum(
        jnp.where(entry_table[None, :] == entry_ids[:, None], pair_lengths[None, :], 0), axis=1
    )
    position = jnp.arange(SEQ, dtype=jnp.int32)
    return position[None, :] < live_len[:, None]


def shift(value, axis, size, step):
    return lax.ppermute(value, axis, [(i, (i + step) % size) for i in range(size)])


def spread(value, axis, size):
    copies = jnp.broadcast_to(value[None], (size,) + value.shape)
    return lax.all_to_all(copies, axis, split_axis=0, concat_axis=0, tiled=True)


def sum_over(value, axis, size):
    blocks = value.reshape(size, value.shape[0] // size, value.shape[1])
    received = lax.all_to_all(blocks, axis, split_axis=0, concat_axis=0, tiled=True)
    return jnp.sum(received, axis=0, dtype=jnp.float32).astype(jnp.bfloat16)


def gather_x(block):
    x = lax.axis_index("x")
    half = block.shape[0] // 2
    left = shift(block, "x", N_X, 1)
    right = shift(block, "x", N_X, -1)
    far_low = shift(left[:half], "x", N_X, 1)
    far_high = shift(right[half:], "x", N_X, -1)
    far = jnp.concatenate([far_low, far_high], axis=0)
    out = jnp.zeros((N_X,) + block.shape, block.dtype)
    for step, part in ((0, block), (N_X - 1, left), (1, right), (2, far)):
        out = lax.dynamic_update_slice_in_dim(out, part[None], (x + step) % N_X, 0)
    return out


def on_device(
    activations, cotangent, gate_saved, up_saved, w_gate, w_up, w_down, assignment, pair_lengths
):
    batch = lax.axis_index("dp")
    rows, width = cotangent.shape
    half = width // 2
    own, ffw = gate_saved.shape
    row_axes = ("y", "core")
    n_row = N_Y * N_CORE
    tok = rows * n_row
    n_dp = 2

    saved = jnp.stack([gate_saved, up_saved])[None]
    saved = lax.all_gather(saved, ("dp", "z"), axis=0, tiled=True)
    saved = lax.all_gather(saved, "x", axis=0, tiled=True)
    saved = saved.reshape(N_X, n_dp, N_Z, 2, own, ffw)

    act_own = lax.dynamic_slice_in_dim(activations, batch * half, half, 1)
    act_other = lax.dynamic_slice_in_dim(activations, (1 - batch) * half, half, 1)
    partner = shift(jnp.concatenate([cotangent, act_other], axis=1), "dp", n_dp, 1)

    live = live_mask(assignment, pair_lengths, n_dp * tok).reshape(n_dp, tok)
    live_own = lax.dynamic_index_in_dim(live, batch, 0, keepdims=False)
    live_away = lax.dynamic_index_in_dim(live, 1 - batch, 0, keepdims=False)

    cot_own = spread(cotangent, row_axes, n_row).reshape(tok, width)
    zero = jnp.zeros((), cotangent.dtype)
    masked_own = jnp.where(live_own[:, None], cot_own, zero)
    block_term = contract_last(masked_own, w_down).astype(jnp.bfloat16)
    head = sum_over(block_term, "x", N_X)
    head, partner = lax.optimization_barrier((head, partner))
    head = sum_over(head, "z", N_Z)
    head = lax.all_gather(head, ("dp", "z"), axis=0, tiled=True)
    head = gather_x(head).reshape(N_X, n_dp, N_Z, own, ffw)

    rest = jnp.concatenate([partner, act_own], axis=1)
    rest = lax.all_gather(rest, row_axes, axis=0, tiled=True)
    masked_away = jnp.where(live_away[:, None], rest[:, :width], zero)
    act_away = rest[:, width : width + half]
    act_here = rest[:, width + half :]

    head_f = head.astype(jnp.float32)
    gate = saved[:, :, :, 0].astype(jnp.float32)
    up = saved[:, :, :, 1].astype(jnp.float32)
    sig = jax.nn.sigmoid(gate)
    silu = gate * sig
    hidden = (silu * up).astype(jnp.bfloat16)
    grad_gate = (head_f * up * sig * (1.0 + gate * (1.0 - sig))).astype(jnp.bfloat16)
    grad_up = (head_f * silu).astype(jnp.bfloat16)

    def of_batch(value, index):
        part = lax.dynamic_index_in_dim(value, index, 1, keepdims=False)
        return part.reshape(tok, ffw)

    gg_own, gg_away = of_batch(grad_gate, batch), of_batch(grad_gate, 1 - batch)
    gu_own, gu_away = of_batch(grad_up, batch), of_batch(grad_up, 1 - batch)
    f_half = ffw // 2
    hid_own = lax.dynamic_slice_in_dim(of_batch(hidden, batch), batch * f_half, f_half, 1)
    hid_away = lax.dynamic_slice_in_dim(of_batch(hidden, 1 - batch), batch * f_half, f_half, 1)

    term = (contract_last(gg_own, w_gate) + contract_last(gu_own, w_up)).astype(jnp.bfloat16)
    input_grad = sum_over(term, row_axes, n_row)

    scale = 1.0 / jnp.sqrt(jnp.float32(n_dp * tok))
    gate_grad = (contract_first(act_here, gg_own) + contract_first(act_away, gg_away)) * scale
    up_grad = (contract_first(act_here, gu_own) + contract_first(act_away, gu_away)) * scale
    down_grad = (contract_first(hid_own, masked_own) + contract_first(hid_away, masked_away)) * scale
    return (
        input_grad,
        gate_grad.astype(jnp.bfloat16),
        up_grad.astype(jnp.bfloat16),
        down_grad.astype(jnp.bfloat16),
    )


def solution(mesh):
    fine = Mesh(
        mesh.devices.reshape(2, N_Y, N_CORE, N_X, N_Z), ("dp", "y", "core", "x", "z")
    )
    row, col = ("y", "core"), ("x", "z")
    return jax.shard_map(
        on_device,
        mesh=fine,
        in_specs=(
            P(("dp",) + row, col),
            P(("dp",) + row, col),
            P(("dp",) + col, row),
            P(("dp",) + col, row),
            P(col, row),
            P(col, row),
            P(row, col),
            P(),
            P(),
        ),
        out_specs=(
            P(("dp",) + row, col),
            P(col + ("dp",), row),
            P(col + ("dp",), row),
            P(row + ("dp",), col),
        ),
        check_vma=False,
    )
```

time: 1080 us -> 306 us (0.28)
  the two profiles are of different devices: /device:TPU:2 before, /device:TPU:38 now
where the time goes in v1:
time: 306 us; the launch traced here: 305 us
  waiting for transfers between devices  144 us (47%)
  blocking collectives  63.5 us (21%)
  starting transfers between devices  32.8 us (11%)
  local copies, waits for them, and re-layouts  18.7 us (6%)
  matrix products  17.2 us (6%)
  other arithmetic  14.6 us (5%)
  between operations  14.2 us (5%)
    all_gather x1, waiting for transfers between devices, on_device(): saved = lax.all_gather(saved, ('dp', 'z'), axis=0, tiled=True)  78.1 us
    all_to_all x2, waiting for transfers between devices, sum_over(): lax.all_to_all(blocks, axis, split_axis=0, concat_axis=0, tiled=True)  34.2 us
    all_gather x1, blocking collectives, on_device(): head = lax.all_gather(head, ('dp', 'z'), axis=0, tiled=True)  33.5 us
    all_to_all x1, blocking collectives, sum_over(): lax.all_to_all(blocks, axis, split_axis=0, concat_axis=0, tiled=True)  30 us
    ppermute x5, starting transfers between devices, shift(): lax.ppermute(value, axis, [(i, (i + step) % size) for i in range(size)])  19 us
    ppermute x5, waiting for transfers between devices, shift(): lax.ppermute(value, axis, [(i, (i + step) % size) for i in range(size)])  16 us
    all_to_all x1, waiting for transfers between devices, spread(): return lax.all_to_all(copies, axis, split_axis=0, concat_axis=0, tiled=True)  15.4 us
    dot_general x6, matrix products, contract_first(): lax.dot_general(left, right, (((0,), (0,)), ((), ())), preferred_element_...  12.6 us
  transfers between devices with their start and end apart: 11, of which 7 were waited for; matrix products, arithmetic and copies ran while one was open for 15% of the time, Pallas kernels for 0%

profile of v1, /device:TPU:38, one launch (start us, length us, event | category | flops | bytes accessed | tf_op | source)
XLA Modules:
  0.0 304.8 jit_solution(11381241807909773325)
XLA Ops:
  8.9 78.1 %all-gather.9.cloned.1.call-done = bf16[32,32,832]{2,1,0:T(8,128)(2,1)} async-done(((bf16[2,32,832]{2,1,0:T(8,128)(2,1)}), bf16[32,32,832]{2,1,0:T(8,128)(2,1)}) %all-gather.9.cloned.1.call-update) | async-done | bytes 1703952 | tf_op jit(solution)/shard_map/all_gather | solution.py:80
  88.2 4.3 %all-to-all-start = ((bf16[8,128,512]{2,1,0:T(8,128)(2,1)}), bf16[8,128,512]{2,1,0:T(8,128)(2,1)S(1)}, u32[]{:S(2)}, u32[]{:S(2)}) async-start(bf16[8,128,512]{2,1,0:T(8,128)(2,1)} %broadcast_in_dim.87), calls=%async_computation | async-start | bytes 2097152 | tf_op jit(solution)/shard_map/all_to_all | solution.py:44
  93.1 15.4 %all-to-all-done = bf16[8,128,512]{2,1,0:T(8,128)(2,1)S(1)} async-done(((bf16[8,128,512]{2,1,0:T(8,128)(2,1)}), bf16[8,128,512]{2,1,0:T(8,128)(2,1)S(1)}, u32[]{:S(2)}, u32[]{:S(2)}) %all-to-all-start) | async-done | bytes 1048608 | tf_op jit(solution)/shard_map/all_to_all | solution.py:44
  111.1 4.9 %all-to-all-start.1 = ((bf16[4,256,832]{1,2,0:T(8,128)(2,1)}), bf16[4,256,832]{1,2,0:T(8,128)(2,1)S(1)}, u32[]{:S(2)}, u32[]{:S(2)}) async-start(bf16[4,256,832]{1,2,0:T(8,128)(2,1)} %bitcast.72), calls=%async_computation.1 | async-start | bytes 3407872 | tf_op jit(solution)/shard_map/all_to_all | solution.py:49
  116.7 7.3 %collective-permute-start = (bf16[128,768]{1,0:T(8,128)(2,1)S(1)}, bf16[128,768]{1,0:T(8,128)(2,1)}, u32[]{:S(2)}, u32[]{:S(2)}) collective-permute-start(bf16[128,768]{1,0:T(8,128)(2,1)S(1)} %pad_maximum_fusion.1), channel_id=1, source_target_pairs={{0,256},{256,0},{1,257},{257,1},{2,258},{258,2},{3,259},{259,3},{4... | collective-permute-start | bytes 589832 | tf_op jit(solution)/shard_map/ppermute | solution.py:39
  124.0 31.2 %all-to-all-done.1 = bf16[4,256,832]{1,2,0:T(8,128)(2,1)S(1)} async-done(((bf16[4,256,832]{1,2,0:T(8,128)(2,1)}), bf16[4,256,832]{1,2,0:T(8,128)(2,1)S(1)}, u32[]{:S(2)}, u32[]{:S(2)}) %all-to-all-start.1) | async-done | bytes 1703968 | tf_op jit(solution)/shard_map/all_to_all | solution.py:49
  156.0 30.0 %all_to_all.20 = bf16[8,32,832]{2,1,0:T(8,128)(2,1)S(1)} all-to-all(bf16[8,32,832]{2,1,0:T(8,128)(2,1)S(1)} %bitcast.74), channel_id=1, replica_groups=mesh['dp'=2,'y'=4,'core'=2,'x'=4,'z'=8] {'z'}, dimensions={0} | all-to-all | bytes 851968 | tf_op jit(solution)/shard_map/all_to_all | solution.py:49
  186.1 33.5 %all_gather.12 = bf16[512,832]{1,0:T(8,128)(2,1)S(1)} all-gather(bf16[32,832]{1,0:T(8,128)(2,1)S(1)} %reduce_sum.57), channel_id=1, replica_groups=mesh['dp'=2,'y'=4,'core'=2,'x'=4,'z'=8] {'dp','z'}, dimensions={0}, use_global_device_ids=true | all-gather | bytes 905216 | tf_op jit(solution)/shard_map/all_gather | solution.py:99
  220.1 4.0 %collective-permute-start.1 = (bf16[512,832]{0,1:T(8,128)(2,1)S(1)}, bf16[512,832]{0,1:T(8,128)(2,1)S(1)}, u32[]{:S(2)}, u32[]{:S(2)}) collective-permute-start(bf16[512,832]{0,1:T(8,128)(2,1)S(1)} %copy.30), channel_id=1, source_target_pairs={{0,8},{8,16},{16,24},{24,0},{1,9},{9,17},{17,25},{25,1},{2,10},{10... | collective-permute-start | bytes 2555912 | tf_op jit(solution)/shard_map/ppermute | solution.py:39
  227.8 2.2 broadcast_in_dim.80
  231.0 8.4 %collective-permute-done.1 = bf16[512,832]{0,1:T(8,128)(2,1)S(1)} collective-permute-done((bf16[512,832]{0,1:T(8,128)(2,1)S(1)}, bf16[512,832]{0,1:T(8,128)(2,1)S(1)}, u32[]{:S(2)}, u32[]{:S(2)}) %collective-permute-start.1) | collective-permute-done | bytes 852000 | tf_op jit(solution)/shard_map/ppermute | solution.py:39
  240.8 4.0 %collective-permute-start.3 = (bf16[256,832]{1,0:T(8,128)(2,1)}, bf16[256,832]{1,0:T(8,128)(2,1)}, u32[]{:S(2)}, u32[]{:S(2)}) collective-permute-start(bf16[256,832]{1,0:T(8,128)(2,1)} %slice.28), channel_id=1, source_target_pairs={{0,8},{8,16},{16,24},{24,0},{1,9},{9,17},{17,25},{25,1},{2,10},{10... | collective-permute-start | bytes 1277960 | tf_op jit(solution)/shard_map/ppermute | solution.py:39
  249.4 2.1 collective-permute-done.3
  251.4 5.5 %collective-permute-done.4 = bf16[256,832]{1,0:T(8,128)(2,1)S(1)} collective-permute-done((bf16[256,832]{1,0:T(8,128)(2,1)S(1)}, bf16[256,832]{1,0:T(8,128)(2,1)S(1)}, u32[]{:S(2)}, u32[]{:S(2)}) %collective-permute-start.4) | collective-permute-done | bytes 426016 | tf_op jit(solution)/shard_map/ppermute | solution.py:39
  257.0 2.1 fusion.19
  259.1 3.8 %copy.36 = bf16[64,2,32,832]{3,2,0,1:T(8,128)(2,1)S(1)} copy(bf16[64,2,32,832]{3,2,1,0:T(8,128)(2,1)} %all-gather.5.cloned.1.call-done) | data formatting | bytes 13631488 | tf_op jit(solution)/shard_map/all_gather | solution.py:81
  262.9 6.1 %fusion = (bf16[4,2,8,32,832]{4,3,2,1,0:T(8,128)(2,1)S(1)}, bf16[4,2,8,32,832]{4,3,2,1,0:T(8,128)(2,1)S(1)}, bf16[4,2,8,32,832]{4,3,2,1,0:T(8,128)(2,1)S(1)}) fusion(bf16[4,2,8,32,832]{4,3,2,1,0:T(8,128)(2,1)} %bitcast.15, bf16[4,2,8,2,32,832]{5,4,2,1,0,3:T(8,128)(2,1)S(1)} %bitcast.65), kind=kLoop, calls=%fused_computation.6 | loop fusion | flops 30670848 | bytes 20447232 | tf_op jit(solution)/shard_map/convert_element_type | solution.py:115
  269.3 2.6 constant_dynamic-slice_fusion
  273.8 2.2 add_convert_fusion
  276.0 4.4 %all-to-all-start.3 = ((bf16[8,128,512]{2,1,0:T(8,128)(2,1)}), bf16[8,128,512]{2,1,0:T(8,128)(2,1)}, u32[]{:S(2)}, u32[]{:S(2)}) async-start(bf16[8,128,512]{2,1,0:T(8,128)(2,1)} %bitcast.78), calls=%async_computation.3 | async-start | bytes 2097152 | tf_op jit(solution)/shard_map/all_to_all | solution.py:49
  280.4 2.7 fusion.16
  283.1 2.6 fusion.23
  287.9 2.1 fusion.12
  293.2 3.0 all-to-all-done.3
  (80 shorter events, 28.1 us)
Async XLA Ops:
  7.2 101.5 %copy-start = (bf16[832,512]{1,0:T(8,128)(2,1)S(1)}, bf16[832,512]{1,0:T(8,128)(2,1)}, u32[]{:S(2)}) copy-start(bf16[832,512]{1,0:T(8,128)(2,1)} %param.15) | copy-start | bytes 2555908
  7.2 79.9 %copy-start.9 = (bf16[128,512]{1,0:T(8,128)(2,1)S(1)}, bf16[128,512]{1,0:T(8,128)(2,1)}, u32[]{:S(2)}) copy-start(bf16[128,512]{1,0:T(8,128)(2,1)} %param.10) | copy-start | bytes 393220
  7.2 79.8 %all-gather.9.cloned.1.call-start = ((), (), s32[]{:S(2)}) async-start(), calls=%async_computation.6 | async-start | bytes 1949696 | tf_op jit(solution)/shard_map/all_gather | solution.py:80
  8.9 250.2 %all-gather.5.cloned.1.call-start = ((), (), s32[]{:S(2)}) async-start(), calls=%async_computation.4 | async-start | bytes 9175040 | tf_op jit(solution)/shard_map/all_gather | solution.py:81
  87.1 5.5 %copy-start.14 = (s32[4]{0:T(128)S(1)}, s32[4]{0:T(128)}, u32[]{:S(2)}) copy-start(s32[4]{0:T(128)} %param.16) | copy-start | bytes 52
  87.1 5.5 %copy-start.15 = (s32[8]{0:T(128)S(1)}, s32[8]{0:T(128)}, u32[]{:S(2)}) copy-start(s32[8]{0:T(128)} %param.17) | copy-start | bytes 100
  88.2 20.2 %all-to-all-start = ((bf16[8,128,512]{2,1,0:T(8,128)(2,1)}), bf16[8,128,512]{2,1,0:T(8,128)(2,1)S(1)}, u32[]{:S(2)}, u32[]{:S(2)}) async-start(bf16[8,128,512]{2,1,0:T(8,128)(2,1)} %broadcast_in_dim.87), calls=%async_computation | async-start | bytes 2097152 | tf_op jit(solution)/shard_map/all_to_all | solution.py:44
  111.1 4.9 %copy-start.11 = (bf16[128,512]{1,0:T(8,128)(2,1)S(1)}, bf16[128,512]{1,0:T(8,128)(2,1)}, u32[]{:S(2)}) copy-start(bf16[128,512]{1,0:T(8,128)(2,1)} %param.9) | copy-start | bytes 393220
  111.1 44.1 %all-to-all-start.1 = ((bf16[4,256,832]{1,2,0:T(8,128)(2,1)}), bf16[4,256,832]{1,2,0:T(8,128)(2,1)S(1)}, u32[]{:S(2)}, u32[]{:S(2)}) async-start(bf16[4,256,832]{1,2,0:T(8,128)(2,1)} %bitcast.72), calls=%async_computation.1 | async-start | bytes 3407872 | tf_op jit(solution)/shard_map/all_to_all | solution.py:49
  116.1 167.0 %all-gather.7.cloned.1.call-start = ((), (), s32[]{:S(2)}) async-start(), calls=%async_computation.5 | async-start | bytes 2359296 | tf_op jit(solution)/shard_map/all_gather | solution.py:103
  116.7 39.0 %collective-permute-start = (bf16[128,768]{1,0:T(8,128)(2,1)S(1)}, bf16[128,768]{1,0:T(8,128)(2,1)}, u32[]{:S(2)}, u32[]{:S(2)}) collective-permute-start(bf16[128,768]{1,0:T(8,128)(2,1)S(1)} %pad_maximum_fusion.1), channel_id=1, source_target_pairs={{0,256},{256,0},{1,257},{257,1},{2,258},{258,2},{3,259},{259,3},{4... | collective-permute-start | bytes 589832 | tf_op jit(solution)/shard_map/ppermute | solution.py:39
  156.0 70.1 %copy-start.10 = (bf16[128,256]{1,0:T(8,128)(2,1)S(1)}, bf16[128,256]{1,0:T(8,128)(2,1)}, u32[]{:S(2)}) copy-start(bf16[128,256]{1,0:T(8,128)(2,1)} %get-tuple-element.19) | copy-start | bytes 196612
  220.1 19.2 %collective-permute-start.1 = (bf16[512,832]{0,1:T(8,128)(2,1)S(1)}, bf16[512,832]{0,1:T(8,128)(2,1)S(1)}, u32[]{:S(2)}, u32[]{:S(2)}) collective-permute-start(bf16[512,832]{0,1:T(8,128)(2,1)S(1)} %copy.30), channel_id=1, source_target_pairs={{0,8},{8,16},{16,24},{24,0},{1,9},{9,17},{17,25},{25,1},{2,10},{10... | collective-permute-start | bytes 2555912 | tf_op jit(solution)/shard_map/ppermute | solution.py:39
  224.1 20.6 %collective-permute-start.2 = (bf16[512,832]{0,1:T(8,128)(2,1)S(1)}, bf16[512,832]{0,1:T(8,128)(2,1)S(1)}, u32[]{:S(2)}, u32[]{:S(2)}) collective-permute-start(bf16[512,832]{0,1:T(8,128)(2,1)S(1)} %copy.30), channel_id=1, source_target_pairs={{0,24},{8,0},{16,8},{24,16},{1,25},{9,1},{17,9},{25,17},{2,26},{10... | collective-permute-start | bytes 2555912 | tf_op jit(solution)/shard_map/ppermute | solution.py:39
  240.8 10.7 %collective-permute-start.3 = (bf16[256,832]{1,0:T(8,128)(2,1)}, bf16[256,832]{1,0:T(8,128)(2,1)}, u32[]{:S(2)}, u32[]{:S(2)}) collective-permute-start(bf16[256,832]{1,0:T(8,128)(2,1)} %slice.28), channel_id=1, source_target_pairs={{0,8},{8,16},{16,24},{24,0},{1,9},{9,17},{17,25},{25,1},{2,10},{10... | collective-permute-start | bytes 1277960 | tf_op jit(solution)/shard_map/ppermute | solution.py:39
  245.4 11.6 %collective-permute-start.4 = (bf16[256,832]{1,0:T(8,128)(2,1)S(1)}, bf16[256,832]{1,0:T(8,128)(2,1)S(1)}, u32[]{:S(2)}, u32[]{:S(2)}) collective-permute-start(bf16[256,832]{1,0:T(8,128)(2,1)S(1)} %slice.29), channel_id=1, source_target_pairs={{0,24},{8,0},{16,8},{24,16},{1,25},{9,1},{17,9},{25,17},{2,26},{10... | collective-permute-start | bytes 1277960 | tf_op jit(solution)/shard_map/ppermute | solution.py:39
  269.3 3.0 copy-start.2
  269.3 3.0 copy-start.12
  276.0 20.2 %all-to-all-start.3 = ((bf16[8,128,512]{2,1,0:T(8,128)(2,1)}), bf16[8,128,512]{2,1,0:T(8,128)(2,1)}, u32[]{:S(2)}, u32[]{:S(2)}) async-start(bf16[8,128,512]{2,1,0:T(8,128)(2,1)} %bitcast.78), calls=%async_computation.3 | async-start | bytes 2097152 | tf_op jit(solution)/shard_map/all_to_all | solution.py:49
  283.1 2.7 copy-start.3
  283.1 4.7 %copy-start.7 = (bf16[4,1,8,32,832]{4,3,2,1,0:T(8,128)(2,1)S(1)}, bf16[4,1,8,32,832]{4,3,2,1,0:T(8,128)(2,1)}, u32[]{:S(2)}) copy-start(bf16[4,1,8,32,832]{4,3,2,1,0:T(8,128)(2,1)} %get-tuple-element.13) | copy-start | bytes 5111812
  285.8 2.1 copy-start.6
  287.9 2.1 copy-start.4
  291.6 6.7 %copy-start.1 = (bf16[832,512]{1,0:T(8,128)(2,1)S(1)}, bf16[832,512]{1,0:T(8,128)(2,1)}, u32[]{:S(2)}) copy-start(bf16[832,512]{1,0:T(8,128)(2,1)} %param.15) | copy-start | bytes 2555908
  (3 other events, 4.2 us)
Sparse Core Ops, SparseCore 0:
  10.7 76.3 all-gather.8
  89.1 95.8 all-gather.4
  227.9 27.1 all-gather.6

commit v2 on v1

v2 whole, which is shorter than its diff:
```python
import jax
import jax.numpy as jnp
from jax import lax
from jax.sharding import Mesh, PartitionSpec as P

SEQ = 256
N_Y, N_CORE, N_X, N_Z = 4, 2, 4, 8


def contract_last(left, right):
    return lax.dot_general(
        left, right, (((1,), (1,)), ((), ())), preferred_element_type=jnp.float32
    )


def contract_first(left, right):
    return lax.dot_general(
        left, right, (((0,), (0,)), ((), ())), preferred_element_type=jnp.float32
    )


def live_mask(assignment, pair_lengths, row_count):
    seq_count = row_count // SEQ
    seq_index = jnp.arange(seq_count, dtype=jnp.int32)
    slot_table = jnp.arange(assignment.shape[0], dtype=jnp.int32)
    pair_ids = jnp.sum(
        jnp.where(slot_table[None, :] == seq_index[:, None] // 2, assignment[None, :], 0), axis=1
    )
    entry_ids = 2 * pair_ids + seq_index % 2
    entry_table = jnp.arange(pair_lengths.shape[0], dtype=jnp.int32)
    live_len = jnp.sum(
        jnp.where(entry_table[None, :] == entry_ids[:, None], pair_lengths[None, :], 0), axis=1
    )
    position = jnp.arange(SEQ, dtype=jnp.int32)
    return position[None, :] < live_len[:, None]


def shift(value, axis, size, step):
    return lax.ppermute(value, axis, [(i, (i + step) % size) for i in range(size)])


def spread(value, axis, size):
    copies = jnp.broadcast_to(value[None], (size,) + value.shape)
    return lax.all_to_all(copies, axis, split_axis=0, concat_axis=0, tiled=True)


def sum_over(value, axis, size):
    blocks = value.reshape(size, value.shape[0] // size, value.shape[1])
    received = lax.all_to_all(blocks, axis, split_axis=0, concat_axis=0, tiled=True)
    return jnp.sum(received, axis=0, dtype=jnp.float32).astype(jnp.bfloat16)


def gather_x(block):
    x = lax.axis_index("x")
    left, right = shift(block, "x", N_X, 1), shift(block, "x", N_X, -1)
    far_low, far_high = shift(left[0], "x", N_X, 1), shift(right[1], "x", N_X, -1)
    outs = []
    for side, far in ((0, far_low), (1, far_high)):
        out = jnp.zeros((N_X,) + block.shape[1:], block.dtype)
        for step, part in ((0, block[side]), (N_X - 1, left[side]), (1, right[side]), (2, far)):
            out = lax.dynamic_update_slice_in_dim(out, part[None], (x + step) % N_X, 0)
        outs.append(out)
    return outs


def on_device(
    activations, cotangent, gate_saved, up_saved, w_gate, w_up, w_down, assignment, pair_lengths
):
    batch = lax.axis_index("dp")
    rows, width = cotangent.shape
    half = width // 2
    own, ffw = gate_saved.shape
    row_axes = ("y", "core")
    n_row = N_Y * N_CORE
    tok = rows * n_row
    n_dp = 2
    away = 1 - batch

    def pick(value, index):
        return lax.dynamic_index_in_dim(value, index, 0, keepdims=False)

    act_own = lax.dynamic_slice_in_dim(activations, batch * half, half, 1)
    act_other = lax.dynamic_slice_in_dim(activations, away * half, half, 1)
    partner = shift(jnp.concatenate([cotangent, act_other], axis=1), "dp", n_dp, 1)

    saved = jnp.stack([gate_saved, up_saved])[None]
    saved = lax.all_gather(saved, ("dp", "z"), axis=0, tiled=True)

    live = live_mask(assignment, pair_lengths, n_dp * tok).reshape(n_dp, tok)
    zero = jnp.zeros((), cotangent.dtype)

    cot_own = spread(cotangent, row_axes, n_row).reshape(tok, width)
    masked_own = jnp.where(pick(live, batch)[:, None], cot_own, zero)
    block_term = contract_last(masked_own, w_down).astype(jnp.bfloat16)
    head_x = sum_over(block_term, "x", N_X)
    _, saved, partner = lax.optimization_barrier((head_x, saved, partner))
    saved = saved.reshape(n_dp, N_Z, 2, own, ffw)
    saved_own = pick(saved, batch).transpose(1, 0, 2, 3).reshape(2, N_Z * own, ffw)
    saved_away = pick(saved, away).transpose(1, 0, 2, 3).reshape(2, N_Z * own, ffw)
    saved_own, saved_away = gather_x(jnp.stack([saved_own, saved_away]))

    rest = jnp.concatenate([partner, act_own], axis=1)
    rest = lax.all_gather(rest, row_axes, axis=0, tiled=True)
    masked_away = jnp.where(pick(live, away)[:, None], rest[:, :width], zero)
    act_away = rest[:, width : width + half]
    act_here = rest[:, width + half :]

    def factors(pair):
        gate = pair[:, 0].astype(jnp.float32).reshape(tok, ffw)
        up = pair[:, 1].astype(jnp.float32).reshape(tok, ffw)
        sig = jax.nn.sigmoid(gate)
        silu = gate * sig
        slope = (up * sig * (1.0 + gate * (1.0 - sig))).astype(jnp.bfloat16)
        hidden = (silu * up).astype(jnp.bfloat16)
        return lax.optimization_barrier((slope, silu.astype(jnp.bfloat16), hidden))

    slope_own, silu_own, hid_own = factors(saved_own)
    slope_away, silu_away, hid_away = factors(saved_away)

    head = sum_over(head_x, "z", N_Z)
    head = lax.all_gather(head, ("dp", "z"), axis=0, tiled=True)
    head = head.reshape(n_dp, N_Z * own, ffw)
    head_own, head_away = pick(head, batch), pick(head, away)
    halves = (2, N_Z * own // 2, ffw)
    head_own = jnp.concatenate(gather_x(head_own.reshape(halves)), axis=1)
    head_away = jnp.concatenate(gather_x(head_away.reshape(halves)), axis=1)

    def times(head_rows, factor):
        value = head_rows.reshape(tok, ffw).astype(jnp.float32) * factor.astype(jnp.float32)
        return value.astype(jnp.bfloat16)

    gg_own, gu_own = times(head_own, slope_own), times(head_own, silu_own)
    gg_away, gu_away = times(head_away, slope_away), times(head_away, silu_away)
    term = (contract_last(gg_own, w_gate) + contract_last(gu_own, w_up)).astype(jnp.bfloat16)
    input_grad = sum_over(term, row_axes, n_row)

    scale = 1.0 / jnp.sqrt(jnp.float32(n_dp * tok))
    f_half = ffw // 2
    hid_own = lax.dynamic_slice_in_dim(hid_own, batch * f_half, f_half, 1)
    hid_away = lax.dynamic_slice_in_dim(hid_away, batch * f_half, f_half, 1)
    down_grad = (contract_first(hid_own, masked_own) + contract_first(hid_away, masked_away)) * scale
    gate_grad = (contract_first(act_here, gg_own) + contract_first(act_away, gg_away)) * scale
    up_grad = (contract_first(act_here, gu_own) + contract_first(act_away, gu_away)) * scale
    return (
        input_grad,
        gate_grad.astype(jnp.bfloat16),
        up_grad.astype(jnp.bfloat16),
        down_grad.astype(jnp.bfloat16),
    )


def solution(mesh):
    fine = Mesh(
        mesh.devices.reshape(2, N_Y, N_CORE, N_X, N_Z), ("dp", "y", "core", "x", "z")
    )
    row, col = ("y", "core"), ("x", "z")

    return jax.shard_map(
        on_device,
        mesh=fine,
        in_specs=(
            P(("dp",) + row, col),
            P(("dp",) + row, col),
            P(("dp",) + col, row),
            P(("dp",) + col, row),
            P(col, row),
            P(col, row),
            P(row, col),
            P(),
            P(),
        ),
        out_specs=(
            P(("dp",) + row, col),
            P(col + ("dp",), row),
            P(col + ("dp",), row),
            P(row + ("dp",), col),
        ),
        check_vma=False,
    )
```

time: 306 us -> 299 us (0.977)
  the two profiles are of different devices: /device:TPU:38 before, /device:TPU:1 now
where the time goes in v2:
time: 299 us; the launch traced here: 297 us
  starting transfers between devices  81.1 us (27%)
  waiting for transfers between devices  74.7 us (25%)
  local copies, waits for them, and re-layouts  49.3 us (16%)
  blocking collectives  46.9 us (16%)
  other arithmetic  16.3 us (5%)
  between operations  14.7 us (5%)
  matrix products  14.5 us (5%)
    all_gather x1, blocking collectives, on_device(): head = lax.all_gather(head, ('dp', 'z'), axis=0, tiled=True)  46.9 us
    ppermute x13, starting transfers between devices, shift(): lax.ppermute(value, axis, [(i, (i + step) % size) for i in range(size)])  45.7 us
    ppermute x13, waiting for transfers between devices, shift(): lax.ppermute(value, axis, [(i, (i + step) % size) for i in range(size)])  32.3 us
    all_to_all x3, waiting for transfers between devices, sum_over(): lax.all_to_all(blocks, axis, split_axis=0, concat_axis=0, tiled=True)  28.6 us
    all_to_all x3, starting transfers between devices, sum_over(): lax.all_to_all(blocks, axis, split_axis=0, concat_axis=0, tiled=True)  25.1 us
    all_to_all x1, waiting for transfers between devices, spread(): return lax.all_to_all(copies, axis, split_axis=0, concat_axis=0, tiled=True)  13.7 us
    dynamic_update_slice x17, local copies, waits for them, and re-layouts, gather_x(): out = lax.dynamic_update_slice_in_dim(out, part[None], (x + step) % N_X, 0)  12 us
    all_to_all x1, starting transfers between devices, spread(): return lax.all_to_all(copies, axis, split_axis=0, concat_axis=0, tiled=True)  10.3 us
  transfers between devices with their start and end apart: 19, of which 9 were waited for; matrix products, arithmetic and copies ran while one was open for 23% of the time, Pallas kernels for 0%

profile of v2, /device:TPU:1, one launch (start us, length us, event | category | flops | bytes accessed | tf_op | source)
XLA Modules:
  0.0 297.4 jit_solution(7502947241557582860)
XLA Ops:
  9.3 10.3 %all-to-all-start = ((bf16[8,128,512]{2,1,0:T(8,128)(2,1)}), bf16[8,128,512]{2,1,0:T(8,128)(2,1)S(1)}, u32[]{:S(2)}, u32[]{:S(2)}) async-start(bf16[8,128,512]{2,1,0:T(8,128)(2,1)} %broadcast_in_dim.89), calls=%async_computation | async-start | bytes 2097152 | tf_op jit(solution)/shard_map/all_to_all | solution.py:44
  20.9 13.7 %all-to-all-done = bf16[8,128,512]{2,1,0:T(8,128)(2,1)S(1)} async-done(((bf16[8,128,512]{2,1,0:T(8,128)(2,1)}), bf16[8,128,512]{2,1,0:T(8,128)(2,1)S(1)}, u32[]{:S(2)}, u32[]{:S(2)}) %all-to-all-start) | async-done | bytes 1048608 | tf_op jit(solution)/shard_map/all_to_all | solution.py:44
  37.2 3.6 %all-to-all-start.1 = ((bf16[4,256,832]{1,2,0:T(8,128)(2,1)}), bf16[4,256,832]{1,2,0:T(8,128)(2,1)S(1)}, u32[]{:S(2)}, u32[]{:S(2)}) async-start(bf16[4,256,832]{1,2,0:T(8,128)(2,1)} %bitcast.103), calls=%async_computation.1 | async-start | bytes 3407872 | tf_op jit(solution)/shard_map/all_to_all | solution.py:49
  40.8 21.2 %all-to-all-done.1 = bf16[4,256,832]{1,2,0:T(8,128)(2,1)S(1)} async-done(((bf16[4,256,832]{1,2,0:T(8,128)(2,1)}), bf16[4,256,832]{1,2,0:T(8,128)(2,1)S(1)}, u32[]{:S(2)}, u32[]{:S(2)}) %all-to-all-start.1) | async-done | bytes 1703968 | tf_op jit(solution)/shard_map/all_to_all | solution.py:49
  63.5 8.1 %all-to-all-start.2 = ((bf16[8,32,832]{2,1,0:T(8,128)(2,1)}), bf16[8,32,832]{2,1,0:T(8,128)(2,1)S(1)}, u32[]{:S(2)}, u32[]{:S(2)}) async-start(bf16[8,32,832]{2,1,0:T(8,128)(2,1)} %bitcast.1), calls=%async_computation.2 | async-start | bytes 917504 | tf_op jit(solution)/shard_map/all_to_all | solution.py:49
  71.7 7.9 %collective-permute-start.4 = (bf16[128,768]{1,0:T(8,128)(2,1)S(1)}, bf16[128,768]{1,0:T(8,128)(2,1)S(1)}, u32[]{:S(2)}, u32[]{:S(2)}) collective-permute-start(bf16[128,768]{1,0:T(8,128)(2,1)S(1)} %pad_maximum_fusion.4), channel_id=1, source_target_pairs={{0,256},{256,0},{1,257},{257,1},{2,258},{258,2},{3,259},{259,3},{4... | collective-permute-start | bytes 589832 | tf_op jit(solution)/shard_map/ppermute | solution.py:39
  79.7 20.3 %collective-permute-done.4 = bf16[128,768]{1,0:T(8,128)(2,1)S(1)} collective-permute-done((bf16[128,768]{1,0:T(8,128)(2,1)S(1)}, bf16[128,768]{1,0:T(8,128)(2,1)S(1)}, u32[]{:S(2)}, u32[]{:S(2)}) %collective-permute-start.4) | collective-permute-done | bytes 196640 | tf_op jit(solution)/shard_map/ppermute | solution.py:39
  103.3 3.5 %copy.52 = bf16[2,2,256,832]{2,3,1,0:T(8,128)(2,1)} copy(bf16[2,2,256,832]{3,2,1,0:T(8,128)(2,1)} %pad_maximum_fusion.1) | data formatting | bytes 3407872 | tf_op jit(solution)/shard_map/stack | solution.py:100
  109.2 4.8 %collective-permute-start.6 = (bf16[2,2,256,832]{2,3,1,0:T(8,128)(2,1)}, bf16[2,2,256,832]{2,3,1,0:T(8,128)(2,1)}, u32[]{:S(2)}, u32[]{:S(2)}) collective-permute-start(bf16[2,2,256,832]{2,3,1,0:T(8,128)(2,1)} %copy.52), channel_id=1, source_target_pairs={{0,24},{8,0},{16,8},{24,16},{1,25},{9,1},{17,9},{25,17},{2,26},{10... | collective-permute-start | bytes 5111816 | tf_op jit(solution)/shard_map/ppermute | solution.py:39
  121.5 46.9 %all_gather.9 = bf16[512,832]{1,0:T(8,128)(2,1)S(1)} all-gather(bf16[32,832]{1,0:T(8,128)(2,1)S(1)} %reduce_sum.57), channel_id=1, replica_groups=mesh['dp'=2,'y'=4,'core'=2,'x'=4,'z'=8] {'dp','z'}, dimensions={0}, use_global_device_ids=true | all-gather | bytes 905216 | tf_op jit(solution)/shard_map/all_gather | solution.py:121
  170.4 4.6 %collective-permute-start.9 = (bf16[2,128,832]{2,1,0:T(8,128)(2,1)S(1)}, bf16[2,128,832]{2,1,0:T(8,128)(2,1)S(1)}, u32[]{:S(2)}, u32[]{:S(2)}) collective-permute-start(bf16[2,128,832]{2,1,0:T(8,128)(2,1)S(1)} %bitcast.110), channel_id=1, source_target_pairs={{0,24},{8,0},{16,8},{24,16},{1,25},{9,1},{17,9},{25,17},{2,26},{10... | collective-permute-start | bytes 1277960 | tf_op jit(solution)/shard_map/ppermute | solution.py:39
  178.9 3.1 %collective-permute-start.1 = (bf16[2,128,832]{2,1,0:T(8,128)(2,1)S(1)}, bf16[2,128,832]{2,1,0:T(8,128)(2,1)S(1)}, u32[]{:S(2)}, u32[]{:S(2)}) collective-permute-start(bf16[2,128,832]{2,1,0:T(8,128)(2,1)S(1)} %bitcast.108), channel_id=1, source_target_pairs={{0,24},{8,0},{16,8},{24,16},{1,25},{9,1},{17,9},{25,17},{2,26},{10... | collective-permute-start | bytes 1277960 | tf_op jit(solution)/shard_map/ppermute | solution.py:39
  182.2 3.3 %collective-permute-start.11 = (bf16[128,832]{1,0:T(8,128)(2,1)S(1)}, bf16[128,832]{1,0:T(8,128)(2,1)S(1)}, u32[]{:S(2)}, u32[]{:S(2)}) collective-permute-start(bf16[128,832]{1,0:T(8,128)(2,1)S(1)} %get-tuple-element.48), channel_id=1, source_target_pairs={{0,24},{8,0},{16,8},{24,16},{1,25},{9,1},{17,9},{25,17},{2,26},{10... | collective-permute-start | bytes 638984 | tf_op jit(solution)/shard_map/ppermute | solution.py:39
  185.5 4.4 %collective-permute-done = bf16[2,128,832]{2,1,0:T(8,128)(2,1)S(1)} collective-permute-done((bf16[2,128,832]{2,1,0:T(8,128)(2,1)S(1)}, bf16[2,128,832]{2,1,0:T(8,128)(2,1)S(1)}, u32[]{:S(2)}, u32[]{:S(2)}) %collective-permute-start) | collective-permute-done | bytes 426016 | tf_op jit(solution)/shard_map/ppermute | solution.py:39
  196.0 5.3 %collective-permute-start.3 = (bf16[128,832]{1,0:T(8,128)(2,1)S(1)}, bf16[128,832]{1,0:T(8,128)(2,1)S(1)}, u32[]{:S(2)}, u32[]{:S(2)}) collective-permute-start(bf16[128,832]{1,0:T(8,128)(2,1)S(1)} %get-tuple-element.54), channel_id=1, source_target_pairs={{0,24},{8,0},{16,8},{24,16},{1,25},{9,1},{17,9},{25,17},{2,26},{10... | collective-permute-start | bytes 638984 | tf_op jit(solution)/shard_map/ppermute | solution.py:39
  201.4 4.0 %collective-permute-done.3 = bf16[128,832]{1,0:T(8,128)(2,1)S(1)} collective-permute-done((bf16[128,832]{1,0:T(8,128)(2,1)S(1)}, bf16[128,832]{1,0:T(8,128)(2,1)S(1)}, u32[]{:S(2)}, u32[]{:S(2)}) %collective-permute-start.3) | collective-permute-done | bytes 213024 | tf_op jit(solution)/shard_map/ppermute | solution.py:39
  210.0 3.0 %slice_bitcast_fusion.4 = (bf16[2,256,832]{1,2,0:T(8,128)(2,1)}, bf16[1,2,256,832]{2,3,1,0:T(8,128)(2,1)}, bf16[1,2,256,832]{2,3,1,0:T(8,128)(2,1)}) fusion(bf16[2,2,256,832]{2,3,1,0:T(8,128)(2,1)} %collective-permute-done.6), kind=kLoop, calls=%fused_computation.117 | loop fusion | bytes 4259840 | tf_op jit(solution)/shard_map/squeeze | solution.py:56
  213.0 4.7 %collective-permute-start.12 = (bf16[2,256,832]{1,2,0:T(8,128)(2,1)}, bf16[2,256,832]{1,2,0:T(8,128)(2,1)}, u32[]{:S(2)}, u32[]{:S(2)}) collective-permute-start(bf16[2,256,832]{1,2,0:T(8,128)(2,1)} %get-tuple-element.36), channel_id=1, source_target_pairs={{0,24},{8,0},{16,8},{24,16},{1,25},{9,1},{17,9},{25,17},{2,26},{10... | collective-permute-start | bytes 2555912 | tf_op jit(solution)/shard_map/ppermute | solution.py:39
  236.6 2.8 constant_dynamic-update-slice_fusion
  241.8 3.4 %fusion.2 = (bf16[1024,832]{1,0:T(8,128)(2,1)}, bf16[1024,832]{1,0:T(8,128)(2,1)S(1)}, bf16[1024,832]{1,0:T(8,128)(2,1)S(1)}) fusion(bf16[4,1,256,832]{3,2,1,0:T(8,128)(2,1)S(1)} %get-tuple-element.29, bf16[4,1,256,832]{3,2,1,0:T(8,128)(2,1)S(1)} %get-tuple-element.28), kind=kLoop, calls=%fused_computation.16 | loop fusion | flops 12779520 | bytes 8519680 | tf_op jit(solution)/shard_map/convert_element_type | solution.py:114
  250.3 13.5 %all-to-all-start.3 = ((bf16[8,128,512]{2,1,0:T(8,128)(2,1)}), bf16[8,128,512]{2,1,0:T(8,128)(2,1)}, u32[]{:S(2)}, u32[]{:S(2)}) async-start(bf16[8,128,512]{2,1,0:T(8,128)(2,1)} %bitcast.106), calls=%async_computation.3 | async-start | bytes 2097152 | tf_op jit(solution)/shard_map/all_to_all | solution.py:49
  266.2 4.2 %fusion.7 = (bf16[1024,832]{1,0:T(8,128)(2,1)}, bf16[1024,832]{1,0:T(8,128)(2,1)}, bf16[1024,832]{1,0:T(8,128)(2,1)}) fusion(bf16[4,1,256,832]{3,2,1,0:T(8,128)(2,1)S(1)} %get-tuple-element.25, bf16[4,1,256,832]{3,2,1,0:T(8,128)(2,1)S(1)} %get-tuple-element.24), kind=kLoop, calls=%fused_computation.21 | loop fusion | flops 12779520 | bytes 8519680 | tf_op jit(solution)/shard_map/convert_element_type | solution.py:114
  271.5 7.4 %all-to-all-done.3 = bf16[8,128,512]{2,1,0:T(8,128)(2,1)} async-done(((bf16[8,128,512]{2,1,0:T(8,128)(2,1)}), bf16[8,128,512]{2,1,0:T(8,128)(2,1)}, u32[]{:S(2)}, u32[]{:S(2)}) %all-to-all-start.3) | async-done | bytes 1048608 | tf_op jit(solution)/shard_map/all_to_all | solution.py:49
  281.0 2.7 fusion.18
  (142 shorter events, 76.0 us)
Async XLA Ops:
  7.2 27.6 %copy-start = (bf16[832,512]{1,0:T(8,128)(2,1)S(1)}, bf16[832,512]{1,0:T(8,128)(2,1)}, u32[]{:S(2)}) copy-start(bf16[832,512]{1,0:T(8,128)(2,1)} %param.15) | copy-start | bytes 2555908
  7.2 13.1 %copy-start.22 = (s32[4]{0:T(128)S(1)}, s32[4]{0:T(128)}, u32[]{:S(2)}) copy-start(s32[4]{0:T(128)} %param.16) | copy-start | bytes 52
  7.2 13.2 %copy-start.23 = (s32[8]{0:T(128)S(1)}, s32[8]{0:T(128)}, u32[]{:S(2)}) copy-start(s32[8]{0:T(128)} %param.17) | copy-start | bytes 100
  9.3 25.3 %all-to-all-start = ((bf16[8,128,512]{2,1,0:T(8,128)(2,1)}), bf16[8,128,512]{2,1,0:T(8,128)(2,1)S(1)}, u32[]{:S(2)}, u32[]{:S(2)}) async-start(bf16[8,128,512]{2,1,0:T(8,128)(2,1)} %broadcast_in_dim.89), calls=%async_computation | async-start | bytes 2097152 | tf_op jit(solution)/shard_map/all_to_all | solution.py:44
  19.6 80.5 %all-gather.6.cloned.1.call-start = ((), (), s32[]{:S(2)}) async-start(), calls=%async_computation.5 | async-start | bytes 1949696 | tf_op jit(solution)/shard_map/all_gather | solution.py:87
  37.2 24.8 %all-to-all-start.1 = ((bf16[4,256,832]{1,2,0:T(8,128)(2,1)}), bf16[4,256,832]{1,2,0:T(8,128)(2,1)S(1)}, u32[]{:S(2)}, u32[]{:S(2)}) async-start(bf16[4,256,832]{1,2,0:T(8,128)(2,1)} %bitcast.103), calls=%async_computation.1 | async-start | bytes 3407872 | tf_op jit(solution)/shard_map/all_to_all | solution.py:49
  40.8 30.8 %copy-start.17 = (bf16[128,512]{1,0:T(8,128)(2,1)S(1)}, bf16[128,512]{1,0:T(8,128)(2,1)}, u32[]{:S(2)}) copy-start(bf16[128,512]{1,0:T(8,128)(2,1)} %param.9) | copy-start | bytes 393220
  40.8 30.9 %copy-start.16 = (bf16[128,512]{1,0:T(8,128)(2,1)S(1)}, bf16[128,512]{1,0:T(8,128)(2,1)}, u32[]{:S(2)}) copy-start(bf16[128,512]{1,0:T(8,128)(2,1)} %param.10) | copy-start | bytes 393220
  63.5 57.9 %all-to-all-start.2 = ((bf16[8,32,832]{2,1,0:T(8,128)(2,1)}), bf16[8,32,832]{2,1,0:T(8,128)(2,1)S(1)}, u32[]{:S(2)}, u32[]{:S(2)}) async-start(bf16[8,32,832]{2,1,0:T(8,128)(2,1)} %bitcast.1), calls=%async_computation.2 | async-start | bytes 917504 | tf_op jit(solution)/shard_map/all_to_all | solution.py:49
  71.6 209.4 %all-gather.4.cloned.1.call-start = ((), (), s32[]{:S(2)}) async-start(), calls=%async_computation.4 | async-start | bytes 2359296 | tf_op jit(solution)/shard_map/all_gather | solution.py:103
  71.7 28.3 %collective-permute-start.4 = (bf16[128,768]{1,0:T(8,128)(2,1)S(1)}, bf16[128,768]{1,0:T(8,128)(2,1)S(1)}, u32[]{:S(2)}, u32[]{:S(2)}) collective-permute-start(bf16[128,768]{1,0:T(8,128)(2,1)S(1)} %pad_maximum_fusion.4), channel_id=1, source_target_pairs={{0,256},{256,0},{1,257},{257,1},{2,258},{258,2},{3,259},{259,3},{4... | collective-permute-start | bytes 589832 | tf_op jit(solution)/shard_map/ppermute | solution.py:39
  106.8 98.7 %collective-permute-start.5 = (bf16[2,2,256,832]{2,3,1,0:T(8,128)(2,1)}, bf16[2,2,256,832]{2,3,1,0:T(8,128)(2,1)}, u32[]{:S(2)}, u32[]{:S(2)}) collective-permute-start(bf16[2,2,256,832]{2,3,1,0:T(8,128)(2,1)} %copy.52), channel_id=1, source_target_pairs={{0,8},{8,16},{16,24},{24,0},{1,9},{9,17},{17,25},{25,1},{2,10},{10... | collective-permute-start | bytes 5111816 | tf_op jit(solution)/shard_map/ppermute | solution.py:39
  109.2 100.8 %collective-permute-start.6 = (bf16[2,2,256,832]{2,3,1,0:T(8,128)(2,1)}, bf16[2,2,256,832]{2,3,1,0:T(8,128)(2,1)}, u32[]{:S(2)}, u32[]{:S(2)}) collective-permute-start(bf16[2,2,256,832]{2,3,1,0:T(8,128)(2,1)} %copy.52), channel_id=1, source_target_pairs={{0,24},{8,0},{16,8},{24,16},{1,25},{9,1},{17,9},{25,17},{2,26},{10... | collective-permute-start | bytes 5111816 | tf_op jit(solution)/shard_map/ppermute | solution.py:39
  168.5 10.4 %collective-permute-start.8 = (bf16[2,128,832]{2,1,0:T(8,128)(2,1)S(1)}, bf16[2,128,832]{2,1,0:T(8,128)(2,1)S(1)}, u32[]{:S(2)}, u32[]{:S(2)}) collective-permute-start(bf16[2,128,832]{2,1,0:T(8,128)(2,1)S(1)} %bitcast.109), channel_id=1, source_target_pairs={{0,8},{8,16},{16,24},{24,0},{1,9},{9,17},{17,25},{25,1},{2,10},{10... | collective-permute-start | bytes 1277960 | tf_op jit(solution)/shard_map/ppermute | solution.py:39
  170.4 11.7 %collective-permute-start.9 = (bf16[2,128,832]{2,1,0:T(8,128)(2,1)S(1)}, bf16[2,128,832]{2,1,0:T(8,128)(2,1)S(1)}, u32[]{:S(2)}, u32[]{:S(2)}) collective-permute-start(bf16[2,128,832]{2,1,0:T(8,128)(2,1)S(1)} %bitcast.110), channel_id=1, source_target_pairs={{0,24},{8,0},{16,8},{24,16},{1,25},{9,1},{17,9},{25,17},{2,26},{10... | collective-permute-start | bytes 1277960 | tf_op jit(solution)/shard_map/ppermute | solution.py:39
  175.0 14.9 %collective-permute-start = (bf16[2,128,832]{2,1,0:T(8,128)(2,1)S(1)}, bf16[2,128,832]{2,1,0:T(8,128)(2,1)S(1)}, u32[]{:S(2)}, u32[]{:S(2)}) collective-permute-start(bf16[2,128,832]{2,1,0:T(8,128)(2,1)S(1)} %bitcast.107), channel_id=1, source_target_pairs={{0,8},{8,16},{16,24},{24,0},{1,9},{9,17},{17,25},{25,1},{2,10},{10... | collective-permute-start | bytes 1277960 | tf_op jit(solution)/shard_map/ppermute | solution.py:39
  178.9 14.4 %collective-permute-start.1 = (bf16[2,128,832]{2,1,0:T(8,128)(2,1)S(1)}, bf16[2,128,832]{2,1,0:T(8,128)(2,1)S(1)}, u32[]{:S(2)}, u32[]{:S(2)}) collective-permute-start(bf16[2,128,832]{2,1,0:T(8,128)(2,1)S(1)} %bitcast.108), channel_id=1, source_target_pairs={{0,24},{8,0},{16,8},{24,16},{1,25},{9,1},{17,9},{25,17},{2,26},{10... | collective-permute-start | bytes 1277960 | tf_op jit(solution)/shard_map/ppermute | solution.py:39
  182.2 13.8 %collective-permute-start.11 = (bf16[128,832]{1,0:T(8,128)(2,1)S(1)}, bf16[128,832]{1,0:T(8,128)(2,1)S(1)}, u32[]{:S(2)}, u32[]{:S(2)}) collective-permute-start(bf16[128,832]{1,0:T(8,128)(2,1)S(1)} %get-tuple-element.48), channel_id=1, source_target_pairs={{0,24},{8,0},{16,8},{24,16},{1,25},{9,1},{17,9},{25,17},{2,26},{10... | collective-permute-start | bytes 638984 | tf_op jit(solution)/shard_map/ppermute | solution.py:39
  189.9 11.4 %collective-permute-start.10 = (bf16[128,832]{1,0:T(8,128)(2,1)S(1)}, bf16[128,832]{1,0:T(8,128)(2,1)S(1)}, u32[]{:S(2)}, u32[]{:S(2)}) collective-permute-start(bf16[128,832]{1,0:T(8,128)(2,1)S(1)} %get-tuple-element.44), channel_id=1, source_target_pairs={{0,8},{8,16},{16,24},{24,0},{1,9},{9,17},{17,25},{25,1},{2,10},{10... | collective-permute-start | bytes 638984 | tf_op jit(solution)/shard_map/ppermute | solution.py:39
  193.3 8.0 %collective-permute-start.2 = (bf16[128,832]{1,0:T(8,128)(2,1)S(1)}, bf16[128,832]{1,0:T(8,128)(2,1)S(1)}, u32[]{:S(2)}, u32[]{:S(2)}) collective-permute-start(bf16[128,832]{1,0:T(8,128)(2,1)S(1)} %get-tuple-element.50), channel_id=1, source_target_pairs={{0,8},{8,16},{16,24},{24,0},{1,9},{9,17},{17,25},{25,1},{2,10},{10... | collective-permute-start | bytes 638984 | tf_op jit(solution)/shard_map/ppermute | solution.py:39
  196.0 9.5 %collective-permute-start.3 = (bf16[128,832]{1,0:T(8,128)(2,1)S(1)}, bf16[128,832]{1,0:T(8,128)(2,1)S(1)}, u32[]{:S(2)}, u32[]{:S(2)}) collective-permute-start(bf16[128,832]{1,0:T(8,128)(2,1)S(1)} %get-tuple-element.54), channel_id=1, source_target_pairs={{0,24},{8,0},{16,8},{24,16},{1,25},{9,1},{17,9},{25,17},{2,26},{10... | collective-permute-start | bytes 638984 | tf_op jit(solution)/shard_map/ppermute | solution.py:39
  208.0 24.1 %collective-permute-start.7 = (bf16[2,256,832]{1,2,0:T(8,128)(2,1)}, bf16[2,256,832]{1,2,0:T(8,128)(2,1)}, u32[]{:S(2)}, u32[]{:S(2)}) collective-permute-start(bf16[2,256,832]{1,2,0:T(8,128)(2,1)} %get-tuple-element.40), channel_id=1, source_target_pairs={{0,8},{8,16},{16,24},{24,0},{1,9},{9,17},{17,25},{25,1},{2,10},{10... | collective-permute-start | bytes 2555912 | tf_op jit(solution)/shard_map/ppermute | solution.py:39
  213.0 21.4 %collective-permute-start.12 = (bf16[2,256,832]{1,2,0:T(8,128)(2,1)}, bf16[2,256,832]{1,2,0:T(8,128)(2,1)}, u32[]{:S(2)}, u32[]{:S(2)}) collective-permute-start(bf16[2,256,832]{1,2,0:T(8,128)(2,1)} %get-tuple-element.36), channel_id=1, source_target_pairs={{0,24},{8,0},{16,8},{24,16},{1,25},{9,1},{17,9},{25,17},{2,26},{10... | collective-permute-start | bytes 2555912 | tf_op jit(solution)/shard_map/ppermute | solution.py:39
  250.3 28.6 %all-to-all-start.3 = ((bf16[8,128,512]{2,1,0:T(8,128)(2,1)}), bf16[8,128,512]{2,1,0:T(8,128)(2,1)}, u32[]{:S(2)}, u32[]{:S(2)}) async-start(bf16[8,128,512]{2,1,0:T(8,128)(2,1)} %bitcast.106), calls=%async_computation.3 | async-start | bytes 2097152 | tf_op jit(solution)/shard_map/all_to_all | solution.py:49
  (19 other events, 67.9 us)
Sparse Core Ops, SparseCore 0:
  23.0 67.2 all-gather.5
  114.8 50.3 all-gather.3

commit v3 on v2

--- a/solution.py
+++ b/solution.py
@@ -53,14 +53,11 @@
 def gather_x(block):
     x = lax.axis_index("x")
     left, right = shift(block, "x", N_X, 1), shift(block, "x", N_X, -1)
-    far_low, far_high = shift(left[0], "x", N_X, 1), shift(right[1], "x", N_X, -1)
-    outs = []
-    for side, far in ((0, far_low), (1, far_high)):
-        out = jnp.zeros((N_X,) + block.shape[1:], block.dtype)
-        for step, part in ((0, block[side]), (N_X - 1, left[side]), (1, right[side]), (2, far)):
-            out = lax.dynamic_update_slice_in_dim(out, part[None], (x + step) % N_X, 0)
-        outs.append(out)
-    return outs
+    far = jnp.stack([shift(left[0], "x", N_X, 1), shift(right[1], "x", N_X, -1)])
+    out = jnp.zeros((N_X,) + block.shape, block.dtype)
+    for step, part in ((0, block), (N_X - 1, left), (1, right), (2, far)):
+        out = lax.dynamic_update_slice_in_dim(out, part[None], (x + step) % N_X, 0)
+    return out
 
 
 def on_device(
@@ -95,19 +92,19 @@
     head_x = sum_over(block_term, "x", N_X)
     _, saved, partner = lax.optimization_barrier((head_x, saved, partner))
     saved = saved.reshape(n_dp, N_Z, 2, own, ffw)
-    saved_own = pick(saved, batch).transpose(1, 0, 2, 3).reshape(2, N_Z * own, ffw)
-    saved_away = pick(saved, away).transpose(1, 0, 2, 3).reshape(2, N_Z * own, ffw)
-    saved_own, saved_away = gather_x(jnp.stack([saved_own, saved_away]))
+    saved_own, saved_away = pick(saved, batch), pick(saved, away)
+    saved_own = lax.all_gather(saved_own, "x", axis=0)
+    saved_away = lax.all_gather(saved_away, "x", axis=0)
 
-    rest = jnp.concatenate([partner, act_own], axis=1)
-    rest = lax.all_gather(rest, row_axes, axis=0, tiled=True)
+    rest = spread(jnp.concatenate([partner, act_own], axis=1), row_axes, n_row)
+    rest = rest.reshape(tok, 2 * width)
     masked_away = jnp.where(pick(live, away)[:, None], rest[:, :width], zero)
     act_away = rest[:, width : width + half]
     act_here = rest[:, width + half :]
 
     def factors(pair):
-        gate = pair[:, 0].astype(jnp.float32).reshape(tok, ffw)
-        up = pair[:, 1].astype(jnp.float32).reshape(tok, ffw)
+        gate = pair[:, :, 0].astype(jnp.float32).reshape(tok, ffw)
+        up = pair[:, :, 1].astype(jnp.float32).reshape(tok, ffw)
         sig = jax.nn.sigmoid(gate)
         silu = gate * sig
         slope = (up * sig * (1.0 + gate * (1.0 - sig))).astype(jnp.bfloat16)
@@ -120,10 +117,11 @@
     head = sum_over(head_x, "z", N_Z)
     head = lax.all_gather(head, ("dp", "z"), axis=0, tiled=True)
     head = head.reshape(n_dp, N_Z * own, ffw)
-    head_own, head_away = pick(head, batch), pick(head, away)
+    head_own = spread(pick(head, batch), "x", N_X)
     halves = (2, N_Z * own // 2, ffw)
-    head_own = jnp.concatenate(gather_x(head_own.reshape(halves)), axis=1)
-    head_away = jnp.concatenate(gather_x(head_away.reshape(halves)), axis=1)
+    head_away = gather_x(pick(head, away).reshape(halves))
+
+    head_own, head_away = lax.optimization_barrier(head_own), lax.optimization_barrier(head_away)
 
     def times(head_rows, factor):
         value = head_rows.reshape(tok, ffw).astype(jnp.float32) * factor.astype(jnp.float32)

time: 299 us -> 318 us (1.064)
  the two profiles are of different devices: /device:TPU:1 before, /device:TPU:2 now
where the time goes in v3:
time: 318 us; the launch traced here: 316 us
  waiting for transfers between devices  120 us (38%)
  starting transfers between devices  59 us (19%)
  local copies, waits for them, and re-layouts  46.3 us (15%)
  blocking collectives  31.7 us (10%)
  other arithmetic  25.2 us (8%)
  matrix products  20.1 us (6%)
  between operations  14.1 us (4%)
    ppermute x5, waiting for transfers between devices, shift(): lax.ppermute(value, axis, [(i, (i + step) % size) for i in range(size)])  37.3 us
    all_gather x1, waiting for transfers between devices, on_device(): saved = lax.all_gather(saved, ('dp', 'z'), axis=0, tiled=True)  34.5 us
    all_to_all x3, waiting for transfers between devices, sum_over(): lax.all_to_all(blocks, axis, split_axis=0, concat_axis=0, tiled=True)  32.1 us
    all_gather x1, blocking collectives, on_device(): head = lax.all_gather(head, ('dp', 'z'), axis=0, tiled=True)  31.7 us
    ppermute x5, starting transfers between devices, shift(): lax.ppermute(value, axis, [(i, (i + step) % size) for i in range(size)])  24.6 us
    all_to_all x3, starting transfers between devices, sum_over(): lax.all_to_all(blocks, axis, split_axis=0, concat_axis=0, tiled=True)  19.2 us
    dot_general x6, matrix products, contract_first(): lax.dot_general(left, right, (((0,), (0,)), ((), ())), preferred_element_...  15.5 us
    all_to_all x3, waiting for transfers between devices, spread(): return lax.all_to_all(copies, axis, split_axis=0, concat_axis=0, tiled=True)  15.4 us
  transfers between devices with their start and end apart: 14, of which 10 were waited for; matrix products, arithmetic and copies ran while one was open for 24% of the time, Pallas kernels for 0%

profile of v3, /device:TPU:2, one launch (start us, length us, event | category | flops | bytes accessed | tf_op | source)
XLA Modules:
  0.0 316.4 jit_solution(11831667206336044504)
XLA Ops:
  10.8 4.5 %all-to-all-start = ((bf16[8,128,512]{2,1,0:T(8,128)(2,1)}), bf16[8,128,512]{2,1,0:T(8,128)(2,1)S(1)}, u32[]{:S(2)}, u32[]{:S(2)}) async-start(bf16[8,128,512]{2,1,0:T(8,128)(2,1)} %broadcast_in_dim.97), calls=%async_computation | async-start | bytes 2097152 | tf_op jit(solution)/shard_map/all_to_all | solution.py:44
  15.8 15.4 %all-to-all-done = bf16[8,128,512]{2,1,0:T(8,128)(2,1)S(1)} async-done(((bf16[8,128,512]{2,1,0:T(8,128)(2,1)}), bf16[8,128,512]{2,1,0:T(8,128)(2,1)S(1)}, u32[]{:S(2)}, u32[]{:S(2)}) %all-to-all-start) | async-done | bytes 1048608 | tf_op jit(solution)/shard_map/all_to_all | solution.py:44
  33.9 8.6 %all-to-all-start.1 = ((bf16[4,256,832]{1,2,0:T(8,128)(2,1)}), bf16[4,256,832]{1,2,0:T(8,128)(2,1)S(1)}, u32[]{:S(2)}, u32[]{:S(2)}) async-start(bf16[4,256,832]{1,2,0:T(8,128)(2,1)} %bitcast.75), calls=%async_computation.1 | async-start | bytes 3407872 | tf_op jit(solution)/shard_map/all_to_all | solution.py:49
  42.5 12.1 %collective-permute-start = (bf16[128,768]{1,0:T(8,128)(2,1)S(1)}, bf16[128,768]{1,0:T(8,128)(2,1)S(1)}, u32[]{:S(2)}, u32[]{:S(2)}) collective-permute-start(bf16[128,768]{1,0:T(8,128)(2,1)S(1)} %pad_maximum_fusion.1), channel_id=1, source_target_pairs={{0,256},{256,0},{1,257},{257,1},{2,258},{258,2},{3,259},{259,3},{4... | collective-permute-start | bytes 589832 | tf_op jit(solution)/shard_map/ppermute | solution.py:39
  54.6 8.5 %all-to-all-done.1 = bf16[4,256,832]{1,2,0:T(8,128)(2,1)S(1)} async-done(((bf16[4,256,832]{1,2,0:T(8,128)(2,1)}), bf16[4,256,832]{1,2,0:T(8,128)(2,1)S(1)}, u32[]{:S(2)}, u32[]{:S(2)}) %all-to-all-start.1) | async-done | bytes 1703968 | tf_op jit(solution)/shard_map/all_to_all | solution.py:49
  65.7 34.5 %all-gather.9.cloned.1.call-done = bf16[32,32,832]{2,1,0:T(8,128)(2,1)} async-done(((bf16[2,32,832]{2,1,0:T(8,128)(2,1)}), bf16[32,32,832]{2,1,0:T(8,128)(2,1)}) %all-gather.9.cloned.1.call-update) | async-done | bytes 1703952 | tf_op jit(solution)/shard_map/all_gather | solution.py:84
  104.1 6.1 %all-to-all-start.2 = ((bf16[8,32,832]{2,1,0:T(8,128)(2,1)}), bf16[8,32,832]{2,1,0:T(8,128)(2,1)S(1)}, u32[]{:S(2)}, u32[]{:S(2)}) async-start(bf16[8,32,832]{2,1,0:T(8,128)(2,1)} %bitcast.1), calls=%async_computation.2 | async-start | bytes 917504 | tf_op jit(solution)/shard_map/all_to_all | solution.py:49
  111.0 17.9 %all-to-all-done.2 = bf16[8,32,832]{2,1,0:T(8,128)(2,1)S(1)} async-done(((bf16[8,32,832]{2,1,0:T(8,128)(2,1)}), bf16[8,32,832]{2,1,0:T(8,128)(2,1)S(1)}, u32[]{:S(2)}, u32[]{:S(2)}) %all-to-all-start.2) | async-done | bytes 426016 | tf_op jit(solution)/shard_map/all_to_all | solution.py:49
  128.9 31.7 %all_gather.14 = bf16[512,832]{1,0:T(8,128)(2,1)S(1)} all-gather(bf16[32,832]{1,0:T(8,128)(2,1)S(1)} %reduce_sum.57), channel_id=1, replica_groups=mesh['dp'=2,'y'=4,'core'=2,'x'=4,'z'=8] {'dp','z'}, dimensions={0}, use_global_device_ids=true | all-gather | bytes 905216 | tf_op jit(solution)/shard_map/all_gather | solution.py:118
  169.2 6.1 %all-to-all-start.3 = ((bf16[4,256,832]{1,2,0:T(8,128)(2,1)}), bf16[4,256,832]{1,2,0:T(8,128)(2,1)}, u32[]{:S(2)}, u32[]{:S(2)}) async-start(bf16[4,256,832]{1,2,0:T(8,128)(2,1)} %broadcast_in_dim.100), calls=%async_computation.3 | async-start | bytes 3407872 | tf_op jit(solution)/shard_map/all_to_all | solution.py:44
  181.2 6.2 %collective-permute-done.1 = bf16[2,128,832]{1,0,2:T(2,128)(2,1)S(1)} collective-permute-done((bf16[2,128,832]{1,0,2:T(2,128)(2,1)}, bf16[2,128,832]{1,0,2:T(2,128)(2,1)S(1)}, u32[]{:S(2)}, u32[]{:S(2)}) %collective-permute-start.1) | collective-permute-done | bytes 426016 | tf_op jit(solution)/shard_map/ppermute | solution.py:39
  187.5 4.3 %collective-permute-start.3 = (bf16[128,832]{0,1:T(8,128)(2,1)S(1)}, bf16[128,832]{0,1:T(8,128)(2,1)S(1)}, u32[]{:S(2)}, u32[]{:S(2)}) collective-permute-start(bf16[128,832]{0,1:T(8,128)(2,1)S(1)} %bitcast.83), channel_id=1, source_target_pairs={{0,8},{8,16},{16,24},{24,0},{1,9},{9,17},{17,25},{25,1},{2,10},{10... | collective-permute-start | bytes 638984 | tf_op jit(solution)/shard_map/ppermute | solution.py:39
  192.9 23.5 %collective-permute-done.4 = bf16[128,832]{0,1:T(8,128)(2,1)S(1)} collective-permute-done((bf16[128,832]{0,1:T(8,128)(2,1)S(1)}, bf16[128,832]{0,1:T(8,128)(2,1)S(1)}, u32[]{:S(2)}, u32[]{:S(2)}) %collective-permute-start.4) | collective-permute-done | bytes 213024 | tf_op jit(solution)/shard_map/ppermute | solution.py:39
  216.4 4.8 %collective-permute-done.3 = bf16[128,832]{0,1:T(8,128)(2,1)S(1)} collective-permute-done((bf16[128,832]{0,1:T(8,128)(2,1)S(1)}, bf16[128,832]{0,1:T(8,128)(2,1)S(1)}, u32[]{:S(2)}, u32[]{:S(2)}) %collective-permute-start.3) | collective-permute-done | bytes 213024 | tf_op jit(solution)/shard_map/ppermute | solution.py:39
  225.9 4.5 %all-to-all-start.5 = ((bf16[8,128,1024]{2,1,0:T(8,128)(2,1)}), bf16[8,128,1024]{2,1,0:T(8,128)(2,1)}, u32[]{:S(2)}, u32[]{:S(2)}) async-start(bf16[8,128,1024]{2,1,0:T(8,128)(2,1)} %broadcast_in_dim.102), calls=%async_computation.5 | async-start | bytes 4194304 | tf_op jit(solution)/shard_map/all_to_all | solution.py:44
  236.7 3.7 %bitcast_convert_fusion = (f32[1024,832]{1,0:T(8,128)}, f32[1024,832]{1,0:T(8,128)}) fusion(bf16[4,8,1,32,832]{4,3,2,1,0:T(8,128)(2,1)S(1)} %get-tuple-element.26, bf16[4,8,1,32,832]{4,3,2,1,0:T(8,128)(2,1)S(1)} %get-tuple-element.27), kind=kLoop, calls=%fused_computation.14 | loop fusion | flops 1703936 | bytes 10223616 | tf_op jit(solution)/shard_map/convert_element_type | solution.py:107
  240.4 4.9 %copy.97 = f32[1024,832]{0,1:T(8,128)} copy(f32[1024,832]{1,0:T(8,128)} %get-tuple-element.41) | data formatting | bytes 6815744 | tf_op jit(solution)/shard_map/convert_element_type | solution.py:106
  245.4 4.9 %copy.98 = f32[1024,832]{0,1:T(8,128)} copy(f32[1024,832]{1,0:T(8,128)} %get-tuple-element.40) | data formatting | bytes 6815744 | tf_op jit(solution)/shard_map/convert_element_type | solution.py:107
  250.3 5.6 %multiply_convert_fusion.2 = (bf16[1024,832]{0,1:T(8,128)(2,1)}, bf16[1024,832]{0,1:T(8,128)(2,1)}, bf16[1024,832]{0,1:T(8,128)(2,1)}) fusion(f32[1024,832]{0,1:T(8,128)} %copy.98, f32[1024,832]{0,1:T(8,128)} %copy.97), kind=kLoop, calls=%fused_computation.3 | loop fusion | flops 11075584 | bytes 11927552 | tf_op jit(solution)/shard_map/convert_element_type | solution.py:111
  261.9 4.9 %copy.88 = f32[1024,832]{0,1:T(8,128)} copy(f32[1024,832]{1,0:T(8,128)} %get-tuple-element.39) | data formatting | bytes 6815744 | tf_op jit(solution)/shard_map/convert_element_type | solution.py:106
  266.9 4.9 %copy.89 = f32[1024,832]{0,1:T(8,128)} copy(f32[1024,832]{1,0:T(8,128)} %get-tuple-element.38) | data formatting | bytes 6815744 | tf_op jit(solution)/shard_map/convert_element_type | solution.py:107
  271.8 5.0 %multiply_convert_fusion.6 = (bf16[1024,832]{0,1:T(8,128)(2,1)}, bf16[1024,832]{0,1:T(8,128)(2,1)S(1)}, bf16[1024,832]{0,1:T(8,128)(2,1)}) fusion(f32[1024,832]{0,1:T(8,128)} %copy.89, f32[1024,832]{0,1:T(8,128)} %copy.88), kind=kLoop, calls=%fused_computation.9 | loop fusion | flops 11075584 | bytes 11927552 | tf_op jit(solution)/shard_map/convert_element_type | solution.py:111
  287.3 4.5 %all-to-all-start.4 = ((bf16[8,128,512]{2,1,0:T(8,128)(2,1)}), bf16[8,128,512]{2,1,0:T(8,128)(2,1)}, u32[]{:S(2)}, u32[]{:S(2)}) async-start(bf16[8,128,512]{2,1,0:T(8,128)(2,1)} %bitcast.76), calls=%async_computation.4 | async-start | bytes 2097152 | tf_op jit(solution)/shard_map/all_to_all | solution.py:49
  302.1 5.7 %all-to-all-done.4 = bf16[8,128,512]{2,1,0:T(8,128)(2,1)} async-done(((bf16[8,128,512]{2,1,0:T(8,128)(2,1)}), bf16[8,128,512]{2,1,0:T(8,128)(2,1)}, u32[]{:S(2)}, u32[]{:S(2)}) %all-to-all-start.4) | async-done | bytes 1048608 | tf_op jit(solution)/shard_map/all_to_all | solution.py:49
  (101 shorter events, 69.4 us)
Async XLA Ops:
  7.2 24.3 %copy-start = (bf16[832,512]{1,0:T(8,128)(2,1)S(1)}, bf16[832,512]{1,0:T(8,128)(2,1)}, u32[]{:S(2)}) copy-start(bf16[832,512]{1,0:T(8,128)(2,1)} %param.15) | copy-start | bytes 2555908
  7.2 8.1 %copy-start.14 = (s32[4]{0:T(128)S(1)}, s32[4]{0:T(128)}, u32[]{:S(2)}) copy-start(s32[4]{0:T(128)} %param.16) | copy-start | bytes 52
  7.2 8.2 %copy-start.15 = (s32[8]{0:T(128)S(1)}, s32[8]{0:T(128)}, u32[]{:S(2)}) copy-start(s32[8]{0:T(128)} %param.17) | copy-start | bytes 100
  7.2 92.9 %all-gather.9.cloned.1.call-start = ((), (), s32[]{:S(2)}) async-start(), calls=%async_computation.8 | async-start | bytes 1949696 | tf_op jit(solution)/shard_map/all_gather | solution.py:84
  10.8 20.4 %all-to-all-start = ((bf16[8,128,512]{2,1,0:T(8,128)(2,1)}), bf16[8,128,512]{2,1,0:T(8,128)(2,1)S(1)}, u32[]{:S(2)}, u32[]{:S(2)}) async-start(bf16[8,128,512]{2,1,0:T(8,128)(2,1)} %broadcast_in_dim.97), calls=%async_computation | async-start | bytes 2097152 | tf_op jit(solution)/shard_map/all_to_all | solution.py:44
  33.9 8.6 %copy-start.13 = (bf16[128,512]{1,0:T(8,128)(2,1)S(1)}, bf16[128,512]{1,0:T(8,128)(2,1)}, u32[]{:S(2)}) copy-start(bf16[128,512]{1,0:T(8,128)(2,1)} %param.9) | copy-start | bytes 393220
  33.9 8.6 %copy-start.12 = (bf16[128,512]{1,0:T(8,128)(2,1)S(1)}, bf16[128,512]{1,0:T(8,128)(2,1)}, u32[]{:S(2)}) copy-start(bf16[128,512]{1,0:T(8,128)(2,1)} %param.10) | copy-start | bytes 393220
  33.9 29.2 %all-to-all-start.1 = ((bf16[4,256,832]{1,2,0:T(8,128)(2,1)}), bf16[4,256,832]{1,2,0:T(8,128)(2,1)S(1)}, u32[]{:S(2)}, u32[]{:S(2)}) async-start(bf16[4,256,832]{1,2,0:T(8,128)(2,1)} %bitcast.75), calls=%async_computation.1 | async-start | bytes 3407872 | tf_op jit(solution)/shard_map/all_to_all | solution.py:49
  42.5 191.9 %all-gather.7.cloned.1.call-start = ((), (), s32[]{:S(2)}) async-start(), calls=%async_computation.7 | async-start | bytes 4587520 | tf_op jit(solution)/shard_map/all_gather | solution.py:97
  42.5 23.2 %collective-permute-start = (bf16[128,768]{1,0:T(8,128)(2,1)S(1)}, bf16[128,768]{1,0:T(8,128)(2,1)S(1)}, u32[]{:S(2)}, u32[]{:S(2)}) collective-permute-start(bf16[128,768]{1,0:T(8,128)(2,1)S(1)} %pad_maximum_fusion.1), channel_id=1, source_target_pairs={{0,256},{256,0},{1,257},{257,1},{2,258},{258,2},{3,259},{259,3},{4... | collective-permute-start | bytes 589832 | tf_op jit(solution)/shard_map/ppermute | solution.py:39
  104.1 24.7 %all-to-all-start.2 = ((bf16[8,32,832]{2,1,0:T(8,128)(2,1)}), bf16[8,32,832]{2,1,0:T(8,128)(2,1)S(1)}, u32[]{:S(2)}, u32[]{:S(2)}) async-start(bf16[8,32,832]{2,1,0:T(8,128)(2,1)} %bitcast.1), calls=%async_computation.2 | async-start | bytes 917504 | tf_op jit(solution)/shard_map/all_to_all | solution.py:49
  110.2 145.6 %all-gather.5.cloned.1.call-start = ((), (), s32[]{:S(2)}) async-start(), calls=%async_computation.6 | async-start | bytes 4587520 | tf_op jit(solution)/shard_map/all_gather | solution.py:96
  161.8 16.5 %collective-permute-start.2 = (bf16[2,128,832]{1,0,2:T(2,128)(2,1)}, bf16[2,128,832]{1,0,2:T(2,128)(2,1)S(1)}, u32[]{:S(2)}, u32[]{:S(2)}) collective-permute-start(bf16[2,128,832]{1,0,2:T(2,128)(2,1)} %reshape.129), channel_id=1, source_target_pairs={{0,24},{8,0},{16,8},{24,16},{1,25},{9,1},{17,9},{25,17},{2,26},{10... | collective-permute-start | bytes 1277960 | tf_op jit(solution)/shard_map/ppermute | solution.py:39
  164.8 22.7 %collective-permute-start.1 = (bf16[2,128,832]{1,0,2:T(2,128)(2,1)}, bf16[2,128,832]{1,0,2:T(2,128)(2,1)S(1)}, u32[]{:S(2)}, u32[]{:S(2)}) collective-permute-start(bf16[2,128,832]{1,0,2:T(2,128)(2,1)} %reshape.129), channel_id=1, source_target_pairs={{0,8},{8,16},{16,24},{24,0},{1,9},{9,17},{17,25},{25,1},{2,10},{10... | collective-permute-start | bytes 1277960 | tf_op jit(solution)/shard_map/ppermute | solution.py:39
  169.2 55.1 %all-to-all-start.3 = ((bf16[4,256,832]{1,2,0:T(8,128)(2,1)}), bf16[4,256,832]{1,2,0:T(8,128)(2,1)}, u32[]{:S(2)}, u32[]{:S(2)}) async-start(bf16[4,256,832]{1,2,0:T(8,128)(2,1)} %broadcast_in_dim.100), calls=%async_computation.3 | async-start | bytes 3407872 | tf_op jit(solution)/shard_map/all_to_all | solution.py:44
  178.8 37.6 %collective-permute-start.4 = (bf16[128,832]{0,1:T(8,128)(2,1)S(1)}, bf16[128,832]{0,1:T(8,128)(2,1)S(1)}, u32[]{:S(2)}, u32[]{:S(2)}) collective-permute-start(bf16[128,832]{0,1:T(8,128)(2,1)S(1)} %bitcast.82), channel_id=1, source_target_pairs={{0,24},{8,0},{16,8},{24,16},{1,25},{9,1},{17,9},{25,17},{2,26},{10... | collective-permute-start | bytes 638984 | tf_op jit(solution)/shard_map/ppermute | solution.py:39
  187.5 33.8 %collective-permute-start.3 = (bf16[128,832]{0,1:T(8,128)(2,1)S(1)}, bf16[128,832]{0,1:T(8,128)(2,1)S(1)}, u32[]{:S(2)}, u32[]{:S(2)}) collective-permute-start(bf16[128,832]{0,1:T(8,128)(2,1)S(1)} %bitcast.83), channel_id=1, source_target_pairs={{0,8},{8,16},{16,24},{24,0},{1,9},{9,17},{17,25},{25,1},{2,10},{10... | collective-permute-start | bytes 638984 | tf_op jit(solution)/shard_map/ppermute | solution.py:39
  225.9 51.0 %all-to-all-start.5 = ((bf16[8,128,1024]{2,1,0:T(8,128)(2,1)}), bf16[8,128,1024]{2,1,0:T(8,128)(2,1)}, u32[]{:S(2)}, u32[]{:S(2)}) async-start(bf16[8,128,1024]{2,1,0:T(8,128)(2,1)} %broadcast_in_dim.102), calls=%async_computation.5 | async-start | bytes 4194304 | tf_op jit(solution)/shard_map/all_to_all | solution.py:44
  276.8 3.7 %copy-start.4 = (f32[1024,832]{0,1:T(8,128)S(1)}, f32[1024,832]{0,1:T(8,128)}, u32[]{:S(2)}) copy-start(f32[1024,832]{0,1:T(8,128)} %reshape.133) | copy-start | bytes 10223620
  276.8 4.2 %copy-start.7 = (bf16[1024,832]{0,1:T(8,128)(2,1)S(1)}, bf16[1024,832]{0,1:T(8,128)(2,1)}, u32[]{:S(2)}) copy-start(bf16[1024,832]{0,1:T(8,128)(2,1)} %get-tuple-element.16) | copy-start | bytes 5111812
  287.3 20.5 %all-to-all-start.4 = ((bf16[8,128,512]{2,1,0:T(8,128)(2,1)}), bf16[8,128,512]{2,1,0:T(8,128)(2,1)}, u32[]{:S(2)}, u32[]{:S(2)}) async-start(bf16[8,128,512]{2,1,0:T(8,128)(2,1)} %bitcast.76), calls=%async_computation.4 | async-start | bytes 2097152 | tf_op jit(solution)/shard_map/all_to_all | solution.py:49
  291.8 5.3 %copy-start.6 = (bf16[1024,832]{0,1:T(8,128)(2,1)S(1)}, bf16[1024,832]{0,1:T(8,128)(2,1)}, u32[]{:S(2)}) copy-start(bf16[1024,832]{0,1:T(8,128)(2,1)} %get-tuple-element.14) | copy-start | bytes 5111812
  294.0 3.1 copy-start.3
  299.6 10.3 %copy-start.1 = (bf16[832,512]{1,0:T(8,128)(2,1)S(1)}, bf16[832,512]{1,0:T(8,128)(2,1)}, u32[]{:S(2)}) copy-start(bf16[832,512]{1,0:T(8,128)(2,1)} %param.15) | copy-start | bytes 2555908
  (6 other events, 11.0 us)
Sparse Core Ops, SparseCore 0:
  10.7 89.4 all-gather.8
  103.3 46.6 all-gather.6
  152.1 71.8 all-gather.4

commit v4 on v3

--- a/solution.py
+++ b/solution.py
@@ -1,6 +1,10 @@
+import functools
+import math
 import jax
 import jax.numpy as jnp
 from jax import lax
+from jax.experimental import pallas as pl
+from jax.experimental.pallas import tpu as pltpu
 from jax.sharding import Mesh, PartitionSpec as P
 
 SEQ = 256
@@ -10,12 +14,6 @@
 def contract_last(left, right):
     return lax.dot_general(
         left, right, (((1,), (1,)), ((), ())), preferred_element_type=jnp.float32
-    )
-
-
-def contract_first(left, right):
-    return lax.dot_general(
-        left, right, (((0,), (0,)), ((), ())), preferred_element_type=jnp.float32
     )
 
 
@@ -58,6 +56,108 @@
     for step, part in ((0, block), (N_X - 1, left), (1, right), (2, far)):
         out = lax.dynamic_update_slice_in_dim(out, part[None], (x + step) % N_X, 0)
     return out
+
+
+def swiglu_terms(saved_ref):
+    pair = saved_ref[0].astype(jnp.float32)
+    rows, ffw = pair.shape[0] * pair.shape[2], pair.shape[3]
+    gate, up = pair[:, 0].reshape(rows, ffw), pair[:, 1].reshape(rows, ffw)
+    sig = jax.nn.sigmoid(gate)
+    silu = gate * sig
+    return up, sig, silu, up * sig * (1.0 + gate * (1.0 - sig))
+
+
+def input_kernel(head_ref, saved_ref, w_gate_ref, w_up_ref, out_ref):
+    head = head_ref[0].astype(jnp.float32)
+    _, _, silu, slope = swiglu_terms(saved_ref)
+    grad_gate, grad_up = (head * slope).astype(jnp.bfloat16), (head * silu).astype(jnp.bfloat16)
+    term = jnp.dot(grad_gate, w_gate_ref[...], preferred_element_type=jnp.float32)
+    term += jnp.dot(grad_up, w_up_ref[...], preferred_element_type=jnp.float32)
+    out_ref[...] = term.astype(jnp.bfloat16)
+
+
+def input_term(head, saved, w_gate, w_up):
+    chunks, rows, ffw = head.shape
+    width = w_gate.shape[1]
+    whole = pl.BlockSpec((ffw, width), lambda i: (0, 0))
+    return pl.pallas_call(
+        input_kernel,
+        grid=(chunks,),
+        in_specs=[
+            pl.BlockSpec((1, rows, ffw), lambda i: (i, 0, 0)),
+            pl.BlockSpec((1,) + saved.shape[1:], lambda i: (i, 0, 0, 0, 0)),
+            whole,
+            whole,
+        ],
+        out_specs=pl.BlockSpec((rows, width), lambda i: (i, 0)),
+        out_shape=jax.ShapeDtypeStruct((chunks * rows, width), jnp.bfloat16),
+        name="input_term",
+        cost_estimate=pl.CostEstimate(
+            flops=4 * chunks * rows * ffw * width,
+            bytes_accessed=2 * (3 * head.size + 2 * w_gate.size + chunks * rows * width),
+            transcendentals=head.size,
+        ),
+    )(head, saved, w_gate, w_up)
+
+
+def weight_kernel(
+    scale, head_own, head_away, saved_own, saved_away, act_own, act_away, cot_own, cot_away,
+    gate_ref, up_ref, down_ref, gate_acc, up_acc, down_acc,
+):
+    @pl.when(pl.program_id(0) == 0)
+    def _():
+        gate_acc[...] = jnp.zeros_like(gate_acc)
+        up_acc[...] = jnp.zeros_like(up_acc)
+        down_acc[...] = jnp.zeros_like(down_acc)
+
+    for head_ref, saved_ref, act_ref, cot_ref in (
+        (head_own, saved_own, act_own, cot_own),
+        (head_away, saved_away, act_away, cot_away),
+    ):
+        head = head_ref[0].astype(jnp.float32)
+        up, _, silu, slope = swiglu_terms(saved_ref)
+        hidden = (silu * up).astype(jnp.bfloat16)
+        grad_gate = (head * slope).astype(jnp.bfloat16)
+        grad_up = (head * silu).astype(jnp.bfloat16)
+        act, cot = act_ref[...], cot_ref[...]
+        gate_acc[...] += jnp.dot(act, grad_gate, preferred_element_type=jnp.float32)
+        up_acc[...] += jnp.dot(act, grad_up, preferred_element_type=jnp.float32)
+        down_acc[...] += jnp.dot(cot, hidden, preferred_element_type=jnp.float32)
+
+    @pl.when(pl.program_id(0) == pl.num_programs(0) - 1)
+    def _():
+        gate_ref[...] = (gate_acc[...] * scale).T.astype(jnp.bfloat16)
+        up_ref[...] = (up_acc[...] * scale).T.astype(jnp.bfloat16)
+        down_ref[...] = (down_acc[...] * scale).T.astype(jnp.bfloat16)
+
+
+def weight_grads(scale, head_own, head_away, saved_own, saved_away, acts, cots):
+    chunks, rows, ffw = head_own.shape
+    half, width = acts[0].shape[0], cots[0].shape[0]
+    head_spec = pl.BlockSpec((1, rows, ffw), lambda i: (i, 0, 0))
+    saved_spec = pl.BlockSpec((1,) + saved_own.shape[1:], lambda i: (i, 0, 0, 0, 0))
+    act_spec = pl.BlockSpec((half, rows), lambda i: (0, i))
+    cot_spec = pl.BlockSpec((width, rows), lambda i: (0, i))
+    out = lambda cols: pl.BlockSpec((ffw, cols), lambda i: (0, 0))
+    shape = lambda cols: jax.ShapeDtypeStruct((ffw, cols), jnp.bfloat16)
+    return pl.pallas_call(
+        functools.partial(weight_kernel, scale),
+        grid=(chunks,),
+        in_specs=[head_spec] * 2 + [saved_spec] * 2 + [act_spec] * 2 + [cot_spec] * 2,
+        out_specs=[out(half), out(half), out(width)],
+        out_shape=[shape(half), shape(half), shape(width)],
+        scratch_shapes=[
+            pltpu.VMEM((half, ffw), jnp.float32),
+            pltpu.VMEM((half, ffw), jnp.float32),
+            pltpu.VMEM((width, ffw), jnp.float32),
+        ],
+        name="weight_grads",
+        cost_estimate=pl.CostEstimate(
+            flops=4 * chunks * rows * ffw * (2 * half + width),
+            bytes_accessed=2 * (6 * head_own.size + 2 * acts[0].size + 2 * cots[0].size),
+            transcendentals=2 * head_own.size,
+        ),
+    )(head_own, head_away, saved_own, saved_away, *acts, *cots)
 
 
 def on_device(
@@ -102,17 +202,8 @@
     act_away = rest[:, width : width + half]
     act_here = rest[:, width + half :]
 
-    def factors(pair):
-        gate = pair[:, :, 0].astype(jnp.float32).reshape(tok, ffw)
-        up = pair[:, :, 1].astype(jnp.float32).reshape(tok, ffw)
-        sig = jax.nn.sigmoid(gate)
-        silu = gate * sig
-        slope = (up * sig * (1.0 + gate * (1.0 - sig))).astype(jnp.bfloat16)
-        hidden = (silu * up).astype(jnp.bfloat16)
-        return lax.optimization_barrier((slope, silu.astype(jnp.bfloat16), hidden))
-
-    slope_own, silu_own, hid_own = factors(saved_own)
-    slope_away, silu_away, hid_away = factors(saved_away)
+    acts = lax.optimization_barrier((act_here.T, act_away.T))
+    cots = lax.optimization_barrier((masked_own.T, masked_away.T))
 
     head = sum_over(head_x, "z", N_Z)
     head = lax.all_gather(head, ("dp", "z"), axis=0, tiled=True)
@@ -121,30 +212,17 @@
     halves = (2, N_Z * own // 2, ffw)
     head_away = gather_x(pick(head, away).reshape(halves))
 
-    head_own, head_away = lax.optimization_barrier(head_own), lax.optimization_barrier(head_away)
-
-    def times(head_rows, factor):
-        value = head_rows.reshape(tok, ffw).astype(jnp.float32) * factor.astype(jnp.float32)
-        return value.astype(jnp.bfloat16)
-
-    gg_own, gu_own = times(head_own, slope_own), times(head_own, silu_own)
-    gg_away, gu_away = times(head_away, slope_away), times(head_away, silu_away)
-    term = (contract_last(gg_own, w_gate) + contract_last(gu_own, w_up)).astype(jnp.bfloat16)
+    head_away = head_away.reshape(N_X, N_Z * own, ffw)
+    term = input_term(head_own, saved_own, w_gate.T, w_up.T)
     input_grad = sum_over(term, row_axes, n_row)
 
-    scale = 1.0 / jnp.sqrt(jnp.float32(n_dp * tok))
+    scale = 1.0 / math.sqrt(n_dp * tok)
+    gate_grad, up_grad, down_grad = weight_grads(
+        scale, head_own, head_away, saved_own, saved_away, acts, cots
+    )
     f_half = ffw // 2
-    hid_own = lax.dynamic_slice_in_dim(hid_own, batch * f_half, f_half, 1)
-    hid_away = lax.dynamic_slice_in_dim(hid_away, batch * f_half, f_half, 1)
-    down_grad = (contract_first(hid_own, masked_own) + contract_first(hid_away, masked_away)) * scale
-    gate_grad = (contract_first(act_here, gg_own) + contract_first(act_away, gg_away)) * scale
-    up_grad = (contract_first(act_here, gu_own) + contract_first(act_away, gu_away)) * scale
-    return (
-        input_grad,
-        gate_grad.astype(jnp.bfloat16),
-        up_grad.astype(jnp.bfloat16),
-        down_grad.astype(jnp.bfloat16),
-    )
+    down_grad = lax.dynamic_slice_in_dim(down_grad, batch * f_half, f_half, 0)
+    return input_grad, gate_grad.T, up_grad.T, down_grad
 
 
 def solution(mesh):

time: 318 us -> 281 us (0.88)
  the two profiles are of different devices: /device:TPU:2 before, /device:TPU:15 now
where the time goes in v4:
time: 281 us; the launch traced here: 280 us
  starting transfers between devices  89.9 us (32%)
  waiting for transfers between devices  88.3 us (31%)
  blocking collectives  30.7 us (11%)
  local copies, waits for them, and re-layouts  28.4 us (10%)
  Pallas kernels  18.4 us (7%)
  between operations  14 us (5%)
  other arithmetic  9.17 us (3%)
    all_to_all x3, starting transfers between devices, spread(): return lax.all_to_all(copies, axis, split_axis=0, concat_axis=0, tiled=True)  44.4 us
    all_gather x1, blocking collectives, on_device(): head = lax.all_gather(head, ('dp', 'z'), axis=0, tiled=True)  30.7 us
    all_gather x1, waiting for transfers between devices, on_device(): saved = lax.all_gather(saved, ('dp', 'z'), axis=0, tiled=True)  30.3 us
    ppermute x5, starting transfers between devices, shift(): lax.ppermute(value, axis, [(i, (i + step) % size) for i in range(size)])  24.2 us
    all_to_all x3, waiting for transfers between devices, spread(): return lax.all_to_all(copies, axis, split_axis=0, concat_axis=0, tiled=True)  23 us
    all_to_all x3, waiting for transfers between devices, sum_over(): lax.all_to_all(blocks, axis, split_axis=0, concat_axis=0, tiled=True)  21.8 us
    all_to_all x3, starting transfers between devices, sum_over(): lax.all_to_all(blocks, axis, split_axis=0, concat_axis=0, tiled=True)  21.2 us
    ppermute x5, waiting for transfers between devices, shift(): lax.ppermute(value, axis, [(i, (i + step) % size) for i in range(size)])  12.5 us
  transfers between devices with their start and end apart: 14, of which 7 were waited for; matrix products, arithmetic and copies ran while one was open for 11% of the time, Pallas kernels for 7%

profile of v4, /device:TPU:15, one launch (start us, length us, event | category | flops | bytes accessed | tf_op | source)
XLA Modules:
  0.0 279.9 jit_solution(4906281437829761434)
XLA Ops:
  11.0 5.2 %all-to-all-start = ((bf16[8,128,512]{1,2,0:T(8,128)(2,1)}), bf16[8,128,512]{1,2,0:T(8,128)(2,1)S(1)}, u32[]{:S(2)}, u32[]{:S(2)}) async-start(bf16[8,128,512]{1,2,0:T(8,128)(2,1)} %broadcast_in_dim.97), calls=%async_computation | async-start | bytes 2097152 | tf_op jit(solution)/shard_map/all_to_all | solution.py:42
  16.7 13.4 %all-to-all-done = bf16[8,128,512]{1,2,0:T(8,128)(2,1)S(1)} async-done(((bf16[8,128,512]{1,2,0:T(8,128)(2,1)}), bf16[8,128,512]{1,2,0:T(8,128)(2,1)S(1)}, u32[]{:S(2)}, u32[]{:S(2)}) %all-to-all-start) | async-done | bytes 1048608 | tf_op jit(solution)/shard_map/all_to_all | solution.py:42
  32.5 8.3 %all-to-all-start.1 = ((bf16[4,256,832]{1,2,0:T(8,128)(2,1)}), bf16[4,256,832]{1,2,0:T(8,128)(2,1)S(1)}, u32[]{:S(2)}, u32[]{:S(2)}) async-start(bf16[4,256,832]{1,2,0:T(8,128)(2,1)} %bitcast.64), calls=%async_computation.1 | async-start | bytes 3407872 | tf_op jit(solution)/shard_map/all_to_all | solution.py:47
  40.8 11.6 %collective-permute-start = (bf16[128,768]{1,0:T(8,128)(2,1)S(1)}, bf16[128,768]{1,0:T(8,128)(2,1)S(1)}, u32[]{:S(2)}, u32[]{:S(2)}) collective-permute-start(bf16[128,768]{1,0:T(8,128)(2,1)S(1)} %pad_maximum_fusion.1), channel_id=1, source_target_pairs={{0,256},{256,0},{1,257},{257,1},{2,258},{258,2},{3,259},{259,3},{4... | collective-permute-start | bytes 589832 | tf_op jit(solution)/shard_map/ppermute | solution.py:37
  52.4 7.8 %all-to-all-done.1 = bf16[4,256,832]{1,2,0:T(8,128)(2,1)S(1)} async-done(((bf16[4,256,832]{1,2,0:T(8,128)(2,1)}), bf16[4,256,832]{1,2,0:T(8,128)(2,1)S(1)}, u32[]{:S(2)}, u32[]{:S(2)}) %all-to-all-start.1) | async-done | bytes 1703968 | tf_op jit(solution)/shard_map/all_to_all | solution.py:47
  60.7 30.3 %all-gather.9.cloned.1.call-done = bf16[32,32,832]{2,1,0:T(8,128)(2,1)} async-done(((bf16[2,32,832]{2,1,0:T(8,128)(2,1)}), bf16[32,32,832]{2,1,0:T(8,128)(2,1)}) %all-gather.9.cloned.1.call-update) | async-done | bytes 1703952 | tf_op jit(solution)/shard_map/all_gather | solution.py:184
  91.0 2.8 %constant_dynamic-slice_fusion.2 = (bf16[1,8,2,32,832]{4,3,2,1,0:T(8,128)(2,1)}, bf16[1,8,2,32,832]{4,3,2,1,0:T(8,128)(2,1)}) fusion(bf16[2,8,2,32,832]{4,3,2,1,0:T(8,128)(2,1)} %bitcast.70, s32[]{:T(128)S(6)} %select_n.95, s32[]{:T(128)S(6)} %select_n.92), kind=kLoop, calls=%fused_computation.28 | loop fusion | bytes 3407880 | tf_op jit(solution)/shard_map/jit(dynamic_index_in_dim)/dynamic_slice | solution.py:177
  94.9 5.5 %all-to-all-start.2 = ((bf16[8,32,832]{2,1,0:T(8,128)(2,1)}), bf16[8,32,832]{2,1,0:T(8,128)(2,1)S(1)}, u32[]{:S(2)}, u32[]{:S(2)}) async-start(bf16[8,32,832]{2,1,0:T(8,128)(2,1)} %bitcast), calls=%async_computation.2 | async-start | bytes 917504 | tf_op jit(solution)/shard_map/all_to_all | solution.py:47
  101.1 14.0 %all-to-all-done.2 = bf16[8,32,832]{2,1,0:T(8,128)(2,1)S(1)} async-done(((bf16[8,32,832]{2,1,0:T(8,128)(2,1)}), bf16[8,32,832]{2,1,0:T(8,128)(2,1)S(1)}, u32[]{:S(2)}, u32[]{:S(2)}) %all-to-all-start.2) | async-done | bytes 426016 | tf_op jit(solution)/shard_map/all_to_all | solution.py:47
  115.2 30.7 %all_gather.14 = bf16[512,832]{1,0:T(8,128)(2,1)S(1)} all-gather(bf16[32,832]{1,0:T(8,128)(2,1)S(1)} %reduce_sum.57), channel_id=1, replica_groups=mesh['dp'=2,'y'=4,'core'=2,'x'=4,'z'=8] {'dp','z'}, dimensions={0}, use_global_device_ids=true | all-gather | bytes 905216 | tf_op jit(solution)/shard_map/all_gather | solution.py:209
  147.5 4.1 %all-to-all-start.3 = ((bf16[4,256,832]{1,2,0:T(8,128)(2,1)}), bf16[4,256,832]{1,2,0:T(8,128)(2,1)S(1)}, u32[]{:S(2)}, u32[]{:S(2)}) async-start(bf16[4,256,832]{1,2,0:T(8,128)(2,1)} %broadcast_in_dim.100), calls=%async_computation.3 | async-start | bytes 3407872 | tf_op jit(solution)/shard_map/all_to_all | solution.py:42
  153.5 9.6 %all-to-all-done.3 = bf16[4,256,832]{1,2,0:T(8,128)(2,1)S(1)} async-done(((bf16[4,256,832]{1,2,0:T(8,128)(2,1)}), bf16[4,256,832]{1,2,0:T(8,128)(2,1)S(1)}, u32[]{:S(2)}, u32[]{:S(2)}) %all-to-all-start.3) | async-done | bytes 1703968 | tf_op jit(solution)/shard_map/all_to_all | solution.py:42
  165.0 35.2 %all-to-all-start.5 = ((bf16[8,128,1024]{1,2,0:T(8,128)(2,1)}), bf16[8,128,1024]{1,2,0:T(8,128)(2,1)S(1)}, u32[]{:S(2)}, u32[]{:S(2)}) async-start(bf16[8,128,1024]{1,2,0:T(8,128)(2,1)} %broadcast_in_dim.106), calls=%async_computation.5 | async-start | bytes 4194304 | tf_op jit(solution)/shard_map/all_to_all | solution.py:42
  200.2 4.8 %collective-permute-start.1 = (bf16[2,128,832]{2,1,0:T(8,128)(2,1)S(1)}, bf16[2,128,832]{2,1,0:T(8,128)(2,1)}, u32[]{:S(2)}, u32[]{:S(2)}) collective-permute-start(bf16[2,128,832]{2,1,0:T(8,128)(2,1)S(1)} %bitcast.67), channel_id=1, source_target_pairs={{0,8},{8,16},{16,24},{24,0},{1,9},{9,17},{17,25},{25,1},{2,10},{10... | collective-permute-start | bytes 1277960 | tf_op jit(solution)/shard_map/ppermute | solution.py:37
  204.9 1.9 collective-permute-start.2
  209.4 8.7 %collective-permute-done.1 = bf16[2,128,832]{2,1,0:T(8,128)(2,1)} collective-permute-done((bf16[2,128,832]{2,1,0:T(8,128)(2,1)S(1)}, bf16[2,128,832]{2,1,0:T(8,128)(2,1)}, u32[]{:S(2)}, u32[]{:S(2)}) %collective-permute-start.1) | collective-permute-done | bytes 426016 | tf_op jit(solution)/shard_map/ppermute | solution.py:37
  219.0 4.0 %collective-permute-start.3 = (bf16[128,832]{1,0:T(8,128)(2,1)S(1)}, bf16[128,832]{1,0:T(8,128)(2,1)S(1)}, u32[]{:S(2)}, u32[]{:S(2)}) collective-permute-start(bf16[128,832]{1,0:T(8,128)(2,1)S(1)} %slice_bitcast_fusion.3), channel_id=1, source_target_pairs={{0,8},{8,16},{16,24},{24,0},{1,9},{9,17},{17,25},{25,1},{2,10},{10... | collective-permute-start | bytes 638984 | tf_op jit(solution)/shard_map/ppermute | solution.py:37
  229.6 3.7 %collective-permute-done.4 = bf16[128,832]{1,0:T(8,128)(2,1)S(1)} collective-permute-done((bf16[128,832]{1,0:T(8,128)(2,1)S(1)}, bf16[128,832]{1,0:T(8,128)(2,1)S(1)}, u32[]{:S(2)}, u32[]{:S(2)}) %collective-permute-start.4) | collective-permute-done | bytes 213024 | tf_op jit(solution)/shard_map/ppermute | solution.py:37
  234.2 3.5 %copy.40.head_ref.head_own = bf16[4,256,832]{2,1,0:T(8,128)(2,1)} copy(bf16[4,256,832]{1,2,0:T(8,128)(2,1)} %copy-done.2) | data formatting | bytes 3407872 | tf_op jit(solution)/shard_map/all_to_all | solution.py:42
  239.4 6.4 %input_term.1 = bf16[1024,512]{1,0:T(8,128)(2,1)} custom-call(bf16[4,256,832]{2,1,0:T(8,128)(2,1)} %copy.40.head_ref.head_own, bf16[4,8,2,32,832]{4,3,2,1,0:T(8,128)(2,1)} %all-gather.5.cloned.1.call-done.saved_ref.saved_own, bf16[832,512]{1,0:T(8,128)(2,1)} %bitcast.73, bf16[832,512]{1,0:T(8,128)(2,1)} %bitcast.74), custom_call_target="tpu_custom_call" | custom-call | flops 1744830464 | bytes 7864320 | tf_op jit(solution)/shard_map/input_term/pallas_call | solution.py:83
  245.8 7.4 %all-to-all-start.4 = ((bf16[8,128,512]{2,1,0:T(8,128)(2,1)}), bf16[8,128,512]{2,1,0:T(8,128)(2,1)}, u32[]{:S(2)}, u32[]{:S(2)}) async-start(bf16[8,128,512]{2,1,0:T(8,128)(2,1)} %bitcast.65), calls=%async_computation.4 | async-start | bytes 2097152 | tf_op jit(solution)/shard_map/all_to_all | solution.py:47
  253.3 3.1 %fusion = (bf16[512,1024]{1,0:T(8,128)(2,1)}, bf16[512,1024]{1,0:T(8,128)(2,1)}) fusion(bf16[1024,1024]{0,1:T(8,128)(2,1)S(1)} %copy-done.1, pred[1024]{0:T(1024)(128)(4,1)S(1)} %get-tuple-element.22, pred[1024]{0:T(1024)(128)(4,1)S(1)} %get-tuple-element.23, bf16[8,128,512]{1,2,0:T(8,128)(2,1)} %copy-done.3), kind=kLoop, calls=%fused_computation.5 | loop fusion | flops 1048576 | bytes 4196352 | tf_op jit(solution)/shard_map/transpose | solution.py:206
  257.5 12.0 %weight_grads.1 = (bf16[832,256]{1,0:T(8,128)(2,1)}, bf16[832,256]{1,0:T(8,128)(2,1)}, bf16[832,512]{1,0:T(8,128)(2,1)}) custom-call(bf16[4,256,832]{2,1,0:T(8,128)(2,1)} %copy.40.head_ref.head_own, bf16[4,256,832]{2,1,0:T(8,128)(2,1)} %bitcast.19.head_away, bf16[4,8,2,32,832]{4,3,2,1,0:T(8,128)(2,1)} %all-gather.5.cloned.1.call-done.saved_ref.saved_own, ...), custom_call_target="tpu_custom_call" | custom-call | flops 3489660928 | bytes 13369344 | tf_op jit(solution)/shard_map/weight_grads/pallas_call | solution.py:143
  271.3 2.1 reduce_sum.58
  (71 shorter events, 29.8 us)
Async XLA Ops:
  7.2 22.9 %copy-start = (bf16[832,512]{1,0:T(8,128)(2,1)S(1)}, bf16[832,512]{1,0:T(8,128)(2,1)}, u32[]{:S(2)}) copy-start(bf16[832,512]{1,0:T(8,128)(2,1)} %param.15) | copy-start | bytes 2555908
  7.2 83.9 %all-gather.9.cloned.1.call-start = ((), (), s32[]{:S(2)}) async-start(), calls=%async_computation.8 | async-start | bytes 1949696 | tf_op jit(solution)/shard_map/all_gather | solution.py:184
  8.8 7.4 %copy-start.8 = (s32[4]{0:T(128)S(1)}, s32[4]{0:T(128)}, u32[]{:S(2)}) copy-start(s32[4]{0:T(128)} %param.16) | copy-start | bytes 52
  8.8 7.5 %copy-start.9 = (s32[8]{0:T(128)S(1)}, s32[8]{0:T(128)}, u32[]{:S(2)}) copy-start(s32[8]{0:T(128)} %param.17) | copy-start | bytes 100
  11.0 19.1 %all-to-all-start = ((bf16[8,128,512]{1,2,0:T(8,128)(2,1)}), bf16[8,128,512]{1,2,0:T(8,128)(2,1)S(1)}, u32[]{:S(2)}, u32[]{:S(2)}) async-start(bf16[8,128,512]{1,2,0:T(8,128)(2,1)} %broadcast_in_dim.97), calls=%async_computation | async-start | bytes 2097152 | tf_op jit(solution)/shard_map/all_to_all | solution.py:42
  30.1 1.1 copy-start.3
  32.5 8.3 %copy-start.7 = (bf16[128,512]{1,0:T(8,128)(2,1)S(1)}, bf16[128,512]{1,0:T(8,128)(2,1)}, u32[]{:S(2)}) copy-start(bf16[128,512]{1,0:T(8,128)(2,1)} %param.9) | copy-start | bytes 393220
  32.5 8.3 %copy-start.4 = (bf16[128,512]{1,0:T(8,128)(2,1)S(1)}, bf16[128,512]{1,0:T(8,128)(2,1)}, u32[]{:S(2)}) copy-start(bf16[128,512]{1,0:T(8,128)(2,1)} %param.10) | copy-start | bytes 393220
  32.5 27.7 %all-to-all-start.1 = ((bf16[4,256,832]{1,2,0:T(8,128)(2,1)}), bf16[4,256,832]{1,2,0:T(8,128)(2,1)S(1)}, u32[]{:S(2)}, u32[]{:S(2)}) async-start(bf16[4,256,832]{1,2,0:T(8,128)(2,1)} %bitcast.64), calls=%async_computation.1 | async-start | bytes 3407872 | tf_op jit(solution)/shard_map/all_to_all | solution.py:47
  40.8 198.7 %all-gather.5.cloned.1.call-start = ((), (), s32[]{:S(2)}) async-start(), calls=%async_computation.6 | async-start | bytes 4587520 | tf_op jit(solution)/shard_map/all_gather | solution.py:196
  40.8 19.9 %collective-permute-start = (bf16[128,768]{1,0:T(8,128)(2,1)S(1)}, bf16[128,768]{1,0:T(8,128)(2,1)S(1)}, u32[]{:S(2)}, u32[]{:S(2)}) collective-permute-start(bf16[128,768]{1,0:T(8,128)(2,1)S(1)} %pad_maximum_fusion.1), channel_id=1, source_target_pairs={{0,256},{256,0},{1,257},{257,1},{2,258},{258,2},{3,259},{259,3},{4... | collective-permute-start | bytes 589832 | tf_op jit(solution)/shard_map/ppermute | solution.py:37
  60.7 33.1 %copy-start.5 = (bf16[128,768]{1,0:T(8,128)(2,1)}, bf16[128,768]{1,0:T(8,128)(2,1)S(1)}, u32[]{:S(2)}) copy-start(bf16[128,768]{1,0:T(8,128)(2,1)S(1)} %collective-permute-done) | copy-start | bytes 589828
  94.9 20.2 %all-to-all-start.2 = ((bf16[8,32,832]{2,1,0:T(8,128)(2,1)}), bf16[8,32,832]{2,1,0:T(8,128)(2,1)S(1)}, u32[]{:S(2)}, u32[]{:S(2)}) async-start(bf16[8,32,832]{2,1,0:T(8,128)(2,1)} %bitcast), calls=%async_computation.2 | async-start | bytes 917504 | tf_op jit(solution)/shard_map/all_to_all | solution.py:47
  100.4 157.1 %all-gather.7.cloned.1.call-start = ((), (), s32[]{:S(2)}) async-start(), calls=%async_computation.7 | async-start | bytes 4587520 | tf_op jit(solution)/shard_map/all_gather | solution.py:197
  147.5 4.1 %copy-start.6 = (bf16[128,768]{1,0:T(8,128)(2,1)S(1)}, bf16[128,768]{1,0:T(8,128)(2,1)}, u32[]{:S(2)}) copy-start(bf16[128,768]{1,0:T(8,128)(2,1)} %copy-done.5) | copy-start | bytes 589828
  147.5 15.5 %all-to-all-start.3 = ((bf16[4,256,832]{1,2,0:T(8,128)(2,1)}), bf16[4,256,832]{1,2,0:T(8,128)(2,1)S(1)}, u32[]{:S(2)}, u32[]{:S(2)}) async-start(bf16[4,256,832]{1,2,0:T(8,128)(2,1)} %broadcast_in_dim.100), calls=%async_computation.3 | async-start | bytes 3407872 | tf_op jit(solution)/shard_map/all_to_all | solution.py:42
  163.1 1.9 copy-start.2
  165.0 72.7 %all-to-all-start.5 = ((bf16[8,128,1024]{1,2,0:T(8,128)(2,1)}), bf16[8,128,1024]{1,2,0:T(8,128)(2,1)S(1)}, u32[]{:S(2)}, u32[]{:S(2)}) async-start(bf16[8,128,1024]{1,2,0:T(8,128)(2,1)} %broadcast_in_dim.106), calls=%async_computation.5 | async-start | bytes 4194304 | tf_op jit(solution)/shard_map/all_to_all | solution.py:42
  200.2 17.9 %collective-permute-start.1 = (bf16[2,128,832]{2,1,0:T(8,128)(2,1)S(1)}, bf16[2,128,832]{2,1,0:T(8,128)(2,1)}, u32[]{:S(2)}, u32[]{:S(2)}) collective-permute-start(bf16[2,128,832]{2,1,0:T(8,128)(2,1)S(1)} %bitcast.67), channel_id=1, source_target_pairs={{0,8},{8,16},{16,24},{24,0},{1,9},{9,17},{17,25},{25,1},{2,10},{10... | collective-permute-start | bytes 1277960 | tf_op jit(solution)/shard_map/ppermute | solution.py:37
  204.9 18.1 %collective-permute-start.2 = (bf16[2,128,832]{2,1,0:T(8,128)(2,1)S(1)}, bf16[2,128,832]{2,1,0:T(8,128)(2,1)}, u32[]{:S(2)}, u32[]{:S(2)}) collective-permute-start(bf16[2,128,832]{2,1,0:T(8,128)(2,1)S(1)} %bitcast.68), channel_id=1, source_target_pairs={{0,24},{8,0},{16,8},{24,16},{1,25},{9,1},{17,9},{25,17},{2,26},{10... | collective-permute-start | bytes 1277960 | tf_op jit(solution)/shard_map/ppermute | solution.py:37
  219.0 10.6 %collective-permute-start.3 = (bf16[128,832]{1,0:T(8,128)(2,1)S(1)}, bf16[128,832]{1,0:T(8,128)(2,1)S(1)}, u32[]{:S(2)}, u32[]{:S(2)}) collective-permute-start(bf16[128,832]{1,0:T(8,128)(2,1)S(1)} %slice_bitcast_fusion.3), channel_id=1, source_target_pairs={{0,8},{8,16},{16,24},{24,0},{1,9},{9,17},{17,25},{25,1},{2,10},{10... | collective-permute-start | bytes 638984 | tf_op jit(solution)/shard_map/ppermute | solution.py:37
  224.0 9.4 %collective-permute-start.4 = (bf16[128,832]{1,0:T(8,128)(2,1)S(1)}, bf16[128,832]{1,0:T(8,128)(2,1)S(1)}, u32[]{:S(2)}, u32[]{:S(2)}) collective-permute-start(bf16[128,832]{1,0:T(8,128)(2,1)S(1)} %slice_bitcast_fusion.2), channel_id=1, source_target_pairs={{0,24},{8,0},{16,8},{24,16},{1,25},{9,1},{17,9},{25,17},{2,26},{10... | collective-permute-start | bytes 638984 | tf_op jit(solution)/shard_map/ppermute | solution.py:37
  245.8 7.5 %copy-start.1 = (bf16[1024,1024]{0,1:T(8,128)(2,1)S(1)}, bf16[1024,1024]{0,1:T(8,128)(2,1)}, u32[]{:S(2)}) copy-start(bf16[1024,1024]{0,1:T(8,128)(2,1)} %copy_bitcast_fusion) | copy-start | bytes 6291460
  245.8 25.5 %all-to-all-start.4 = ((bf16[8,128,512]{2,1,0:T(8,128)(2,1)}), bf16[8,128,512]{2,1,0:T(8,128)(2,1)}, u32[]{:S(2)}, u32[]{:S(2)}) async-start(bf16[8,128,512]{2,1,0:T(8,128)(2,1)} %bitcast.65), calls=%async_computation.4 | async-start | bytes 2097152 | tf_op jit(solution)/shard_map/all_to_all | solution.py:47
Sparse Core Ops, SparseCore 0:
  10.6 80.3 all-gather.8
  94.0 54.2 all-gather.4
  150.4 61.1 all-gather.6

commit v5 on v4

--- a/solution.py
+++ b/solution.py
@@ -59,7 +59,7 @@
 
 
 def swiglu_terms(saved_ref):
-    pair = saved_ref[0].astype(jnp.float32)
+    pair = saved_ref[0, 0].astype(jnp.float32)
     rows, ffw = pair.shape[0] * pair.shape[2], pair.shape[3]
     gate, up = pair[:, 0].reshape(rows, ffw), pair[:, 1].reshape(rows, ffw)
     sig = jax.nn.sigmoid(gate)
@@ -67,7 +67,7 @@
     return up, sig, silu, up * sig * (1.0 + gate * (1.0 - sig))
 
 
-def input_kernel(head_ref, saved_ref, w_gate_ref, w_up_ref, out_ref):
+def input_kernel(order_ref, head_ref, saved_ref, w_gate_ref, w_up_ref, out_ref):
     head = head_ref[0].astype(jnp.float32)
     _, _, silu, slope = swiglu_terms(saved_ref)
     grad_gate, grad_up = (head * slope).astype(jnp.bfloat16), (head * silu).astype(jnp.bfloat16)
@@ -76,20 +76,29 @@
     out_ref[...] = term.astype(jnp.bfloat16)
 
 
-def input_term(head, saved, w_gate, w_up):
+def saved_spec(saved, which):
+    return pl.BlockSpec(
+        (1, 1) + saved.shape[2:], lambda i, order: (i, order[which], 0, 0, 0, 0)
+    )
+
+
+def input_term(order, head, saved, w_gate, w_up):
     chunks, rows, ffw = head.shape
     width = w_gate.shape[1]
-    whole = pl.BlockSpec((ffw, width), lambda i: (0, 0))
+    whole = pl.BlockSpec((ffw, width), lambda i, order: (0, 0))
     return pl.pallas_call(
         input_kernel,
-        grid=(chunks,),
-        in_specs=[
-            pl.BlockSpec((1, rows, ffw), lambda i: (i, 0, 0)),
-            pl.BlockSpec((1,) + saved.shape[1:], lambda i: (i, 0, 0, 0, 0)),
-            whole,
-            whole,
-        ],
-        out_specs=pl.BlockSpec((rows, width), lambda i: (i, 0)),
+        grid_spec=pltpu.PrefetchScalarGridSpec(
+            num_scalar_prefetch=1,
+            grid=(chunks,),
+            in_specs=[
+                pl.BlockSpec((1, rows, ffw), lambda i, order: (i, 0, 0)),
+                saved_spec(saved, 0),
+                whole,
+                whole,
+            ],
+            out_specs=pl.BlockSpec((rows, width), lambda i, order: (i, 0)),
+        ),
         out_shape=jax.ShapeDtypeStruct((chunks * rows, width), jnp.bfloat16),
         name="input_term",
         cost_estimate=pl.CostEstimate(
@@ -97,11 +106,11 @@
             bytes_accessed=2 * (3 * head.size + 2 * w_gate.size + chunks * rows * width),
             transcendentals=head.size,
         ),
-    )(head, saved, w_gate, w_up)
+    )(order, head, saved, w_gate, w_up)
 
 
 def weight_kernel(
-    scale, head_own, head_away, saved_own, saved_away, act_own, act_away, cot_own, cot_away,
+    scale, order_ref, head_own, head_away, saved_own, saved_away, act_own, act_away, cot_own, cot_away,
     gate_ref, up_ref, down_ref, gate_acc, up_acc, down_acc,
 ):
     @pl.when(pl.program_id(0) == 0)
@@ -131,33 +140,38 @@
         down_ref[...] = (down_acc[...] * scale).T.astype(jnp.bfloat16)
 
 
-def weight_grads(scale, head_own, head_away, saved_own, saved_away, acts, cots):
+def weight_grads(scale, order, head_own, head_away, saved, acts, cots):
     chunks, rows, ffw = head_own.shape
     half, width = acts[0].shape[0], cots[0].shape[0]
-    head_spec = pl.BlockSpec((1, rows, ffw), lambda i: (i, 0, 0))
-    saved_spec = pl.BlockSpec((1,) + saved_own.shape[1:], lambda i: (i, 0, 0, 0, 0))
-    act_spec = pl.BlockSpec((half, rows), lambda i: (0, i))
-    cot_spec = pl.BlockSpec((width, rows), lambda i: (0, i))
-    out = lambda cols: pl.BlockSpec((ffw, cols), lambda i: (0, 0))
+    head_spec = pl.BlockSpec((1, rows, ffw), lambda i, order: (i, 0, 0))
+    act_spec = pl.BlockSpec((half, rows), lambda i, order: (0, i))
+    cot_spec = pl.BlockSpec((width, rows), lambda i, order: (0, i))
+    out = lambda cols: pl.BlockSpec((ffw, cols), lambda i, order: (0, 0))
     shape = lambda cols: jax.ShapeDtypeStruct((ffw, cols), jnp.bfloat16)
     return pl.pallas_call(
         functools.partial(weight_kernel, scale),
-        grid=(chunks,),
-        in_specs=[head_spec] * 2 + [saved_spec] * 2 + [act_spec] * 2 + [cot_spec] * 2,
-        out_specs=[out(half), out(half), out(width)],
+        grid_spec=pltpu.PrefetchScalarGridSpec(
+            num_scalar_prefetch=1,
+            grid=(chunks,),
+            in_specs=[head_spec] * 2
+            + [saved_spec(saved, 0), saved_spec(saved, 1)]
+            + [act_spec] * 2
+            + [cot_spec] * 2,
+            out_specs=[out(half), out(half), out(width)],
+            scratch_shapes=[
+                pltpu.VMEM((half, ffw), jnp.float32),
+                pltpu.VMEM((half, ffw), jnp.float32),
+                pltpu.VMEM((width, ffw), jnp.float32),
+            ],
+        ),
         out_shape=[shape(half), shape(half), shape(width)],
-        scratch_shapes=[
-            pltpu.VMEM((half, ffw), jnp.float32),
-            pltpu.VMEM((half, ffw), jnp.float32),
-            pltpu.VMEM((width, ffw), jnp.float32),
-        ],
         name="weight_grads",
         cost_estimate=pl.CostEstimate(
             flops=4 * chunks * rows * ffw * (2 * half + width),
             bytes_accessed=2 * (6 * head_own.size + 2 * acts[0].size + 2 * cots[0].size),
             transcendentals=2 * head_own.size,
         ),
-    )(head_own, head_away, saved_own, saved_away, *acts, *cots)
+    )(order, head_own, head_away, saved, saved, *acts, *cots)
 
 
 def on_device(
@@ -172,6 +186,7 @@
     tok = rows * n_row
     n_dp = 2
     away = 1 - batch
+    order = jnp.stack([batch, away]).astype(jnp.int32)
 
     def pick(value, index):
         return lax.dynamic_index_in_dim(value, index, 0, keepdims=False)
@@ -181,7 +196,8 @@
     partner = shift(jnp.concatenate([cotangent, act_other], axis=1), "dp", n_dp, 1)
 
     saved = jnp.stack([gate_saved, up_saved])[None]
-    saved = lax.all_gather(saved, ("dp", "z"), axis=0, tiled=True)
+    saved = lax.all_gather(saved, ("x", "dp", "z"), axis=0, tiled=True)
+    saved = saved.reshape(N_X, n_dp, N_Z, 2, own, ffw)
 
     live = live_mask(assignment, pair_lengths, n_dp * tok).reshape(n_dp, tok)
     zero = jnp.zeros((), cotangent.dtype)
@@ -190,11 +206,7 @@
     masked_own = jnp.where(pick(live, batch)[:, None], cot_own, zero)
     block_term = contract_last(masked_own, w_down).astype(jnp.bfloat16)
     head_x = sum_over(block_term, "x", N_X)
-    _, saved, partner = lax.optimization_barrier((head_x, saved, partner))
-    saved = saved.reshape(n_dp, N_Z, 2, own, ffw)
-    saved_own, saved_away = pick(saved, batch), pick(saved, away)
-    saved_own = lax.all_gather(saved_own, "x", axis=0)
-    saved_away = lax.all_gather(saved_away, "x", axis=0)
+    _, partner = lax.optimization_barrier((head_x, partner))
 
     rest = spread(jnp.concatenate([partner, act_own], axis=1), row_axes, n_row)
     rest = rest.reshape(tok, 2 * width)
@@ -213,12 +225,12 @@
     head_away = gather_x(pick(head, away).reshape(halves))
 
     head_away = head_away.reshape(N_X, N_Z * own, ffw)
-    term = input_term(head_own, saved_own, w_gate.T, w_up.T)
+    term = input_term(order, head_own, saved, w_gate.T, w_up.T)
     input_grad = sum_over(term, row_axes, n_row)
 
     scale = 1.0 / math.sqrt(n_dp * tok)
     gate_grad, up_grad, down_grad = weight_grads(
-        scale, head_own, head_away, saved_own, saved_away, acts, cots
+        scale, order, head_own, head_away, saved, acts, cots
     )
     f_half = ffw // 2
     down_grad = lax.dynamic_slice_in_dim(down_grad, batch * f_half, f_half, 0)

time: 281 us -> 243 us (0.86)
  the two profiles are of different devices: /device:TPU:15 before, /device:TPU:1 now
where the time goes in v5:
time: 243 us; the launch traced here: 242 us
  starting transfers between devices  78.4 us (32%)
  blocking collectives  56.1 us (23%)
  waiting for transfers between devices  39.6 us (16%)
  local copies, waits for them, and re-layouts  26 us (11%)
  Pallas kernels  19.9 us (8%)
  between operations  14.2 us (6%)
  other arithmetic  6.5 us (3%)
    all_to_all x3, starting transfers between devices, spread(): return lax.all_to_all(copies, axis, split_axis=0, concat_axis=0, tiled=True)  34.1 us
    all_gather x1, blocking collectives, on_device(): head = lax.all_gather(head, ('dp', 'z'), axis=0, tiled=True)  31.8 us
    all_to_all x1, blocking collectives, sum_over(): lax.all_to_all(blocks, axis, split_axis=0, concat_axis=0, tiled=True)  24.3 us
    ppermute x5, starting transfers between devices, shift(): lax.ppermute(value, axis, [(i, (i + step) % size) for i in range(size)])  22.4 us
    all_to_all x2, starting transfers between devices, sum_over(): lax.all_to_all(blocks, axis, split_axis=0, concat_axis=0, tiled=True)  21.8 us
    all_to_all x3, waiting for transfers between devices, spread(): return lax.all_to_all(copies, axis, split_axis=0, concat_axis=0, tiled=True)  18.5 us
    ppermute x5, waiting for transfers between devices, shift(): lax.ppermute(value, axis, [(i, (i + step) % size) for i in range(size)])  12.8 us
    pallas_call x1, Pallas kernels, weight_grads(): pl.pallas_call(functools.partial(weight_kernel, scale), grid_spec=pltpu.P...  12.8 us
  transfers between devices with their start and end apart: 11, of which 4 were waited for; matrix products, arithmetic and copies ran while one was open for 12% of the time, Pallas kernels for 8%

profile of v5, /device:TPU:1, one launch (start us, length us, event | category | flops | bytes accessed | tf_op | source)
XLA Modules:
  0.0 241.8 jit_solution(12702670631812475758)
XLA Ops:
  11.0 10.3 %all-to-all-start = ((bf16[8,128,512]{1,2,0:T(8,128)(2,1)}), bf16[8,128,512]{1,2,0:T(8,128)(2,1)S(1)}, u32[]{:S(2)}, u32[]{:S(2)}) async-start(bf16[8,128,512]{1,2,0:T(8,128)(2,1)} %broadcast_in_dim.97), calls=%async_computation | async-start | bytes 2097152 | tf_op jit(solution)/shard_map/all_to_all | solution.py:42
  21.9 14.5 %all-to-all-done = bf16[8,128,512]{1,2,0:T(8,128)(2,1)S(1)} async-done(((bf16[8,128,512]{1,2,0:T(8,128)(2,1)}), bf16[8,128,512]{1,2,0:T(8,128)(2,1)S(1)}, u32[]{:S(2)}, u32[]{:S(2)}) %all-to-all-start) | async-done | bytes 1048608 | tf_op jit(solution)/shard_map/all_to_all | solution.py:42
  37.5 24.3 %all_to_all.30 = bf16[4,256,832]{1,2,0:T(8,128)(2,1)S(1)} all-to-all(bf16[4,256,832]{1,2,0:T(8,128)(2,1)S(1)} %bitcast.68), channel_id=1, replica_groups=mesh['dp'=2,'y'=4,'core'=2,'x'=4,'z'=8] {'x'}, dimensions={0} | all-to-all | bytes 3407872 | tf_op jit(solution)/shard_map/all_to_all | solution.py:47
  63.3 8.9 %all-to-all-start.2 = ((bf16[8,32,832]{2,1,0:T(8,128)(2,1)}), bf16[8,32,832]{2,1,0:T(8,128)(2,1)S(1)}, u32[]{:S(2)}, u32[]{:S(2)}) async-start(bf16[8,32,832]{2,1,0:T(8,128)(2,1)} %bitcast.2), calls=%async_computation.2 | async-start | bytes 917504 | tf_op jit(solution)/shard_map/all_to_all | solution.py:47
  72.3 8.0 %collective-permute-start.4 = (bf16[128,768]{1,0:T(8,128)(2,1)S(1)}, bf16[128,768]{1,0:T(8,128)(2,1)S(1)}, u32[]{:S(2)}, u32[]{:S(2)}) collective-permute-start(bf16[128,768]{1,0:T(8,128)(2,1)S(1)} %pad_maximum_fusion.1), channel_id=1, source_target_pairs={{0,256},{256,0},{1,257},{257,1},{2,258},{258,2},{3,259},{259,3},{4... | collective-permute-start | bytes 589832 | tf_op jit(solution)/shard_map/ppermute | solution.py:37
  80.3 12.8 %collective-permute-done.4 = bf16[128,768]{1,0:T(8,128)(2,1)S(1)} collective-permute-done((bf16[128,768]{1,0:T(8,128)(2,1)S(1)}, bf16[128,768]{1,0:T(8,128)(2,1)S(1)}, u32[]{:S(2)}, u32[]{:S(2)}) %collective-permute-start.4) | collective-permute-done | bytes 196640 | tf_op jit(solution)/shard_map/ppermute | solution.py:37
  93.2 8.3 %all-to-all-done.2 = bf16[8,32,832]{2,1,0:T(8,128)(2,1)S(1)} async-done(((bf16[8,32,832]{2,1,0:T(8,128)(2,1)}), bf16[8,32,832]{2,1,0:T(8,128)(2,1)S(1)}, u32[]{:S(2)}, u32[]{:S(2)}) %all-to-all-start.2) | async-done | bytes 426016 | tf_op jit(solution)/shard_map/all_to_all | solution.py:47
  103.2 19.4 %all-to-all-start.5 = ((bf16[8,128,1024]{1,2,0:T(8,128)(2,1)}), bf16[8,128,1024]{1,2,0:T(8,128)(2,1)S(1)}, u32[]{:S(2)}, u32[]{:S(2)}) async-start(bf16[8,128,1024]{1,2,0:T(8,128)(2,1)} %broadcast_in_dim.106), calls=%async_computation.5 | async-start | bytes 4194304 | tf_op jit(solution)/shard_map/all_to_all | solution.py:42
  123.3 31.8 %all_gather.6 = bf16[512,832]{1,0:T(8,128)(2,1)S(1)} all-gather(bf16[32,832]{1,0:T(8,128)(2,1)S(1)} %reduce_sum.57), channel_id=1, replica_groups=mesh['dp'=2,'y'=4,'core'=2,'x'=4,'z'=8] {'dp','z'}, dimensions={0}, use_global_device_ids=true | all-gather | bytes 905216 | tf_op jit(solution)/shard_map/all_gather | solution.py:221
  156.0 4.7 %collective-permute-start = (bf16[2,128,832]{2,1,0:T(8,128)(2,1)S(1)}, bf16[2,128,832]{2,1,0:T(8,128)(2,1)}, u32[]{:S(2)}, u32[]{:S(2)}) collective-permute-start(bf16[2,128,832]{2,1,0:T(8,128)(2,1)S(1)} %bitcast.71), channel_id=1, source_target_pairs={{0,8},{8,16},{16,24},{24,0},{1,9},{9,17},{17,25},{25,1},{2,10},{10... | collective-permute-start | bytes 1277960 | tf_op jit(solution)/shard_map/ppermute | solution.py:37
  160.6 3.3 %collective-permute-start.1 = (bf16[2,128,832]{2,1,0:T(8,128)(2,1)S(1)}, bf16[2,128,832]{2,1,0:T(8,128)(2,1)}, u32[]{:S(2)}, u32[]{:S(2)}) collective-permute-start(bf16[2,128,832]{2,1,0:T(8,128)(2,1)S(1)} %bitcast.72), channel_id=1, source_target_pairs={{0,24},{8,0},{16,8},{24,16},{1,25},{9,1},{17,9},{25,17},{2,26},{10... | collective-permute-start | bytes 1277960 | tf_op jit(solution)/shard_map/ppermute | solution.py:37
  163.9 2.0 copy.39
  168.2 2.4 broadcast_in_dim.100
  170.6 4.4 %all-to-all-start.3 = ((bf16[4,256,832]{1,2,0:T(8,128)(2,1)}), bf16[4,256,832]{1,2,0:T(8,128)(2,1)}, u32[]{:S(2)}, u32[]{:S(2)}) async-start(bf16[4,256,832]{1,2,0:T(8,128)(2,1)} %broadcast_in_dim.100), calls=%async_computation.3 | async-start | bytes 3407872 | tf_op jit(solution)/shard_map/all_to_all | solution.py:42
  180.0 3.4 %collective-permute-start.2 = (bf16[128,832]{1,0:T(8,128)(2,1)S(1)}, bf16[128,832]{1,0:T(8,128)(2,1)S(1)}, u32[]{:S(2)}, u32[]{:S(2)}) collective-permute-start(bf16[128,832]{1,0:T(8,128)(2,1)S(1)} %slice_bitcast_fusion.3), channel_id=1, source_target_pairs={{0,8},{8,16},{16,24},{24,0},{1,9},{9,17},{17,25},{25,1},{2,10},{10... | collective-permute-start | bytes 638984 | tf_op jit(solution)/shard_map/ppermute | solution.py:37
  184.4 3.1 %collective-permute-start.3 = (bf16[128,832]{1,0:T(8,128)(2,1)S(1)}, bf16[128,832]{1,0:T(8,128)(2,1)S(1)}, u32[]{:S(2)}, u32[]{:S(2)}) collective-permute-start(bf16[128,832]{1,0:T(8,128)(2,1)S(1)} %slice_bitcast_fusion.2), channel_id=1, source_target_pairs={{0,24},{8,0},{16,8},{24,16},{1,25},{9,1},{17,9},{25,17},{2,26},{10... | collective-permute-start | bytes 638984 | tf_op jit(solution)/shard_map/ppermute | solution.py:37
  187.5 4.1 %all-to-all-done.3 = bf16[4,256,832]{1,2,0:T(8,128)(2,1)} async-done(((bf16[4,256,832]{1,2,0:T(8,128)(2,1)}), bf16[4,256,832]{1,2,0:T(8,128)(2,1)}, u32[]{:S(2)}, u32[]{:S(2)}) %all-to-all-start.3) | async-done | bytes 1703968 | tf_op jit(solution)/shard_map/all_to_all | solution.py:42
  191.6 3.5 %copy.40.head_ref.head_own = bf16[4,256,832]{2,1,0:T(8,128)(2,1)} copy(bf16[4,256,832]{1,2,0:T(8,128)(2,1)} %all-to-all-done.3) | data formatting | bytes 3407872 | tf_op jit(solution)/shard_map/all_to_all | solution.py:42
  195.0 7.1 %input_term.1 = bf16[1024,512]{1,0:T(8,128)(2,1)} custom-call(s32[2]{0:T(128)} %pad_add_fusion.order_ref, bf16[4,256,832]{2,1,0:T(8,128)(2,1)} %copy.40.head_ref.head_own, bf16[4,2,8,2,32,832]{5,4,3,2,1,0:T(8,128)(2,1)} %bitcast.65, bf16[832,512]{1,0:T(8,128)(2,1)} %bitcast.76, bf16[832,512]{1,0:T(8,128)(2,1)} %bitcast.77), custom_call_target="tpu_custom_call" | custom-call | flops 1744830464 | bytes 7864320 | tf_op jit(solution)/shard_map/input_term/pallas_call | solution.py:89
  202.2 12.9 %all-to-all-start.4 = ((bf16[8,128,512]{2,1,0:T(8,128)(2,1)}), bf16[8,128,512]{2,1,0:T(8,128)(2,1)S(1)}, u32[]{:S(2)}, u32[]{:S(2)}) async-start(bf16[8,128,512]{2,1,0:T(8,128)(2,1)} %bitcast.69), calls=%async_computation.4 | async-start | bytes 2097152 | tf_op jit(solution)/shard_map/all_to_all | solution.py:47
  215.1 1.8 bitcast_dynamic-update-slice_fusion.1
  216.9 1.8 bitcast_dynamic-update-slice_fusion
  219.6 12.8 %weight_grads.1 = (bf16[832,256]{1,0:T(8,128)(2,1)}, bf16[832,256]{1,0:T(8,128)(2,1)}, bf16[832,512]{1,0:T(8,128)(2,1)}) custom-call(s32[2]{0:T(128)} %pad_add_fusion.order_ref, bf16[4,256,832]{2,1,0:T(8,128)(2,1)} %copy.40.head_ref.head_own, bf16[4,256,832]{2,1,0:T(8,128)(2,1)} %bitcast.20.head_away, bf16[4,2,8,2,32,832]{5,4,3,2,1,0:T(8,128)(2,1)} %bitcast.66, ...), custom_call_target="tpu_custom_call" | custom-call | flops 3489660928 | bytes 13369344 | tf_op jit(solution)/shard_map/weight_grads/pallas_call | solution.py:151
  232.3 1.8 constant_dynamic-slice_fusion
  (58 shorter events, 20.3 us)
Async XLA Ops:
  7.2 29.2 %copy-start = (bf16[832,512]{1,0:T(8,128)(2,1)S(1)}, bf16[832,512]{1,0:T(8,128)(2,1)}, u32[]{:S(2)}) copy-start(bf16[832,512]{1,0:T(8,128)(2,1)} %param.15) | copy-start | bytes 2555908
  7.2 187.9 %all-gather.3.cloned.1.call-start = ((), (), s32[]{:S(2)}) async-start(), calls=%async_computation.6 | async-start | bytes 7454720 | tf_op jit(solution)/shard_map/all_gather | solution.py:199
  8.8 12.5 %copy-start.5 = (s32[4]{0:T(128)S(1)}, s32[4]{0:T(128)}, u32[]{:S(2)}) copy-start(s32[4]{0:T(128)} %param.16) | copy-start | bytes 52
  8.8 12.6 %copy-start.6 = (s32[8]{0:T(128)S(1)}, s32[8]{0:T(128)}, u32[]{:S(2)}) copy-start(s32[8]{0:T(128)} %param.17) | copy-start | bytes 100
  11.0 25.3 %all-to-all-start = ((bf16[8,128,512]{1,2,0:T(8,128)(2,1)}), bf16[8,128,512]{1,2,0:T(8,128)(2,1)S(1)}, u32[]{:S(2)}, u32[]{:S(2)}) async-start(bf16[8,128,512]{1,2,0:T(8,128)(2,1)} %broadcast_in_dim.97), calls=%async_computation | async-start | bytes 2097152 | tf_op jit(solution)/shard_map/all_to_all | solution.py:42
  36.3 1.1 copy-start.1
  61.8 10.4 %copy-start.4 = (bf16[128,512]{1,0:T(8,128)(2,1)S(1)}, bf16[128,512]{1,0:T(8,128)(2,1)}, u32[]{:S(2)}) copy-start(bf16[128,512]{1,0:T(8,128)(2,1)} %param.9) | copy-start | bytes 393220
  61.8 10.5 %copy-start.3 = (bf16[128,512]{1,0:T(8,128)(2,1)S(1)}, bf16[128,512]{1,0:T(8,128)(2,1)}, u32[]{:S(2)}) copy-start(bf16[128,512]{1,0:T(8,128)(2,1)} %param.10) | copy-start | bytes 393220
  63.3 38.2 %all-to-all-start.2 = ((bf16[8,32,832]{2,1,0:T(8,128)(2,1)}), bf16[8,32,832]{2,1,0:T(8,128)(2,1)S(1)}, u32[]{:S(2)}, u32[]{:S(2)}) async-start(bf16[8,32,832]{2,1,0:T(8,128)(2,1)} %bitcast.2), calls=%async_computation.2 | async-start | bytes 917504 | tf_op jit(solution)/shard_map/all_to_all | solution.py:47
  72.3 20.7 %collective-permute-start.4 = (bf16[128,768]{1,0:T(8,128)(2,1)S(1)}, bf16[128,768]{1,0:T(8,128)(2,1)S(1)}, u32[]{:S(2)}, u32[]{:S(2)}) collective-permute-start(bf16[128,768]{1,0:T(8,128)(2,1)S(1)} %pad_maximum_fusion.1), channel_id=1, source_target_pairs={{0,256},{256,0},{1,257},{257,1},{2,258},{258,2},{3,259},{259,3},{4... | collective-permute-start | bytes 589832 | tf_op jit(solution)/shard_map/ppermute | solution.py:37
  103.2 65.0 %all-to-all-start.5 = ((bf16[8,128,1024]{1,2,0:T(8,128)(2,1)}), bf16[8,128,1024]{1,2,0:T(8,128)(2,1)S(1)}, u32[]{:S(2)}, u32[]{:S(2)}) async-start(bf16[8,128,1024]{1,2,0:T(8,128)(2,1)} %broadcast_in_dim.106), calls=%async_computation.5 | async-start | bytes 4194304 | tf_op jit(solution)/shard_map/all_to_all | solution.py:42
  156.0 23.1 %collective-permute-start = (bf16[2,128,832]{2,1,0:T(8,128)(2,1)S(1)}, bf16[2,128,832]{2,1,0:T(8,128)(2,1)}, u32[]{:S(2)}, u32[]{:S(2)}) collective-permute-start(bf16[2,128,832]{2,1,0:T(8,128)(2,1)S(1)} %bitcast.71), channel_id=1, source_target_pairs={{0,8},{8,16},{16,24},{24,0},{1,9},{9,17},{17,25},{25,1},{2,10},{10... | collective-permute-start | bytes 1277960 | tf_op jit(solution)/shard_map/ppermute | solution.py:37
  160.6 22.8 %collective-permute-start.1 = (bf16[2,128,832]{2,1,0:T(8,128)(2,1)S(1)}, bf16[2,128,832]{2,1,0:T(8,128)(2,1)}, u32[]{:S(2)}, u32[]{:S(2)}) collective-permute-start(bf16[2,128,832]{2,1,0:T(8,128)(2,1)S(1)} %bitcast.72), channel_id=1, source_target_pairs={{0,24},{8,0},{16,8},{24,16},{1,25},{9,1},{17,9},{25,17},{2,26},{10... | collective-permute-start | bytes 1277960 | tf_op jit(solution)/shard_map/ppermute | solution.py:37
  170.6 21.0 %all-to-all-start.3 = ((bf16[4,256,832]{1,2,0:T(8,128)(2,1)}), bf16[4,256,832]{1,2,0:T(8,128)(2,1)}, u32[]{:S(2)}, u32[]{:S(2)}) async-start(bf16[4,256,832]{1,2,0:T(8,128)(2,1)} %broadcast_in_dim.100), calls=%async_computation.3 | async-start | bytes 3407872 | tf_op jit(solution)/shard_map/all_to_all | solution.py:42
  175.0 1.2 copy-start.2
  180.0 38.7 %collective-permute-start.2 = (bf16[128,832]{1,0:T(8,128)(2,1)S(1)}, bf16[128,832]{1,0:T(8,128)(2,1)S(1)}, u32[]{:S(2)}, u32[]{:S(2)}) collective-permute-start(bf16[128,832]{1,0:T(8,128)(2,1)S(1)} %slice_bitcast_fusion.3), channel_id=1, source_target_pairs={{0,8},{8,16},{16,24},{24,0},{1,9},{9,17},{17,25},{25,1},{2,10},{10... | collective-permute-start | bytes 638984 | tf_op jit(solution)/shard_map/ppermute | solution.py:37
  184.4 34.4 %collective-permute-start.3 = (bf16[128,832]{1,0:T(8,128)(2,1)S(1)}, bf16[128,832]{1,0:T(8,128)(2,1)S(1)}, u32[]{:S(2)}, u32[]{:S(2)}) collective-permute-start(bf16[128,832]{1,0:T(8,128)(2,1)S(1)} %slice_bitcast_fusion.2), channel_id=1, source_target_pairs={{0,24},{8,0},{16,8},{24,16},{1,25},{9,1},{17,9},{25,17},{2,26},{10... | collective-permute-start | bytes 638984 | tf_op jit(solution)/shard_map/ppermute | solution.py:37
  202.2 31.9 %all-to-all-start.4 = ((bf16[8,128,512]{2,1,0:T(8,128)(2,1)}), bf16[8,128,512]{2,1,0:T(8,128)(2,1)S(1)}, u32[]{:S(2)}, u32[]{:S(2)}) async-start(bf16[8,128,512]{2,1,0:T(8,128)(2,1)} %bitcast.69), calls=%async_computation.4 | async-start | bytes 2097152 | tf_op jit(solution)/shard_map/all_to_all | solution.py:47
Sparse Core Ops, SparseCore 0:
  11.5 175.5 all-gather.2

commit v6 on v5

v6 whole, which is shorter than its diff:
```python
import functools
import math
import jax
import jax.numpy as jnp
from jax import lax
from jax.experimental import pallas as pl
from jax.experimental.pallas import tpu as pltpu
from jax.sharding import Mesh, PartitionSpec as P

N_Y, N_CORE, N_X, N_Z = 4, 2, 4, 8


def shift(value, axis, size, step):
    return lax.ppermute(value, axis, [(i, (i + step) % size) for i in range(size)])


def spread(value, axis, size):
    copies = jnp.broadcast_to(value[None], (size,) + value.shape)
    return lax.all_to_all(copies, axis, split_axis=0, concat_axis=0, tiled=True)


def sum_over(value, axis, size):
    blocks = value.reshape(size, value.shape[0] // size, value.shape[1])
    received = lax.all_to_all(blocks, axis, split_axis=0, concat_axis=0, tiled=True)
    return jnp.sum(received, axis=0, dtype=jnp.float32).astype(jnp.bfloat16)


def live_length(order_ref, assignment_ref, lengths_ref, which, chunk):
    slot = 2 * order_ref[which] + lax.div(chunk, 2)
    return lengths_ref[2 * assignment_ref[slot] + lax.rem(chunk, 2)]


def rows_below(shape, count):
    return lax.broadcasted_iota(jnp.int32, shape, 0) < count


def head_kernel(order_ref, assignment_ref, lengths_ref, cot_ref, w_ref, out_ref):
    live = live_length(order_ref, assignment_ref, lengths_ref, 0, pl.program_id(0))
    cot = cot_ref[...]
    masked = jnp.where(rows_below(cot.shape, live), cot, jnp.zeros_like(cot))
    term = lax.dot_general(
        masked, w_ref[...], (((1,), (1,)), ((), ())), preferred_element_type=jnp.float32
    )
    ffw = w_ref.shape[0]
    out_ref[0, :, :ffw] = term.astype(jnp.bfloat16)
    out_ref[0, :, ffw:] = jnp.zeros((term.shape[0], out_ref.shape[2] - ffw), jnp.bfloat16)


def head_term(scalars, cot, w_down, lanes):
    tok, width = cot.shape
    ffw = w_down.shape[0]
    rows = tok // N_X
    return pl.pallas_call(
        head_kernel,
        grid_spec=pltpu.PrefetchScalarGridSpec(
            num_scalar_prefetch=3,
            grid=(N_X,),
            in_specs=[
                pl.BlockSpec((rows, width), lambda i, *_: (i, 0)),
                pl.BlockSpec((ffw, width), lambda i, *_: (0, 0)),
            ],
            out_specs=pl.BlockSpec((1, rows, lanes), lambda i, *_: (i, 0, 0)),
        ),
        out_shape=jax.ShapeDtypeStruct((N_X, rows, lanes), jnp.bfloat16),
        name="head_term",
        cost_estimate=pl.CostEstimate(
            flops=2 * tok * width * ffw,
            bytes_accessed=2 * (cot.size + w_down.size + tok * lanes),
            transcendentals=0,
        ),
    )(*scalars, cot, w_down)


def swiglu_terms(saved_ref):
    pair = saved_ref[0, 0].astype(jnp.float32)
    rows, ffw = pair.shape[0] * pair.shape[2], pair.shape[3]
    gate, up = pair[:, 0].reshape(rows, ffw), pair[:, 1].reshape(rows, ffw)
    sig = jax.nn.sigmoid(gate)
    silu = gate * sig
    return up, silu, up * sig * (1.0 + gate * (1.0 - sig))


def input_kernel(order_ref, head_ref, saved_ref, w_gate_ref, w_up_ref, out_ref):
    ffw = w_gate_ref.shape[0]
    head = head_ref[0, :, :ffw].astype(jnp.float32)
    _, silu, slope = swiglu_terms(saved_ref)
    grad_gate, grad_up = (head * slope).astype(jnp.bfloat16), (head * silu).astype(jnp.bfloat16)
    term = jnp.dot(grad_gate, w_gate_ref[...], preferred_element_type=jnp.float32)
    term += jnp.dot(grad_up, w_up_ref[...], preferred_element_type=jnp.float32)
    out_ref[...] = term.astype(jnp.bfloat16)


def input_term(order, head, saved, w_gate, w_up):
    chunks, rows, lanes = head.shape
    ffw, width = w_gate.shape
    whole = pl.BlockSpec((ffw, width), lambda i, order: (0, 0))
    return pl.pallas_call(
        input_kernel,
        grid_spec=pltpu.PrefetchScalarGridSpec(
            num_scalar_prefetch=1,
            grid=(chunks,),
            in_specs=[
                pl.BlockSpec((1, rows, lanes), lambda i, order: (i, 0, 0)),
                pl.BlockSpec(
                    (1, 1) + saved.shape[2:], lambda i, order: (i, order[0], 0, 0, 0, 0)
                ),
                whole,
                whole,
            ],
            out_specs=pl.BlockSpec((rows, width), lambda i, order: (i, 0)),
        ),
        out_shape=jax.ShapeDtypeStruct((chunks * rows, width), jnp.bfloat16),
        name="input_term",
        cost_estimate=pl.CostEstimate(
            flops=4 * chunks * rows * ffw * width,
            bytes_accessed=2 * (3 * head.size + 2 * w_gate.size + chunks * rows * width),
            transcendentals=head.size,
        ),
    )(order, head, saved, w_gate, w_up)


def weight_kernel(
    scale, order_ref, assignment_ref, lengths_ref,
    head_own, here, left, right, far_low, far_high,
    saved_own, saved_away, act_own, act_away, cot_own, cot_away,
    gate_ref, up_ref, down_ref, gate_acc, up_acc, down_acc, head_away,
):
    step = pl.program_id(0)
    chunk = order_ref[2 + step]
    mid = far_low.shape[0]

    @pl.when(step == 0)
    def _():
        gate_acc[...] = jnp.zeros_like(gate_acc)
        up_acc[...] = jnp.zeros_like(up_acc)
        down_acc[...] = jnp.zeros_like(down_acc)

    for index, part in enumerate((here, left, right)):
        @pl.when(step == index)
        def _(part=part):
            head_away[:mid, :] = part[0]
            head_away[mid:, :] = part[1]

    @pl.when(step == 3)
    def _():
        head_away[:mid, :] = far_low[...]
        head_away[mid:, :] = far_high[...]

    def contract(left_rows, right_rows):
        return lax.dot_general(
            left_rows, right_rows, (((0,), (0,)), ((), ())), preferred_element_type=jnp.float32
        )

    ffw = gate_acc.shape[1]
    for which, head_rows, saved_ref, act_ref, cot_ref in (
        (0, head_own[0], saved_own, act_own, cot_own),
        (1, head_away[...], saved_away, act_away, cot_away),
    ):
        head = head_rows[:, :ffw].astype(jnp.float32)
        up, silu, slope = swiglu_terms(saved_ref)
        live = live_length(order_ref, assignment_ref, lengths_ref, which, chunk)
        cot = cot_ref[...]
        masked = jnp.where(rows_below(cot.shape, live), cot, jnp.zeros_like(cot))
        act = act_ref[...]
        gate_acc[...] += contract(act, (head * slope).astype(jnp.bfloat16))
        up_acc[...] += contract(act, (head * silu).astype(jnp.bfloat16))
        down_acc[...] += contract((silu * up).astype(jnp.bfloat16), masked)

    @pl.when(step == pl.num_programs(0) - 1)
    def _():
        gate_ref[...] = (gate_acc[...] * scale).T.astype(jnp.bfloat16)
        up_ref[...] = (up_acc[...] * scale).T.astype(jnp.bfloat16)
        f_half = down_ref.shape[0]
        first = pl.multiple_of(order_ref[0] * f_half, f_half)
        down_ref[...] = (down_acc[pl.ds(first, f_half), :] * scale).astype(jnp.bfloat16)


def weight_grads(scale, scalars, head_own, head_away, saved, cot, rest):
    chunks, rows, lanes = head_own.shape
    ffw, width = saved.shape[-1], cot.shape[1]
    half = width // 2
    whole = lambda value: pl.BlockSpec(value.shape, lambda i, *_: (0,) * value.ndim)
    saved_spec = lambda which: pl.BlockSpec(
        (1, 1) + saved.shape[2:],
        lambda i, order, *_: (order[2 + i], order[which], 0, 0, 0, 0),
    )
    column = lambda cols, index: pl.BlockSpec(
        (rows, cols), lambda i, order, *_: (order[2 + i], index)
    )
    out = lambda *shape: pl.BlockSpec(shape, lambda i, *_: (0, 0))
    shape = lambda *dims: jax.ShapeDtypeStruct(dims, jnp.bfloat16)
    return pl.pallas_call(
        functools.partial(weight_kernel, scale),
        grid_spec=pltpu.PrefetchScalarGridSpec(
            num_scalar_prefetch=3,
            grid=(chunks,),
            in_specs=[pl.BlockSpec((1, rows, lanes), lambda i, order, *_: (order[2 + i], 0, 0))]
            + [whole(part) for part in head_away]
            + [saved_spec(0), saved_spec(1)]
            + [column(half, 3), column(half, 2), column(width, 0), column(width, 0)],
            out_specs=[out(ffw, half), out(ffw, half), out(ffw // 2, width)],
            scratch_shapes=[
                pltpu.VMEM((half, ffw), jnp.float32),
                pltpu.VMEM((half, ffw), jnp.float32),
                pltpu.VMEM((ffw, width), jnp.float32),
                pltpu.VMEM((rows, lanes), jnp.bfloat16),
            ],
        ),
        out_shape=[shape(ffw, half), shape(ffw, half), shape(ffw // 2, width)],
        name="weight_grads",
        cost_estimate=pl.CostEstimate(
            flops=4 * chunks * rows * ffw * 2 * width,
            bytes_accessed=2 * (6 * head_own.size + cot.size + rest.size),
            transcendentals=2 * head_own.size,
        ),
    )(*scalars, head_own, *head_away, saved, saved, rest, rest, cot, rest)


def on_device(
    activations, cotangent, gate_saved, up_saved, w_gate, w_up, w_down, assignment, pair_lengths
):
    batch, x = lax.axis_index("dp"), lax.axis_index("x")
    away = 1 - batch
    rows, width = cotangent.shape
    half = width // 2
    own, ffw = gate_saved.shape
    lanes = -(-ffw // 128) * 128
    row_axes = ("y", "core")
    n_row = N_Y * N_CORE
    tok = rows * n_row
    n_dp = 2
    order = jnp.stack([batch, away] + [(x + step) % N_X for step in (0, N_X - 1, 1, 2)])
    order = order.astype(jnp.int32)
    scalars = (order, assignment, pair_lengths)

    def pick(value, index):
        return lax.dynamic_index_in_dim(value, index, 0, keepdims=False)

    act_own = lax.dynamic_slice_in_dim(activations, batch * half, half, 1)
    act_other = lax.dynamic_slice_in_dim(activations, away * half, half, 1)
    partner = shift(jnp.concatenate([cotangent, act_other], axis=1), "dp", n_dp, 1)

    saved = jnp.stack([gate_saved, up_saved])[None]
    saved = lax.all_gather(saved, ("x", "dp", "z"), axis=0, tiled=True)
    saved = saved.reshape(N_X, n_dp, N_Z, 2, own, ffw)

    cot_own = spread(cotangent, row_axes, n_row).reshape(tok, width)
    block_term = head_term(scalars, cot_own, w_down, lanes)
    head_x = sum_over(block_term.reshape(tok, lanes), "x", N_X)
    _, partner = lax.optimization_barrier((head_x, partner))
    rest = spread(jnp.concatenate([partner, act_own], axis=1), row_axes, n_row)
    rest = rest.reshape(tok, 2 * width)

    head = sum_over(head_x, "z", N_Z)
    head = lax.all_gather(head, ("dp", "z"), axis=0, tiled=True)
    head = head.reshape(n_dp, N_Z * own, lanes)
    head_own = spread(pick(head, batch), "x", N_X)
    here = pick(head, away).reshape(2, N_Z * own // 2, lanes)
    left, right = shift(here, "x", N_X, 1), shift(here, "x", N_X, -1)
    far_low, far_high = shift(left[0], "x", N_X, 1), shift(right[1], "x", N_X, -1)
    head_away = (here, left, right, far_low, far_high)

    term = input_term(order, head_own, saved, w_gate.T, w_up.T)
    input_grad = sum_over(term, row_axes, n_row)

    scale = 1.0 / math.sqrt(n_dp * tok)
    gate_grad, up_grad, down_grad = weight_grads(
        scale, scalars, head_own, head_away, saved, cot_own, rest
    )
    return input_grad, gate_grad.T, up_grad.T, down_grad


def solution(mesh):
    fine = Mesh(
        mesh.devices.reshape(2, N_Y, N_CORE, N_X, N_Z), ("dp", "y", "core", "x", "z")
    )
    row, col = ("y", "core"), ("x", "z")

    return jax.shard_map(
        on_device,
        mesh=fine,
        in_specs=(
            P(("dp",) + row, col),
            P(("dp",) + row, col),
            P(("dp",) + col, row),
            P(("dp",) + col, row),
            P(col, row),
            P(col, row),
            P(row, col),
            P(),
            P(),
        ),
        out_specs=(
            P(("dp",) + row, col),
            P(col + ("dp",), row),
            P(col + ("dp",), row),
            P(row + ("dp",), col),
        ),
        check_vma=False,
    )
```

time: 243 us -> 251 us (1.033)
  waiting for transfers between devices: 39.6 us -> 76.4 us
  starting transfers between devices: 78.4 us -> 56.4 us
  local copies, waits for them, and re-layouts: 26 us -> 9.86 us
  blocking collectives: 56.1 us -> 64.3 us
  Pallas kernels: 19.9 us -> 25.7 us
  other arithmetic: 6.5 us -> 3.59 us
    ppermute x5, waiting for transfers between devices: 12.8 us -> 29.8 us  [shift(): lax.ppermute(value, axis, [(i, (i + step) % size) for i in range(size)])]
    all_to_all x2, waiting for transfers between devices: 8.27 us -> 19.6 us  [sum_over(): lax.all_to_all(blocks, axis, split_axis=0, concat_axis=0, tiled=True)]
    all_to_all x2, starting transfers between devices: 21.8 us -> 12.7 us  [sum_over(): lax.all_to_all(blocks, axis, split_axis=0, concat_axis=0, tiled=True)]
    all_to_all x3, waiting for transfers between devices: 18.5 us -> 26.9 us  [spread(): return lax.all_to_all(copies, axis, split_axis=0, concat_axis=0, tiled=True)]
    all_to_all x3, starting transfers between devices: 34.1 us -> 26 us  [spread(): return lax.all_to_all(copies, axis, split_axis=0, concat_axis=0, tiled=True)]
    all_gather x1, blocking collectives: 31.8 us -> 37.5 us  [on_device(): head = lax.all_gather(head, ('dp', 'z'), axis=0, tiled=True)]
    pallas_call x0 -> x1, Pallas kernels: none -> 5.45 us  [head_term(): pl.pallas_call(head_kernel, grid_spec=pltpu.PrefetchScalarGridSpec(num_sc...]
    ppermute x5, starting transfers between devices: 22.4 us -> 17.6 us  [shift(): lax.ppermute(value, axis, [(i, (i + step) % size) for i in range(size)])]
  transfers between devices with their start and end apart: 11 -> 11, of which waited for: 4 -> 6; matrix products, arithmetic and copies ran while one was open for 12% -> 4% of each run, Pallas kernels for 8% -> 10%
where the time goes in v6:
time: 251 us; the launch traced here: 250 us
  waiting for transfers between devices  76.4 us (30%)
  blocking collectives  64.3 us (26%)
  starting transfers between devices  56.4 us (22%)
  Pallas kernels  25.7 us (10%)
  between operations  14.2 us (6%)
  local copies, waits for them, and re-layouts  9.86 us (4%)
  other arithmetic  3.59 us (1%)
    all_gather x1, blocking collectives, on_device(): head = lax.all_gather(head, ('dp', 'z'), axis=0, tiled=True)  37.5 us
    ppermute x5, waiting for transfers between devices, shift(): lax.ppermute(value, axis, [(i, (i + step) % size) for i in range(size)])  29.8 us
    all_to_all x3, waiting for transfers between devices, spread(): return lax.all_to_all(copies, axis, split_axis=0, concat_axis=0, tiled=True)  26.9 us
    all_to_all x1, blocking collectives, sum_over(): lax.all_to_all(blocks, axis, split_axis=0, concat_axis=0, tiled=True)  26.8 us
    all_to_all x3, starting transfers between devices, spread(): return lax.all_to_all(copies, axis, split_axis=0, concat_axis=0, tiled=True)  26 us
    all_to_all x2, waiting for transfers between devices, sum_over(): lax.all_to_all(blocks, axis, split_axis=0, concat_axis=0, tiled=True)  19.6 us
    ppermute x5, starting transfers between devices, shift(): lax.ppermute(value, axis, [(i, (i + step) % size) for i in range(size)])  17.6 us
    pallas_call x1, Pallas kernels, weight_grads(): pl.pallas_call(functools.partial(weight_kernel, scale), grid_spec=pltpu.P...  13.1 us
  transfers between devices with their start and end apart: 11, of which 6 were waited for; matrix products, arithmetic and copies ran while one was open for 4% of the time, Pallas kernels for 10%

profile of v6, /device:TPU:1, one launch (start us, length us, event | category | flops | bytes accessed | tf_op | source)
XLA Modules:
  0.0 250.3 jit_solution(15963387449965097925)
XLA Ops:
  7.2 1.5 pad_maximum_fusion.2
  8.7 2.0 broadcast_in_dim.10
  10.8 10.3 %all-to-all-start = ((bf16[8,128,512]{2,1,0:T(8,128)(2,1)}), bf16[8,128,512]{2,1,0:T(8,128)(2,1)S(1)}, u32[]{:S(2)}, u32[]{:S(2)}) async-start(bf16[8,128,512]{2,1,0:T(8,128)(2,1)} %broadcast_in_dim.10), calls=%async_computation | async-start | bytes 2097152 | tf_op jit(solution)/shard_map/all_to_all | solution.py:19
  21.7 14.3 %all-to-all-done = bf16[8,128,512]{2,1,0:T(8,128)(2,1)S(1)} async-done(((bf16[8,128,512]{2,1,0:T(8,128)(2,1)}), bf16[8,128,512]{2,1,0:T(8,128)(2,1)S(1)}, u32[]{:S(2)}, u32[]{:S(2)}) %all-to-all-start) | async-done | bytes 1048608 | tf_op jit(solution)/shard_map/all_to_all | solution.py:19
  37.0 5.5 %head_term.1 = bf16[4,256,896]{2,1,0:T(8,128)(2,1)} custom-call(s32[6]{0:T(128)} %stack.36.order_ref, s32[4]{0:T(128)} %assignment_ref.3, s32[8]{0:T(128)} %lengths_ref.3, bf16[1024,512]{1,0:T(8,128)(2,1)} %bitcast.31, bf16[832,512]{1,0:T(8,128)(2,1)} %w_ref.1), custom_call_target="tpu_custom_call" | custom-call | flops 872415232 | bytes 3735552 | tf_op jit(solution)/shard_map/head_term/pallas_call | solution.py:53
  42.5 26.8 %all_to_all.30 = bf16[4,256,896]{2,1,0:T(8,128)(2,1)S(1)} all-to-all(bf16[4,256,896]{2,1,0:T(8,128)(2,1)} %head_term.1), channel_id=1, replica_groups=mesh['dp'=2,'y'=4,'core'=2,'x'=4,'z'=8] {'x'}, dimensions={0} | all-to-all | bytes 3670016 | tf_op jit(solution)/shard_map/all_to_all | solution.py:24
  70.4 8.2 %all-to-all-start.2 = ((bf16[8,32,896]{2,1,0:T(8,128)(2,1)}), bf16[8,32,896]{2,1,0:T(8,128)(2,1)S(1)}, u32[]{:S(2)}, u32[]{:S(2)}) async-start(bf16[8,32,896]{2,1,0:T(8,128)(2,1)} %bitcast.7), calls=%async_computation.2 | async-start | bytes 917504 | tf_op jit(solution)/shard_map/all_to_all | solution.py:24
  78.7 19.6 %all-to-all-done.2 = bf16[8,32,896]{2,1,0:T(8,128)(2,1)S(1)} async-done(((bf16[8,32,896]{2,1,0:T(8,128)(2,1)}), bf16[8,32,896]{2,1,0:T(8,128)(2,1)S(1)}, u32[]{:S(2)}, u32[]{:S(2)}) %all-to-all-start.2) | async-done | bytes 458784 | tf_op jit(solution)/shard_map/all_to_all | solution.py:24
  98.4 37.5 %all_gather.6 = bf16[512,896]{1,0:T(8,128)(2,1)S(1)} all-gather(bf16[32,896]{1,0:T(8,128)(2,1)S(1)} %reduce_sum.37), channel_id=1, replica_groups=mesh['dp'=2,'y'=4,'core'=2,'x'=4,'z'=8] {'dp','z'}, dimensions={0}, use_global_device_ids=true | all-gather | bytes 974848 | tf_op jit(solution)/shard_map/all_gather | solution.py:255
  138.2 3.8 %all-to-all-start.3 = ((bf16[4,256,896]{2,1,0:T(8,128)(2,1)}), bf16[4,256,896]{2,1,0:T(8,128)(2,1)S(1)}, u32[]{:S(2)}, u32[]{:S(2)}) async-start(bf16[4,256,896]{2,1,0:T(8,128)(2,1)} %broadcast_in_dim.12), calls=%async_computation.3 | async-start | bytes 3670016 | tf_op jit(solution)/shard_map/all_to_all | solution.py:19
  142.1 4.6 %collective-permute-start.4 = (bf16[128,768]{1,0:T(8,128)(2,1)S(1)}, bf16[128,768]{1,0:T(8,128)(2,1)S(1)}, u32[]{:S(2)}, u32[]{:S(2)}) collective-permute-start(bf16[128,768]{1,0:T(8,128)(2,1)S(1)} %pad_maximum_fusion.1), channel_id=1, source_target_pairs={{0,256},{256,0},{1,257},{257,1},{2,258},{258,2},{3,259},{259,3},{4... | collective-permute-start | bytes 589832 | tf_op jit(solution)/shard_map/ppermute | solution.py:14
  146.7 24.1 %collective-permute-done.4 = bf16[128,768]{1,0:T(8,128)(2,1)S(1)} collective-permute-done((bf16[128,768]{1,0:T(8,128)(2,1)S(1)}, bf16[128,768]{1,0:T(8,128)(2,1)S(1)}, u32[]{:S(2)}, u32[]{:S(2)}) %collective-permute-start.4) | collective-permute-done | bytes 196640 | tf_op jit(solution)/shard_map/ppermute | solution.py:14
  170.8 1.8 broadcast_in_dim.27
  172.8 11.9 %all-to-all-start.5 = ((bf16[8,128,1024]{2,1,0:T(8,128)(2,1)}), bf16[8,128,1024]{2,1,0:T(8,128)(2,1)S(1)}, u32[]{:S(2)}, u32[]{:S(2)}) async-start(bf16[8,128,1024]{2,1,0:T(8,128)(2,1)} %broadcast_in_dim.27), calls=%async_computation.5 | async-start | bytes 4194304 | tf_op jit(solution)/shard_map/all_to_all | solution.py:19
  184.7 3.4 %collective-permute-start = (bf16[2,128,896]{2,1,0:T(8,128)(2,1)}, bf16[2,128,896]{2,1,0:T(8,128)(2,1)}, u32[]{:S(2)}, u32[]{:S(2)}) collective-permute-start(bf16[2,128,896]{2,1,0:T(8,128)(2,1)} %bitcast.16.here), channel_id=1, source_target_pairs={{0,8},{8,16},{16,24},{24,0},{1,9},{9,17},{17,25},{25,1},{2,10},{10... | collective-permute-start | bytes 1376264 | tf_op jit(solution)/shard_map/ppermute | solution.py:14
  188.1 3.0 %collective-permute-start.1 = (bf16[2,128,896]{2,1,0:T(8,128)(2,1)}, bf16[2,128,896]{2,1,0:T(8,128)(2,1)}, u32[]{:S(2)}, u32[]{:S(2)}) collective-permute-start(bf16[2,128,896]{2,1,0:T(8,128)(2,1)} %bitcast.16.here), channel_id=1, source_target_pairs={{0,24},{8,0},{16,8},{24,16},{1,25},{9,1},{17,9},{25,17},{2,26},{10... | collective-permute-start | bytes 1376264 | tf_op jit(solution)/shard_map/ppermute | solution.py:14
  191.2 7.1 %input_term.1 = bf16[1024,512]{1,0:T(8,128)(2,1)} custom-call(s32[6]{0:T(128)} %stack.36.order_ref, bf16[4,256,896]{2,1,0:T(8,128)(2,1)} %copy-done.1, bf16[4,2,8,2,32,832]{5,4,3,2,1,0:T(8,128)(2,1)} %bitcast.25, bf16[832,512]{1,0:T(8,128)(2,1)} %bitcast.35, bf16[832,512]{1,0:T(8,128)(2,1)} %bitcast.36), custom_call_target="tpu_custom_call" | custom-call | flops 1744830464 | bytes 8257536 | tf_op jit(solution)/shard_map/input_term/pallas_call | solution.py:97
  198.3 12.6 %all-to-all-done.5 = bf16[8,128,1024]{2,1,0:T(8,128)(2,1)S(1)} async-done(((bf16[8,128,1024]{2,1,0:T(8,128)(2,1)}), bf16[8,128,1024]{2,1,0:T(8,128)(2,1)S(1)}, u32[]{:S(2)}, u32[]{:S(2)}) %all-to-all-start.5) | async-done | bytes 2097184 | tf_op jit(solution)/shard_map/all_to_all | solution.py:19
  210.9 4.4 %all-to-all-start.4 = ((bf16[8,128,512]{2,1,0:T(8,128)(2,1)}), bf16[8,128,512]{2,1,0:T(8,128)(2,1)S(1)}, u32[]{:S(2)}, u32[]{:S(2)}) async-start(bf16[8,128,512]{2,1,0:T(8,128)(2,1)} %bitcast.33), calls=%async_computation.4 | async-start | bytes 2097152 | tf_op jit(solution)/shard_map/all_to_all | solution.py:24
  216.3 3.5 %collective-permute-start.2 = (bf16[128,896]{1,0:T(8,128)(2,1)S(1)}, bf16[128,896]{1,0:T(8,128)(2,1)S(1)}, u32[]{:S(2)}, u32[]{:S(2)}) collective-permute-start(bf16[128,896]{1,0:T(8,128)(2,1)S(1)} %slice_bitcast_fusion.1), channel_id=1, source_target_pairs={{0,8},{8,16},{16,24},{24,0},{1,9},{9,17},{17,25},{25,1},{2,10},{10... | collective-permute-start | bytes 688136 | tf_op jit(solution)/shard_map/ppermute | solution.py:14
  220.7 3.0 %collective-permute-start.3 = (bf16[128,896]{1,0:T(8,128)(2,1)S(1)}, bf16[128,896]{1,0:T(8,128)(2,1)}, u32[]{:S(2)}, u32[]{:S(2)}) collective-permute-start(bf16[128,896]{1,0:T(8,128)(2,1)S(1)} %slice_bitcast_fusion), channel_id=1, source_target_pairs={{0,24},{8,0},{16,8},{24,16},{1,25},{9,1},{17,9},{25,17},{2,26},{10... | collective-permute-start | bytes 688136 | tf_op jit(solution)/shard_map/ppermute | solution.py:14
  223.8 2.7 %collective-permute-done.2.far_low = bf16[128,896]{1,0:T(8,128)(2,1)S(1)} collective-permute-done((bf16[128,896]{1,0:T(8,128)(2,1)S(1)}, bf16[128,896]{1,0:T(8,128)(2,1)S(1)}, u32[]{:S(2)}, u32[]{:S(2)}) %collective-permute-start.2) | collective-permute-done | bytes 229408 | tf_op jit(solution)/shard_map/ppermute | solution.py:14
  226.5 3.0 %collective-permute-done.3.far_high = bf16[128,896]{1,0:T(8,128)(2,1)} collective-permute-done((bf16[128,896]{1,0:T(8,128)(2,1)S(1)}, bf16[128,896]{1,0:T(8,128)(2,1)}, u32[]{:S(2)}, u32[]{:S(2)}) %collective-permute-start.3) | collective-permute-done | bytes 229408 | tf_op jit(solution)/shard_map/ppermute | solution.py:14
  229.5 13.1 %weight_grads.1 = (bf16[832,256]{1,0:T(8,128)(2,1)}, bf16[832,256]{1,0:T(8,128)(2,1)}, bf16[416,512]{1,0:T(8,128)(2,1)}) custom-call(s32[6]{0:T(128)} %stack.36.order_ref, s32[4]{0:T(128)} %assignment_ref.3, s32[8]{0:T(128)} %lengths_ref.3, bf16[4,256,896]{2,1,0:T(8,128)(2,1)} %copy-done.1, bf16[2,128,896]{2,1,0:T(8,128)(2,1)} %bitcast.16.here, ...), custom_call_target="tpu_custom_call" | custom-call | flops 3489660928 | bytes 14155776 | tf_op jit(solution)/shard_map/weight_grads/pallas_call | solution.py:192
  (30 shorter events, 8.2 us)
Async XLA Ops:
  7.2 184.0 %all-gather.3.cloned.1.call-start = ((), (), s32[]{:S(2)}) async-start(), calls=%async_computation.6 | async-start | bytes 7454720 | tf_op jit(solution)/shard_map/all_gather | solution.py:244
  10.8 25.3 %all-to-all-start = ((bf16[8,128,512]{2,1,0:T(8,128)(2,1)}), bf16[8,128,512]{2,1,0:T(8,128)(2,1)S(1)}, u32[]{:S(2)}, u32[]{:S(2)}) async-start(bf16[8,128,512]{2,1,0:T(8,128)(2,1)} %broadcast_in_dim.10), calls=%async_computation | async-start | bytes 2097152 | tf_op jit(solution)/shard_map/all_to_all | solution.py:19
  36.1 1.0 copy-start.2
  70.4 27.9 %all-to-all-start.2 = ((bf16[8,32,896]{2,1,0:T(8,128)(2,1)}), bf16[8,32,896]{2,1,0:T(8,128)(2,1)S(1)}, u32[]{:S(2)}, u32[]{:S(2)}) async-start(bf16[8,32,896]{2,1,0:T(8,128)(2,1)} %bitcast.7), calls=%async_computation.2 | async-start | bytes 917504 | tf_op jit(solution)/shard_map/all_to_all | solution.py:24
  138.2 3.8 %copy-start.5 = (bf16[128,512]{1,0:T(8,128)(2,1)S(1)}, bf16[128,512]{1,0:T(8,128)(2,1)}, u32[]{:S(2)}) copy-start(bf16[128,512]{1,0:T(8,128)(2,1)} %param.9) | copy-start | bytes 393220
  138.2 3.8 %copy-start.3 = (bf16[128,512]{1,0:T(8,128)(2,1)S(1)}, bf16[128,512]{1,0:T(8,128)(2,1)}, u32[]{:S(2)}) copy-start(bf16[128,512]{1,0:T(8,128)(2,1)} %param.10) | copy-start | bytes 393220
  138.2 32.6 %all-to-all-start.3 = ((bf16[4,256,896]{2,1,0:T(8,128)(2,1)}), bf16[4,256,896]{2,1,0:T(8,128)(2,1)S(1)}, u32[]{:S(2)}, u32[]{:S(2)}) async-start(bf16[4,256,896]{2,1,0:T(8,128)(2,1)} %broadcast_in_dim.12), calls=%async_computation.3 | async-start | bytes 3670016 | tf_op jit(solution)/shard_map/all_to_all | solution.py:19
  142.1 28.7 %collective-permute-start.4 = (bf16[128,768]{1,0:T(8,128)(2,1)S(1)}, bf16[128,768]{1,0:T(8,128)(2,1)S(1)}, u32[]{:S(2)}, u32[]{:S(2)}) collective-permute-start(bf16[128,768]{1,0:T(8,128)(2,1)S(1)} %pad_maximum_fusion.1), channel_id=1, source_target_pairs={{0,256},{256,0},{1,257},{257,1},{2,258},{258,2},{3,259},{259,3},{4... | collective-permute-start | bytes 589832 | tf_op jit(solution)/shard_map/ppermute | solution.py:14
  170.8 2.0 copy-start.1
  172.8 38.1 %all-to-all-start.5 = ((bf16[8,128,1024]{2,1,0:T(8,128)(2,1)}), bf16[8,128,1024]{2,1,0:T(8,128)(2,1)S(1)}, u32[]{:S(2)}, u32[]{:S(2)}) async-start(bf16[8,128,1024]{2,1,0:T(8,128)(2,1)} %broadcast_in_dim.27), calls=%async_computation.5 | async-start | bytes 4194304 | tf_op jit(solution)/shard_map/all_to_all | solution.py:19
  184.7 30.7 %collective-permute-start = (bf16[2,128,896]{2,1,0:T(8,128)(2,1)}, bf16[2,128,896]{2,1,0:T(8,128)(2,1)}, u32[]{:S(2)}, u32[]{:S(2)}) collective-permute-start(bf16[2,128,896]{2,1,0:T(8,128)(2,1)} %bitcast.16.here), channel_id=1, source_target_pairs={{0,8},{8,16},{16,24},{24,0},{1,9},{9,17},{17,25},{25,1},{2,10},{10... | collective-permute-start | bytes 1376264 | tf_op jit(solution)/shard_map/ppermute | solution.py:14
  188.1 31.6 %collective-permute-start.1 = (bf16[2,128,896]{2,1,0:T(8,128)(2,1)}, bf16[2,128,896]{2,1,0:T(8,128)(2,1)}, u32[]{:S(2)}, u32[]{:S(2)}) collective-permute-start(bf16[2,128,896]{2,1,0:T(8,128)(2,1)} %bitcast.16.here), channel_id=1, source_target_pairs={{0,24},{8,0},{16,8},{24,16},{1,25},{9,1},{17,9},{25,17},{2,26},{10... | collective-permute-start | bytes 1376264 | tf_op jit(solution)/shard_map/ppermute | solution.py:14
  210.9 18.6 %copy-start = (bf16[8,128,1024]{2,1,0:T(8,128)(2,1)}, bf16[8,128,1024]{2,1,0:T(8,128)(2,1)S(1)}, u32[]{:S(2)}) copy-start(bf16[8,128,1024]{2,1,0:T(8,128)(2,1)S(1)} %all-to-all-done.5) | copy-start | bytes 6291460
  210.9 31.7 %all-to-all-start.4 = ((bf16[8,128,512]{2,1,0:T(8,128)(2,1)}), bf16[8,128,512]{2,1,0:T(8,128)(2,1)S(1)}, u32[]{:S(2)}, u32[]{:S(2)}) async-start(bf16[8,128,512]{2,1,0:T(8,128)(2,1)} %bitcast.33), calls=%async_computation.4 | async-start | bytes 2097152 | tf_op jit(solution)/shard_map/all_to_all | solution.py:24
  216.3 10.2 %collective-permute-start.2 = (bf16[128,896]{1,0:T(8,128)(2,1)S(1)}, bf16[128,896]{1,0:T(8,128)(2,1)S(1)}, u32[]{:S(2)}, u32[]{:S(2)}) collective-permute-start(bf16[128,896]{1,0:T(8,128)(2,1)S(1)} %slice_bitcast_fusion.1), channel_id=1, source_target_pairs={{0,8},{8,16},{16,24},{24,0},{1,9},{9,17},{17,25},{25,1},{2,10},{10... | collective-permute-start | bytes 688136 | tf_op jit(solution)/shard_map/ppermute | solution.py:14
  220.7 8.8 %collective-permute-start.3 = (bf16[128,896]{1,0:T(8,128)(2,1)S(1)}, bf16[128,896]{1,0:T(8,128)(2,1)}, u32[]{:S(2)}, u32[]{:S(2)}) collective-permute-start(bf16[128,896]{1,0:T(8,128)(2,1)S(1)} %slice_bitcast_fusion), channel_id=1, source_target_pairs={{0,24},{8,0},{16,8},{24,16},{1,25},{9,1},{17,9},{25,17},{2,26},{10... | collective-permute-start | bytes 688136 | tf_op jit(solution)/shard_map/ppermute | solution.py:14
  226.5 3.0 %copy-start.4 = (bf16[128,896]{1,0:T(8,128)(2,1)}, bf16[128,896]{1,0:T(8,128)(2,1)S(1)}, u32[]{:S(2)}) copy-start(bf16[128,896]{1,0:T(8,128)(2,1)S(1)} %collective-permute-done.2.far_low) | copy-start | bytes 688132
Sparse Core Ops, SparseCore 0:
  11.5 171.8 all-gather.2

commit v7 on v6

v7 whole, which is shorter than its diff:
```python
import functools
import math
import jax
import jax.numpy as jnp
from jax import lax
from jax.experimental import pallas as pl
from jax.experimental.pallas import tpu as pltpu
from jax.sharding import Mesh, PartitionSpec as P

N_Y, N_CORE, N_X, N_Z = 4, 2, 4, 8


def shift(value, axis, size, step):
    return lax.ppermute(value, axis, [(i, (i + step) % size) for i in range(size)])


def spread(value, axis, size):
    copies = jnp.broadcast_to(value[None], (size,) + value.shape)
    return lax.all_to_all(copies, axis, split_axis=0, concat_axis=0, tiled=True)


def sum_over(value, axis, size):
    blocks = value.reshape(size, value.shape[0] // size, value.shape[1])
    received = lax.all_to_all(blocks, axis, split_axis=0, concat_axis=0, tiled=True)
    return jnp.sum(received, axis=0, dtype=jnp.float32).astype(jnp.bfloat16)


def live_length(order_ref, assignment_ref, lengths_ref, which, chunk):
    slot = 2 * order_ref[which] + lax.div(chunk, 2)
    return lengths_ref[2 * assignment_ref[slot] + lax.rem(chunk, 2)]


def rows_below(shape, count):
    return lax.broadcasted_iota(jnp.int32, shape, 0) < count


def head_kernel(order_ref, assignment_ref, lengths_ref, cot_ref, w_ref, out_ref):
    ffw = w_ref.shape[0]
    chunks, rows, lanes = out_ref.shape
    w_turned = w_ref[...].T
    for chunk in range(chunks):
        live = live_length(order_ref, assignment_ref, lengths_ref, 0, jnp.int32(chunk))
        cot = cot_ref[chunk * rows : (chunk + 1) * rows, :]
        masked = jnp.where(rows_below(cot.shape, live), cot, jnp.zeros_like(cot))
        term = jnp.dot(masked, w_turned, preferred_element_type=jnp.float32)
        out_ref[chunk, :, :ffw] = term.astype(jnp.bfloat16)
        out_ref[chunk, :, ffw:] = jnp.zeros((rows, lanes - ffw), jnp.bfloat16)


def head_term(scalars, cot, w_down, lanes):
    tok, width = cot.shape
    ffw = w_down.shape[0]
    return pl.pallas_call(
        head_kernel,
        in_specs=[pl.BlockSpec(memory_space=pltpu.SMEM)] * 3
        + [pl.BlockSpec(memory_space=pltpu.VMEM)] * 2,
        out_specs=pl.BlockSpec(memory_space=pltpu.VMEM),
        out_shape=jax.ShapeDtypeStruct((N_X, tok // N_X, lanes), jnp.bfloat16),
        name="head_term",
        cost_estimate=pl.CostEstimate(
            flops=2 * tok * width * ffw,
            bytes_accessed=2 * (cot.size + w_down.size + tok * lanes),
            transcendentals=0,
        ),
    )(*scalars, cot, w_down)


def take_part(step, parts, head_ref):
    here, left, right, far_low, far_high = parts
    mid = far_low.shape[0]
    for index, part in enumerate((here, left, right)):
        @pl.when(step == index)
        def _(part=part):
            head_ref[:mid, :] = part[0]
            head_ref[mid:, :] = part[1]

    @pl.when(step == 3)
    def _():
        head_ref[:mid, :] = far_low[...]
        head_ref[mid:, :] = far_high[...]


def whole(value):
    return pl.BlockSpec(value.shape, lambda i, *_: (0,) * value.ndim)


def saved_block(saved, which):
    return pl.BlockSpec(
        (1, 1) + saved.shape[2:], lambda i, order, *_: (order[2 + i], order[which], 0, 0, 0, 0)
    )


def swiglu_terms(saved_ref):
    pair = saved_ref[0, 0].astype(jnp.float32)
    rows, ffw = pair.shape[0] * pair.shape[2], pair.shape[3]
    gate, up = pair[:, 0].reshape(rows, ffw), pair[:, 1].reshape(rows, ffw)
    sig = jax.nn.sigmoid(gate)
    silu = gate * sig
    return up, silu, up * sig * (1.0 + gate * (1.0 - sig))


def gradients(head_ref, saved_ref):
    up, silu, slope = swiglu_terms(saved_ref)
    head = head_ref[:, : up.shape[1]].astype(jnp.float32)
    return (
        (head * slope).astype(jnp.bfloat16),
        (head * silu).astype(jnp.bfloat16),
        (silu * up).astype(jnp.bfloat16),
    )


def input_kernel(
    order_ref, here, left, right, far_low, far_high, saved_ref, w_gate_ref, w_up_ref,
    out_ref, gate_ref, up_ref, hidden_ref, head_ref,
):
    take_part(pl.program_id(0), (here, left, right, far_low, far_high), head_ref)
    grad_gate, grad_up, hidden = gradients(head_ref, saved_ref)
    term = jnp.dot(grad_gate, w_gate_ref[...], preferred_element_type=jnp.float32)
    term += jnp.dot(grad_up, w_up_ref[...], preferred_element_type=jnp.float32)
    out_ref[...] = term.astype(jnp.bfloat16)
    gate_ref[...] = grad_gate
    up_ref[...] = grad_up
    hidden_ref[...] = hidden


def input_term(order, head, saved, w_gate, w_up):
    rows, lanes = 2 * head[0].shape[1], head[0].shape[2]
    ffw, width = w_gate.shape
    tok = N_X * rows
    kept = pl.BlockSpec((rows, ffw), lambda i, order: (i, 0))
    return pl.pallas_call(
        input_kernel,
        grid_spec=pltpu.PrefetchScalarGridSpec(
            num_scalar_prefetch=1,
            grid=(N_X,),
            in_specs=[whole(part) for part in head]
            + [saved_block(saved, 0), whole(w_gate), whole(w_up)],
            out_specs=[
                pl.BlockSpec((rows, width), lambda i, order: (order[2 + i], 0)), kept, kept, kept
            ],
            scratch_shapes=[pltpu.VMEM((rows, lanes), jnp.bfloat16)],
        ),
        out_shape=[jax.ShapeDtypeStruct((tok, width), jnp.bfloat16)]
        + [jax.ShapeDtypeStruct((tok, ffw), jnp.bfloat16)] * 3,
        name="input_term",
        cost_estimate=pl.CostEstimate(
            flops=4 * tok * ffw * width,
            bytes_accessed=2 * (6 * tok * ffw + 2 * w_gate.size + tok * width),
            transcendentals=tok * ffw,
        ),
    )(order, *head, saved, w_gate, w_up)


def weight_kernel(
    scale, order_ref, assignment_ref, lengths_ref,
    gate_own, up_own, hidden_own, here, left, right, far_low, far_high, saved_away,
    act_own, act_away, cot_own, cot_away,
    gate_ref, up_ref, down_ref, gate_acc, up_acc, down_acc, head_ref,
):
    step = pl.program_id(0)
    chunk = order_ref[2 + step]

    @pl.when(step == 0)
    def _():
        gate_acc[...] = jnp.zeros_like(gate_acc)
        up_acc[...] = jnp.zeros_like(up_acc)
        down_acc[...] = jnp.zeros_like(down_acc)

    def contract(left_rows, right_rows):
        return lax.dot_general(
            left_rows, right_rows, (((0,), (0,)), ((), ())), preferred_element_type=jnp.float32
        )

    take_part(step, (here, left, right, far_low, far_high), head_ref)
    for which, rows_of, act_ref, cot_ref in (
        (0, lambda: (gate_own[...], up_own[...], hidden_own[...]), act_own, cot_own),
        (1, lambda: gradients(head_ref, saved_away), act_away, cot_away),
    ):
        grad_gate, grad_up, hidden = rows_of()
        live = live_length(order_ref, assignment_ref, lengths_ref, which, chunk)
        cot = cot_ref[...]
        masked = jnp.where(rows_below(cot.shape, live), cot, jnp.zeros_like(cot))
        act = act_ref[...]
        gate_acc[...] += contract(act, grad_gate)
        up_acc[...] += contract(act, grad_up)
        down_acc[...] += contract(hidden, masked)

    @pl.when(step == pl.num_programs(0) - 1)
    def _():
        gate_ref[...] = (gate_acc[...] * scale).T.astype(jnp.bfloat16)
        up_ref[...] = (up_acc[...] * scale).T.astype(jnp.bfloat16)
        f_half = down_ref.shape[0]
        first = pl.multiple_of(order_ref[0] * f_half, f_half)
        down_ref[...] = (down_acc[pl.ds(first, f_half), :] * scale).astype(jnp.bfloat16)


def weight_grads(scale, scalars, own_rows, head_away, saved, cot, rest):
    rows, lanes = 2 * head_away[0].shape[1], head_away[0].shape[2]
    tok, width = cot.shape
    ffw, half = saved.shape[-1], width // 2
    kept = pl.BlockSpec((rows, ffw), lambda i, *_: (i, 0))
    column = lambda cols, index: pl.BlockSpec(
        (rows, cols), lambda i, order, *_: (order[2 + i], index)
    )
    out = lambda *shape: pl.BlockSpec(shape, lambda i, *_: (0, 0))
    shape = lambda *dims: jax.ShapeDtypeStruct(dims, jnp.bfloat16)
    return pl.pallas_call(
        functools.partial(weight_kernel, scale),
        grid_spec=pltpu.PrefetchScalarGridSpec(
            num_scalar_prefetch=3,
            grid=(N_X,),
            in_specs=[kept] * 3
            + [whole(part) for part in head_away]
            + [saved_block(saved, 1)]
            + [column(half, 3), column(half, 2), column(width, 0), column(width, 0)],
            out_specs=[out(ffw, half), out(ffw, half), out(ffw // 2, width)],
            scratch_shapes=[
                pltpu.VMEM((half, ffw), jnp.float32),
                pltpu.VMEM((half, ffw), jnp.float32),
                pltpu.VMEM((ffw, width), jnp.float32),
                pltpu.VMEM((rows, lanes), jnp.bfloat16),
            ],
        ),
        out_shape=[shape(ffw, half), shape(ffw, half), shape(ffw // 2, width)],
        name="weight_grads",
        cost_estimate=pl.CostEstimate(
            flops=8 * tok * ffw * width,
            bytes_accessed=2 * (6 * tok * ffw + cot.size + rest.size),
            transcendentals=tok * ffw,
        ),
    )(*scalars, *own_rows, *head_away, saved, rest, rest, cot, rest)


def gather_x(block):
    left, right = shift(block, "x", N_X, 1), shift(block, "x", N_X, -1)
    far_low, far_high = shift(left[0], "x", N_X, 1), shift(right[1], "x", N_X, -1)
    return block, left, right, far_low, far_high


def on_device(
    activations, cotangent, gate_saved, up_saved, w_gate, w_up, w_down, assignment, pair_lengths
):
    batch, x = lax.axis_index("dp"), lax.axis_index("x")
    away = 1 - batch
    rows, width = cotangent.shape
    half = width // 2
    own, ffw = gate_saved.shape
    lanes = -(-ffw // 128) * 128
    row_axes = ("y", "core")
    n_row = N_Y * N_CORE
    tok = rows * n_row
    n_dp = 2
    order = jnp.stack([batch, away] + [(x + step) % N_X for step in (0, N_X - 1, 1, 2)])
    order = order.astype(jnp.int32)
    scalars = (order, assignment, pair_lengths)

    def pick(value, index):
        return lax.dynamic_index_in_dim(value, index, 0, keepdims=False)

    act_own = lax.dynamic_slice_in_dim(activations, batch * half, half, 1)
    act_other = lax.dynamic_slice_in_dim(activations, away * half, half, 1)
    partner = shift(jnp.concatenate([cotangent, act_other], axis=1), "dp", n_dp, 1)

    saved = jnp.stack([gate_saved, up_saved])[None]
    saved = lax.all_gather(saved, ("x", "dp", "z"), axis=0, tiled=True)
    saved = saved.reshape(N_X, n_dp, N_Z, 2, own, ffw)

    cot_own = spread(cotangent, row_axes, n_row).reshape(tok, width)
    block_term = head_term(scalars, cot_own, w_down, lanes)
    head_x = sum_over(block_term.reshape(tok, lanes), "x", N_X)
    _, partner = lax.optimization_barrier((head_x, partner))
    rest = spread(jnp.concatenate([partner, act_own], axis=1), row_axes, n_row)
    rest = rest.reshape(tok, 2 * width)

    head = sum_over(head_x, "z", N_Z)
    head = lax.all_gather(head, ("dp", "z"), axis=0, tiled=True)
    head = head.reshape(n_dp, N_Z * own, lanes)
    halves = (2, N_Z * own // 2, lanes)
    head_own = gather_x(pick(head, batch).reshape(halves))
    head_away = gather_x(pick(head, away).reshape(halves))

    term, *own_rows = input_term(order, head_own, saved, w_gate.T, w_up.T)
    input_grad = sum_over(term, row_axes, n_row)

    scale = 1.0 / math.sqrt(n_dp * tok)
    gate_grad, up_grad, down_grad = weight_grads(
        scale, scalars, own_rows, head_away, saved, cot_own, rest
    )
    return input_grad, gate_grad.T, up_grad.T, down_grad


def solution(mesh):
    fine = Mesh(
        mesh.devices.reshape(2, N_Y, N_CORE, N_X, N_Z), ("dp", "y", "core", "x", "z")
    )
    row, col = ("y", "core"), ("x", "z")

    return jax.shard_map(
        on_device,
        mesh=fine,
        in_specs=(
            P(("dp",) + row, col),
            P(("dp",) + row, col),
            P(("dp",) + col, row),
            P(("dp",) + col, row),
            P(col, row),
            P(col, row),
            P(row, col),
            P(),
            P(),
        ),
        out_specs=(
            P(("dp",) + row, col),
            P(col + ("dp",), row),
            P(col + ("dp",), row),
            P(row + ("dp",), col),
        ),
        check_vma=False,
    )
```

time: 251 us -> 243 us (0.968)
  the two profiles are of different devices: /device:TPU:1 before, /device:TPU:14 now
where the time goes in v7:
time: 243 us; the launch traced here: 242 us
  blocking collectives  70.2 us (29%)
  waiting for transfers between devices  62.7 us (26%)
  starting transfers between devices  58.3 us (24%)
  Pallas kernels  24.2 us (10%)
  between operations  14.2 us (6%)
  local copies, waits for them, and re-layouts  8.83 us (4%)
  other arithmetic  3.59 us (1%)
    all_gather x1, blocking collectives, on_device(): head = lax.all_gather(head, ('dp', 'z'), axis=0, tiled=True)  39.7 us
    ppermute x9, starting transfers between devices, shift(): lax.ppermute(value, axis, [(i, (i + step) % size) for i in range(size)])  35 us
    all_to_all x1, blocking collectives, sum_over(): lax.all_to_all(blocks, axis, split_axis=0, concat_axis=0, tiled=True)  30.5 us
    ppermute x9, waiting for transfers between devices, shift(): lax.ppermute(value, axis, [(i, (i + step) % size) for i in range(size)])  27.8 us
    all_to_all x2, waiting for transfers between devices, sum_over(): lax.all_to_all(blocks, axis, split_axis=0, concat_axis=0, tiled=True)  21 us
    all_to_all x2, waiting for transfers between devices, spread(): return lax.all_to_all(copies, axis, split_axis=0, concat_axis=0, tiled=True)  13.9 us
    all_to_all x2, starting transfers between devices, sum_over(): lax.all_to_all(blocks, axis, split_axis=0, concat_axis=0, tiled=True)  13.5 us
    pallas_call x1, Pallas kernels, weight_grads(): pl.pallas_call(functools.partial(weight_kernel, scale), grid_spec=pltpu.P...  11.7 us
  transfers between devices with their start and end apart: 14, of which 8 were waited for; matrix products, arithmetic and copies ran while one was open for 3% of the time, Pallas kernels for 10%

profile of v7, /device:TPU:14, one launch (start us, length us, event | category | flops | bytes accessed | tf_op | source)
XLA Modules:
  0.0 242.1 jit_solution(16067572686482461659)
XLA Ops:
  8.7 2.0 broadcast_in_dim.6
  10.8 4.9 %all-to-all-start = ((bf16[8,128,512]{2,1,0:T(8,128)(2,1)}), bf16[8,128,512]{2,1,0:T(8,128)(2,1)S(1)}, u32[]{:S(2)}, u32[]{:S(2)}) async-start(bf16[8,128,512]{2,1,0:T(8,128)(2,1)} %broadcast_in_dim.6), calls=%async_computation | async-start | bytes 2097152 | tf_op jit(solution)/shard_map/all_to_all | solution.py:19
  16.3 13.9 %all-to-all-done = bf16[8,128,512]{2,1,0:T(8,128)(2,1)S(1)} async-done(((bf16[8,128,512]{2,1,0:T(8,128)(2,1)}), bf16[8,128,512]{2,1,0:T(8,128)(2,1)S(1)}, u32[]{:S(2)}, u32[]{:S(2)}) %all-to-all-start) | async-done | bytes 1048608 | tf_op jit(solution)/shard_map/all_to_all | solution.py:19
  31.2 4.1 %head_term.1 = bf16[4,256,896]{2,1,0:T(8,128)(2,1)} custom-call(s32[6]{0:T(128)} %stack.36.order_ref, s32[4]{0:T(128)} %assignment_ref.3, s32[8]{0:T(128)} %lengths_ref.3, bf16[1024,512]{1,0:T(8,128)(2,1)} %bitcast.33, bf16[832,512]{1,0:T(8,128)(2,1)} %w_ref.1), custom_call_target="tpu_custom_call" | custom-call | flops 872415232 | bytes 3735552 | tf_op jit(solution)/shard_map/head_term/pallas_call | solution.py:53
  35.3 30.5 %all_to_all.25 = bf16[4,256,896]{2,1,0:T(8,128)(2,1)S(1)} all-to-all(bf16[4,256,896]{2,1,0:T(8,128)(2,1)} %head_term.1), channel_id=1, replica_groups=mesh['dp'=2,'y'=4,'core'=2,'x'=4,'z'=8] {'x'}, dimensions={0} | all-to-all | bytes 3670016 | tf_op jit(solution)/shard_map/all_to_all | solution.py:24
  66.9 8.6 %all-to-all-start.2 = ((bf16[8,32,896]{2,1,0:T(8,128)(2,1)}), bf16[8,32,896]{2,1,0:T(8,128)(2,1)S(1)}, u32[]{:S(2)}, u32[]{:S(2)}) async-start(bf16[8,32,896]{2,1,0:T(8,128)(2,1)} %bitcast.7), calls=%async_computation.2 | async-start | bytes 917504 | tf_op jit(solution)/shard_map/all_to_all | solution.py:24
  75.6 8.1 %collective-permute-start.8 = (bf16[128,768]{1,0:T(8,128)(2,1)S(1)}, bf16[128,768]{1,0:T(8,128)(2,1)S(1)}, u32[]{:S(2)}, u32[]{:S(2)}) collective-permute-start(bf16[128,768]{1,0:T(8,128)(2,1)S(1)} %pad_maximum_fusion.1), channel_id=1, source_target_pairs={{0,256},{256,0},{1,257},{257,1},{2,258},{258,2},{3,259},{259,3},{4... | collective-permute-start | bytes 589832 | tf_op jit(solution)/shard_map/ppermute | solution.py:14
  83.7 12.9 %collective-permute-done.8 = bf16[128,768]{1,0:T(8,128)(2,1)S(1)} collective-permute-done((bf16[128,768]{1,0:T(8,128)(2,1)S(1)}, bf16[128,768]{1,0:T(8,128)(2,1)S(1)}, u32[]{:S(2)}, u32[]{:S(2)}) %collective-permute-start.8) | collective-permute-done | bytes 196640 | tf_op jit(solution)/shard_map/ppermute | solution.py:14
  96.6 21.0 %all-to-all-done.2 = bf16[8,32,896]{2,1,0:T(8,128)(2,1)S(1)} async-done(((bf16[8,32,896]{2,1,0:T(8,128)(2,1)}), bf16[8,32,896]{2,1,0:T(8,128)(2,1)S(1)}, u32[]{:S(2)}, u32[]{:S(2)}) %all-to-all-start.2) | async-done | bytes 458784 | tf_op jit(solution)/shard_map/all_to_all | solution.py:24
  119.3 4.9 %all-to-all-start.4 = ((bf16[8,128,1024]{2,1,0:T(8,128)(2,1)}), bf16[8,128,1024]{2,1,0:T(8,128)(2,1)S(1)}, u32[]{:S(2)}, u32[]{:S(2)}) async-start(bf16[8,128,1024]{2,1,0:T(8,128)(2,1)} %broadcast_in_dim.8), calls=%async_computation.4 | async-start | bytes 4194304 | tf_op jit(solution)/shard_map/all_to_all | solution.py:19
  124.2 39.7 %all_gather.6 = bf16[512,896]{1,0:T(8,128)(2,1)S(1)} all-gather(bf16[32,896]{1,0:T(8,128)(2,1)S(1)} %reduce_sum.37), channel_id=1, replica_groups=mesh['dp'=2,'y'=4,'core'=2,'x'=4,'z'=8] {'dp','z'}, dimensions={0}, use_global_device_ids=true | all-gather | bytes 974848 | tf_op jit(solution)/shard_map/all_gather | solution.py:276
  164.8 4.5 %collective-permute-start = (bf16[2,128,896]{2,1,0:T(8,128)(2,1)S(1)}, bf16[2,128,896]{2,1,0:T(8,128)(2,1)S(1)}, u32[]{:S(2)}, u32[]{:S(2)}) collective-permute-start(bf16[2,128,896]{2,1,0:T(8,128)(2,1)S(1)} %bitcast.36), channel_id=1, source_target_pairs={{0,8},{8,16},{16,24},{24,0},{1,9},{9,17},{17,25},{25,1},{2,10},{10... | collective-permute-start | bytes 1376264 | tf_op jit(solution)/shard_map/ppermute | solution.py:14
  171.2 5.1 %collective-permute-start.4 = (bf16[2,128,896]{2,1,0:T(8,128)(2,1)}, bf16[2,128,896]{2,1,0:T(8,128)(2,1)}, u32[]{:S(2)}, u32[]{:S(2)}) collective-permute-start(bf16[2,128,896]{2,1,0:T(8,128)(2,1)} %bitcast.18.here), channel_id=1, source_target_pairs={{0,8},{8,16},{16,24},{24,0},{1,9},{9,17},{17,25},{25,1},{2,10},{10... | collective-permute-start | bytes 1376264 | tf_op jit(solution)/shard_map/ppermute | solution.py:14
  176.4 2.5 %collective-permute-done.left = bf16[2,128,896]{2,1,0:T(8,128)(2,1)S(1)} collective-permute-done((bf16[2,128,896]{2,1,0:T(8,128)(2,1)S(1)}, bf16[2,128,896]{2,1,0:T(8,128)(2,1)S(1)}, u32[]{:S(2)}, u32[]{:S(2)}) %collective-permute-start) | collective-permute-done | bytes 458784 | tf_op jit(solution)/shard_map/ppermute | solution.py:14
  178.9 5.6 %collective-permute-start.2 = (bf16[128,896]{1,0:T(8,128)(2,1)S(1)}, bf16[128,896]{1,0:T(8,128)(2,1)S(1)}, u32[]{:S(2)}, u32[]{:S(2)}) collective-permute-start(bf16[128,896]{1,0:T(8,128)(2,1)S(1)} %slice_bitcast_fusion.3), channel_id=1, source_target_pairs={{0,8},{8,16},{16,24},{24,0},{1,9},{9,17},{17,25},{25,1},{2,10},{10... | collective-permute-start | bytes 688136 | tf_op jit(solution)/shard_map/ppermute | solution.py:14
  188.4 2.1 collective-permute-done.2.far_low
  191.2 2.6 %collective-permute-done.3.far_high = bf16[128,896]{1,0:T(8,128)(2,1)} collective-permute-done((bf16[128,896]{1,0:T(8,128)(2,1)S(1)}, bf16[128,896]{1,0:T(8,128)(2,1)}, u32[]{:S(2)}, u32[]{:S(2)}) %collective-permute-start.3) | collective-permute-done | bytes 229408 | tf_op jit(solution)/shard_map/ppermute | solution.py:14
  193.8 8.5 %input_term.1 = (bf16[1024,512]{1,0:T(8,128)(2,1)}, bf16[1024,832]{1,0:T(8,128)(2,1)}, bf16[1024,832]{1,0:T(8,128)(2,1)}, bf16[1024,832]{1,0:T(8,128)(2,1)}) custom-call(s32[6]{0:T(128)} %stack.36.order_ref, bf16[2,128,896]{2,1,0:T(8,128)(2,1)} %bitcast.38, bf16[2,128,896]{2,1,0:T(8,128)(2,1)} %copy-done.3, bf16[2,128,896]{2,1,0:T(8,128)(2,1)} %copy-done.4, ...), custom_call_target="tpu_custom_call" | custom-call | flops 1744830464 | bytes 12976128 | tf_op jit(solution)/shard_map/input_term/pallas_call | solution.py:131
  202.3 4.9 %all-to-all-start.3 = ((bf16[8,128,512]{2,1,0:T(8,128)(2,1)}), bf16[8,128,512]{2,1,0:T(8,128)(2,1)S(1)}, u32[]{:S(2)}, u32[]{:S(2)}) async-start(bf16[8,128,512]{2,1,0:T(8,128)(2,1)} %bitcast.39), calls=%async_computation.3 | async-start | bytes 2097152 | tf_op jit(solution)/shard_map/all_to_all | solution.py:24
  208.2 3.0 %collective-permute-start.6 = (bf16[128,896]{1,0:T(8,128)(2,1)S(1)}, bf16[128,896]{1,0:T(8,128)(2,1)S(1)}, u32[]{:S(2)}, u32[]{:S(2)}) collective-permute-start(bf16[128,896]{1,0:T(8,128)(2,1)S(1)} %slice_bitcast_fusion.1), channel_id=1, source_target_pairs={{0,8},{8,16},{16,24},{24,0},{1,9},{9,17},{17,25},{25,1},{2,10},{10... | collective-permute-start | bytes 688136 | tf_op jit(solution)/shard_map/ppermute | solution.py:14
  212.2 2.8 %collective-permute-start.7 = (bf16[128,896]{1,0:T(8,128)(2,1)S(1)}, bf16[128,896]{1,0:T(8,128)(2,1)}, u32[]{:S(2)}, u32[]{:S(2)}) collective-permute-start(bf16[128,896]{1,0:T(8,128)(2,1)S(1)} %slice_bitcast_fusion), channel_id=1, source_target_pairs={{0,24},{8,0},{16,8},{24,16},{1,25},{9,1},{17,9},{25,17},{2,26},{10... | collective-permute-start | bytes 688136 | tf_op jit(solution)/shard_map/ppermute | solution.py:14
  215.0 2.7 %collective-permute-done.6.far_low = bf16[128,896]{1,0:T(8,128)(2,1)S(1)} collective-permute-done((bf16[128,896]{1,0:T(8,128)(2,1)S(1)}, bf16[128,896]{1,0:T(8,128)(2,1)S(1)}, u32[]{:S(2)}, u32[]{:S(2)}) %collective-permute-start.6) | collective-permute-done | bytes 229408 | tf_op jit(solution)/shard_map/ppermute | solution.py:14
  217.7 5.0 %collective-permute-done.7.far_high = bf16[128,896]{1,0:T(8,128)(2,1)} collective-permute-done((bf16[128,896]{1,0:T(8,128)(2,1)S(1)}, bf16[128,896]{1,0:T(8,128)(2,1)}, u32[]{:S(2)}, u32[]{:S(2)}) %collective-permute-start.7) | collective-permute-done | bytes 229408 | tf_op jit(solution)/shard_map/ppermute | solution.py:14
  222.7 11.7 %weight_grads.1 = (bf16[832,256]{1,0:T(8,128)(2,1)}, bf16[832,256]{1,0:T(8,128)(2,1)}, bf16[416,512]{1,0:T(8,128)(2,1)}) custom-call(s32[6]{0:T(128)} %stack.36.order_ref, s32[4]{0:T(128)} %assignment_ref.3, s32[8]{0:T(128)} %lengths_ref.3, bf16[1024,832]{1,0:T(8,128)(2,1)} %get-tuple-element.13.gate_own, bf16[1024,832]{1,0:T(8,128)(2,1)} %get-tuple-element.14.up_own, ...), custom_call_target="tpu_custom_call" | custom-call | flops 3489660928 | bytes 13369344 | tf_op jit(solution)/shard_map/weight_grads/pallas_call | solution.py:207
  (43 shorter events, 16.2 us)
Async XLA Ops:
  7.2 186.6 %all-gather.3.cloned.1.call-start = ((), (), s32[]{:S(2)}) async-start(), calls=%async_computation.5 | async-start | bytes 7454720 | tf_op jit(solution)/shard_map/all_gather | solution.py:265
  10.8 19.4 %all-to-all-start = ((bf16[8,128,512]{2,1,0:T(8,128)(2,1)}), bf16[8,128,512]{2,1,0:T(8,128)(2,1)S(1)}, u32[]{:S(2)}, u32[]{:S(2)}) async-start(bf16[8,128,512]{2,1,0:T(8,128)(2,1)} %broadcast_in_dim.6), calls=%async_computation | async-start | bytes 2097152 | tf_op jit(solution)/shard_map/all_to_all | solution.py:19
  30.2 1.0 copy-start.1
  65.7 9.8 %copy-start.8 = (bf16[128,512]{1,0:T(8,128)(2,1)S(1)}, bf16[128,512]{1,0:T(8,128)(2,1)}, u32[]{:S(2)}) copy-start(bf16[128,512]{1,0:T(8,128)(2,1)} %param.9) | copy-start | bytes 393220
  65.7 9.8 %copy-start.5 = (bf16[128,512]{1,0:T(8,128)(2,1)S(1)}, bf16[128,512]{1,0:T(8,128)(2,1)}, u32[]{:S(2)}) copy-start(bf16[128,512]{1,0:T(8,128)(2,1)} %param.10) | copy-start | bytes 393220
  66.9 50.7 %all-to-all-start.2 = ((bf16[8,32,896]{2,1,0:T(8,128)(2,1)}), bf16[8,32,896]{2,1,0:T(8,128)(2,1)S(1)}, u32[]{:S(2)}, u32[]{:S(2)}) async-start(bf16[8,32,896]{2,1,0:T(8,128)(2,1)} %bitcast.7), calls=%async_computation.2 | async-start | bytes 917504 | tf_op jit(solution)/shard_map/all_to_all | solution.py:24
  75.6 21.0 %collective-permute-start.8 = (bf16[128,768]{1,0:T(8,128)(2,1)S(1)}, bf16[128,768]{1,0:T(8,128)(2,1)S(1)}, u32[]{:S(2)}, u32[]{:S(2)}) collective-permute-start(bf16[128,768]{1,0:T(8,128)(2,1)S(1)} %pad_maximum_fusion.1), channel_id=1, source_target_pairs={{0,256},{256,0},{1,257},{257,1},{2,258},{258,2},{3,259},{259,3},{4... | collective-permute-start | bytes 589832 | tf_op jit(solution)/shard_map/ppermute | solution.py:14
  119.3 83.0 %all-to-all-start.4 = ((bf16[8,128,1024]{2,1,0:T(8,128)(2,1)}), bf16[8,128,1024]{2,1,0:T(8,128)(2,1)S(1)}, u32[]{:S(2)}, u32[]{:S(2)}) async-start(bf16[8,128,1024]{2,1,0:T(8,128)(2,1)} %broadcast_in_dim.8), calls=%async_computation.4 | async-start | bytes 4194304 | tf_op jit(solution)/shard_map/all_to_all | solution.py:19
  164.8 29.0 %copy-start.2 = (bf16[1,256,896]{2,1,0:T(8,128)(2,1)}, bf16[1,256,896]{2,1,0:T(8,128)(2,1)S(1)}, u32[]{:S(2)}) copy-start(bf16[1,256,896]{2,1,0:T(8,128)(2,1)S(1)} %get-tuple-element.21) | copy-start | bytes 1376260
  164.8 14.1 %collective-permute-start = (bf16[2,128,896]{2,1,0:T(8,128)(2,1)S(1)}, bf16[2,128,896]{2,1,0:T(8,128)(2,1)S(1)}, u32[]{:S(2)}, u32[]{:S(2)}) collective-permute-start(bf16[2,128,896]{2,1,0:T(8,128)(2,1)S(1)} %bitcast.36), channel_id=1, source_target_pairs={{0,8},{8,16},{16,24},{24,0},{1,9},{9,17},{17,25},{25,1},{2,10},{10... | collective-permute-start | bytes 1376264 | tf_op jit(solution)/shard_map/ppermute | solution.py:14
  169.3 15.2 %collective-permute-start.1 = (bf16[2,128,896]{2,1,0:T(8,128)(2,1)S(1)}, bf16[2,128,896]{2,1,0:T(8,128)(2,1)S(1)}, u32[]{:S(2)}, u32[]{:S(2)}) collective-permute-start(bf16[2,128,896]{2,1,0:T(8,128)(2,1)S(1)} %bitcast.37), channel_id=1, source_target_pairs={{0,24},{8,0},{16,8},{24,16},{1,25},{9,1},{17,9},{25,17},{2,26},{10... | collective-permute-start | bytes 1376264 | tf_op jit(solution)/shard_map/ppermute | solution.py:14
  171.2 36.0 %collective-permute-start.4 = (bf16[2,128,896]{2,1,0:T(8,128)(2,1)}, bf16[2,128,896]{2,1,0:T(8,128)(2,1)}, u32[]{:S(2)}, u32[]{:S(2)}) collective-permute-start(bf16[2,128,896]{2,1,0:T(8,128)(2,1)} %bitcast.18.here), channel_id=1, source_target_pairs={{0,8},{8,16},{16,24},{24,0},{1,9},{9,17},{17,25},{25,1},{2,10},{10... | collective-permute-start | bytes 1376264 | tf_op jit(solution)/shard_map/ppermute | solution.py:14
  178.9 14.9 %copy-start.3 = (bf16[2,128,896]{2,1,0:T(8,128)(2,1)}, bf16[2,128,896]{2,1,0:T(8,128)(2,1)S(1)}, u32[]{:S(2)}) copy-start(bf16[2,128,896]{2,1,0:T(8,128)(2,1)S(1)} %collective-permute-done.left) | copy-start | bytes 1376260
  178.9 11.6 %collective-permute-start.2 = (bf16[128,896]{1,0:T(8,128)(2,1)S(1)}, bf16[128,896]{1,0:T(8,128)(2,1)S(1)}, u32[]{:S(2)}, u32[]{:S(2)}) collective-permute-start(bf16[128,896]{1,0:T(8,128)(2,1)S(1)} %slice_bitcast_fusion.3), channel_id=1, source_target_pairs={{0,8},{8,16},{16,24},{24,0},{1,9},{9,17},{17,25},{25,1},{2,10},{10... | collective-permute-start | bytes 688136 | tf_op jit(solution)/shard_map/ppermute | solution.py:14
  184.5 9.3 %copy-start.4 = (bf16[2,128,896]{2,1,0:T(8,128)(2,1)}, bf16[2,128,896]{2,1,0:T(8,128)(2,1)S(1)}, u32[]{:S(2)}) copy-start(bf16[2,128,896]{2,1,0:T(8,128)(2,1)S(1)} %collective-permute-done.1.right) | copy-start | bytes 1376260
  184.6 9.2 %collective-permute-start.3 = (bf16[128,896]{1,0:T(8,128)(2,1)S(1)}, bf16[128,896]{1,0:T(8,128)(2,1)}, u32[]{:S(2)}, u32[]{:S(2)}) collective-permute-start(bf16[128,896]{1,0:T(8,128)(2,1)S(1)} %slice_bitcast_fusion.2), channel_id=1, source_target_pairs={{0,24},{8,0},{16,8},{24,16},{1,25},{9,1},{17,9},{25,17},{2,26},{10... | collective-permute-start | bytes 688136 | tf_op jit(solution)/shard_map/ppermute | solution.py:14
  186.5 24.7 %collective-permute-start.5 = (bf16[2,128,896]{2,1,0:T(8,128)(2,1)}, bf16[2,128,896]{2,1,0:T(8,128)(2,1)}, u32[]{:S(2)}, u32[]{:S(2)}) collective-permute-start(bf16[2,128,896]{2,1,0:T(8,128)(2,1)} %bitcast.18.here), channel_id=1, source_target_pairs={{0,24},{8,0},{16,8},{24,16},{1,25},{9,1},{17,9},{25,17},{2,26},{10... | collective-permute-start | bytes 1376264 | tf_op jit(solution)/shard_map/ppermute | solution.py:14
  190.5 0.7 copy-start.7
  202.3 20.4 %copy-start = (bf16[8,128,1024]{2,1,0:T(8,128)(2,1)}, bf16[8,128,1024]{2,1,0:T(8,128)(2,1)S(1)}, u32[]{:S(2)}) copy-start(bf16[8,128,1024]{2,1,0:T(8,128)(2,1)S(1)} %all-to-all-done.4) | copy-start | bytes 6291460
  202.3 32.1 %all-to-all-start.3 = ((bf16[8,128,512]{2,1,0:T(8,128)(2,1)}), bf16[8,128,512]{2,1,0:T(8,128)(2,1)S(1)}, u32[]{:S(2)}, u32[]{:S(2)}) async-start(bf16[8,128,512]{2,1,0:T(8,128)(2,1)} %bitcast.39), calls=%async_computation.3 | async-start | bytes 2097152 | tf_op jit(solution)/shard_map/all_to_all | solution.py:24
  208.2 9.5 %collective-permute-start.6 = (bf16[128,896]{1,0:T(8,128)(2,1)S(1)}, bf16[128,896]{1,0:T(8,128)(2,1)S(1)}, u32[]{:S(2)}, u32[]{:S(2)}) collective-permute-start(bf16[128,896]{1,0:T(8,128)(2,1)S(1)} %slice_bitcast_fusion.1), channel_id=1, source_target_pairs={{0,8},{8,16},{16,24},{24,0},{1,9},{9,17},{17,25},{25,1},{2,10},{10... | collective-permute-start | bytes 688136 | tf_op jit(solution)/shard_map/ppermute | solution.py:14
  212.2 10.6 %collective-permute-start.7 = (bf16[128,896]{1,0:T(8,128)(2,1)S(1)}, bf16[128,896]{1,0:T(8,128)(2,1)}, u32[]{:S(2)}, u32[]{:S(2)}) collective-permute-start(bf16[128,896]{1,0:T(8,128)(2,1)S(1)} %slice_bitcast_fusion), channel_id=1, source_target_pairs={{0,24},{8,0},{16,8},{24,16},{1,25},{9,1},{17,9},{25,17},{2,26},{10... | collective-permute-start | bytes 688136 | tf_op jit(solution)/shard_map/ppermute | solution.py:14
  217.7 5.0 %copy-start.6 = (bf16[128,896]{1,0:T(8,128)(2,1)}, bf16[128,896]{1,0:T(8,128)(2,1)S(1)}, u32[]{:S(2)}) copy-start(bf16[128,896]{1,0:T(8,128)(2,1)S(1)} %collective-permute-done.6.far_low) | copy-start | bytes 688132
Sparse Core Ops, SparseCore 0:
  11.5 175.4 all-gather.2

commit v8 on v7

--- a/solution.py
+++ b/solution.py
@@ -86,14 +86,24 @@
 
 def saved_block(saved, which):
     return pl.BlockSpec(
-        (1, 1) + saved.shape[2:], lambda i, order, *_: (order[2 + i], order[which], 0, 0, 0, 0)
-    )
+        (1, 1) + saved.shape[2:], lambda i, order, *_: (order[2 + i], order[which], 0, 0, 0)
+    )
+
+
+def pack_pair(gate, up):
+    body = gate.shape[1] // 128 * 128
+    return jnp.concatenate([gate[:, :body], up[:, :body], gate[:, body:], up[:, body:]], axis=1)
 
 
 def swiglu_terms(saved_ref):
-    pair = saved_ref[0, 0].astype(jnp.float32)
-    rows, ffw = pair.shape[0] * pair.shape[2], pair.shape[3]
-    gate, up = pair[:, 0].reshape(rows, ffw), pair[:, 1].reshape(rows, ffw)
+    pair = saved_ref[0, 0]
+    pair = pair.reshape(pair.shape[0] * pair.shape[1], pair.shape[2]).astype(jnp.float32)
+    ffw = pair.shape[1] // 2
+    body = ffw // 128 * 128
+    tail = pair[:, 2 * body :]
+    turned = pltpu.roll(tail, ffw - body, 1)
+    gate = jnp.concatenate([pair[:, :body], tail[:, : ffw - body]], axis=1)
+    up = jnp.concatenate([pair[:, body : 2 * body], turned[:, : ffw - body]], axis=1)
     sig = jax.nn.sigmoid(gate)
     silu = gate * sig
     return up, silu, up * sig * (1.0 + gate * (1.0 - sig))
@@ -111,23 +121,19 @@
 
 def input_kernel(
     order_ref, here, left, right, far_low, far_high, saved_ref, w_gate_ref, w_up_ref,
-    out_ref, gate_ref, up_ref, hidden_ref, head_ref,
+    out_ref, head_ref,
 ):
     take_part(pl.program_id(0), (here, left, right, far_low, far_high), head_ref)
-    grad_gate, grad_up, hidden = gradients(head_ref, saved_ref)
+    grad_gate, grad_up, _ = gradients(head_ref, saved_ref)
     term = jnp.dot(grad_gate, w_gate_ref[...], preferred_element_type=jnp.float32)
     term += jnp.dot(grad_up, w_up_ref[...], preferred_element_type=jnp.float32)
     out_ref[...] = term.astype(jnp.bfloat16)
-    gate_ref[...] = grad_gate
-    up_ref[...] = grad_up
-    hidden_ref[...] = hidden
 
 
 def input_term(order, head, saved, w_gate, w_up):
     rows, lanes = 2 * head[0].shape[1], head[0].shape[2]
     ffw, width = w_gate.shape
     tok = N_X * rows
-    kept = pl.BlockSpec((rows, ffw), lambda i, order: (i, 0))
     return pl.pallas_call(
         input_kernel,
         grid_spec=pltpu.PrefetchScalarGridSpec(
@@ -135,17 +141,14 @@
             grid=(N_X,),
             in_specs=[whole(part) for part in head]
             + [saved_block(saved, 0), whole(w_gate), whole(w_up)],
-            out_specs=[
-                pl.BlockSpec((rows, width), lambda i, order: (order[2 + i], 0)), kept, kept, kept
-            ],
+            out_specs=pl.BlockSpec((rows, width), lambda i, order: (order[2 + i], 0)),
             scratch_shapes=[pltpu.VMEM((rows, lanes), jnp.bfloat16)],
         ),
-        out_shape=[jax.ShapeDtypeStruct((tok, width), jnp.bfloat16)]
-        + [jax.ShapeDtypeStruct((tok, ffw), jnp.bfloat16)] * 3,
+        out_shape=jax.ShapeDtypeStruct((tok, width), jnp.bfloat16),
         name="input_term",
         cost_estimate=pl.CostEstimate(
             flops=4 * tok * ffw * width,
-            bytes_accessed=2 * (6 * tok * ffw + 2 * w_gate.size + tok * width),
+            bytes_accessed=2 * (3 * tok * ffw + 2 * w_gate.size + tok * width),
             transcendentals=tok * ffw,
         ),
     )(order, *head, saved, w_gate, w_up)
@@ -153,10 +156,11 @@
 
 def weight_kernel(
     scale, order_ref, assignment_ref, lengths_ref,
-    gate_own, up_own, hidden_own, here, left, right, far_low, far_high, saved_away,
-    act_own, act_away, cot_own, cot_away,
-    gate_ref, up_ref, down_ref, gate_acc, up_acc, down_acc, head_ref,
+    *refs,
 ):
+    parts_own, parts_away, refs = refs[:5], refs[5:10], refs[10:]
+    saved_own, saved_away, act_own, act_away, cot_own, cot_away = refs[:6]
+    gate_ref, up_ref, down_ref, gate_acc, up_acc, down_acc, head_own, head_away = refs[6:]
     step = pl.program_id(0)
     chunk = order_ref[2 + step]
 
@@ -171,12 +175,13 @@
             left_rows, right_rows, (((0,), (0,)), ((), ())), preferred_element_type=jnp.float32
         )
 
-    take_part(step, (here, left, right, far_low, far_high), head_ref)
-    for which, rows_of, act_ref, cot_ref in (
-        (0, lambda: (gate_own[...], up_own[...], hidden_own[...]), act_own, cot_own),
-        (1, lambda: gradients(head_ref, saved_away), act_away, cot_away),
+    take_part(step, parts_own, head_own)
+    take_part(step, parts_away, head_away)
+    for which, head_ref, saved_ref, act_ref, cot_ref in (
+        (0, head_own, saved_own, act_own, cot_own),
+        (1, head_away, saved_away, act_away, cot_away),
     ):
-        grad_gate, grad_up, hidden = rows_of()
+        grad_gate, grad_up, hidden = gradients(head_ref, saved_ref)
         live = live_length(order_ref, assignment_ref, lengths_ref, which, chunk)
         cot = cot_ref[...]
         masked = jnp.where(rows_below(cot.shape, live), cot, jnp.zeros_like(cot))
@@ -194,11 +199,10 @@
         down_ref[...] = (down_acc[pl.ds(first, f_half), :] * scale).astype(jnp.bfloat16)
 
 
-def weight_grads(scale, scalars, own_rows, head_away, saved, cot, rest):
+def weight_grads(scale, scalars, head_own, head_away, saved, cot, rest):
     rows, lanes = 2 * head_away[0].shape[1], head_away[0].shape[2]
     tok, width = cot.shape
-    ffw, half = saved.shape[-1], width // 2
-    kept = pl.BlockSpec((rows, ffw), lambda i, *_: (i, 0))
+    ffw, half = saved.shape[-1] // 2, width // 2
     column = lambda cols, index: pl.BlockSpec(
         (rows, cols), lambda i, order, *_: (order[2 + i], index)
     )
@@ -209,9 +213,8 @@
         grid_spec=pltpu.PrefetchScalarGridSpec(
             num_scalar_prefetch=3,
             grid=(N_X,),
-            in_specs=[kept] * 3
-            + [whole(part) for part in head_away]
-            + [saved_block(saved, 1)]
+            in_specs=[whole(part) for part in head_own + head_away]
+            + [saved_block(saved, 0), saved_block(saved, 1)]
             + [column(half, 3), column(half, 2), column(width, 0), column(width, 0)],
             out_specs=[out(ffw, half), out(ffw, half), out(ffw // 2, width)],
             scratch_shapes=[
@@ -219,6 +222,7 @@
                 pltpu.VMEM((half, ffw), jnp.float32),
                 pltpu.VMEM((ffw, width), jnp.float32),
                 pltpu.VMEM((rows, lanes), jnp.bfloat16),
+                pltpu.VMEM((rows, lanes), jnp.bfloat16),
             ],
         ),
         out_shape=[shape(ffw, half), shape(ffw, half), shape(ffw // 2, width)],
@@ -226,9 +230,9 @@
         cost_estimate=pl.CostEstimate(
             flops=8 * tok * ffw * width,
             bytes_accessed=2 * (6 * tok * ffw + cot.size + rest.size),
-            transcendentals=tok * ffw,
-        ),
-    )(*scalars, *own_rows, *head_away, saved, rest, rest, cot, rest)
+            transcendentals=2 * tok * ffw,
+        ),
+    )(*scalars, *head_own, *head_away, saved, saved, rest, rest, cot, rest)
 
 
 def gather_x(block):
@@ -261,9 +265,9 @@
     act_other = lax.dynamic_slice_in_dim(activations, away * half, half, 1)
     partner = shift(jnp.concatenate([cotangent, act_other], axis=1), "dp", n_dp, 1)
 
-    saved = jnp.stack([gate_saved, up_saved])[None]
+    saved = pack_pair(gate_saved, up_saved)[None]
     saved = lax.all_gather(saved, ("x", "dp", "z"), axis=0, tiled=True)
-    saved = saved.reshape(N_X, n_dp, N_Z, 2, own, ffw)
+    saved = saved.reshape(N_X, n_dp, N_Z, own, 2 * ffw)
 
     cot_own = spread(cotangent, row_axes, n_row).reshape(tok, width)
     block_term = head_term(scalars, cot_own, w_down, lanes)
@@ -279,12 +283,12 @@
     head_own = gather_x(pick(head, batch).reshape(halves))
     head_away = gather_x(pick(head, away).reshape(halves))
 
-    term, *own_rows = input_term(order, head_own, saved, w_gate.T, w_up.T)
+    term = input_term(order, head_own, saved, w_gate.T, w_up.T)
     input_grad = sum_over(term, row_axes, n_row)
 
     scale = 1.0 / math.sqrt(n_dp * tok)
     gate_grad, up_grad, down_grad = weight_grads(
-        scale, scalars, own_rows, head_away, saved, cot_own, rest
+        scale, scalars, head_own, head_away, saved, cot_own, rest
     )
     return input_grad, gate_grad.T, up_grad.T, down_grad
 

time: 243 us -> 246 us (1.012)
  local copies, waits for them, and re-layouts: 8.83 us -> 11.8 us
    slice x0 -> x4, local copies, waits for them, and re-layouts: none -> 3.01 us  [the longest x1 0.8 us: pack_pair(): gate[:, :body]]
where the time goes in v8:
time: 246 us; the launch traced here: 245 us
  blocking collectives  70 us (28%)
  waiting for transfers between devices  63.3 us (26%)
  starting transfers between devices  57.8 us (23%)
  Pallas kernels  25.4 us (10%)
  between operations  14.2 us (6%)
  local copies, waits for them, and re-layouts  11.8 us (5%)
    all_gather x1, blocking collectives, on_device(): head = lax.all_gather(head, ('dp', 'z'), axis=0, tiled=True)  39.6 us
    ppermute x9, starting transfers between devices, shift(): lax.ppermute(value, axis, [(i, (i + step) % size) for i in range(size)])  33.8 us
    all_to_all x1, blocking collectives, sum_over(): lax.all_to_all(blocks, axis, split_axis=0, concat_axis=0, tiled=True)  30.4 us
    ppermute x9, waiting for transfers between devices, shift(): lax.ppermute(value, axis, [(i, (i + step) % size) for i in range(size)])  27.9 us
    all_to_all x2, waiting for transfers between devices, sum_over(): lax.all_to_all(blocks, axis, split_axis=0, concat_axis=0, tiled=True)  21.5 us
    all_to_all x2, starting transfers between devices, sum_over(): lax.all_to_all(blocks, axis, split_axis=0, concat_axis=0, tiled=True)  14.1 us
    pallas_call x1, Pallas kernels, weight_grads(): pl.pallas_call(functools.partial(weight_kernel, scale), grid_spec=pltpu.P...  13.9 us
    all_to_all x2, waiting for transfers between devices, spread(): return lax.all_to_all(copies, axis, split_axis=0, concat_axis=0, tiled=True)  13.9 us
  transfers between devices with their start and end apart: 14, of which 8 were waited for; matrix products, arithmetic and copies ran while one was open for 3% of the time, Pallas kernels for 10%

profile of v8, /device:TPU:14, one launch (start us, length us, event | category | flops | bytes accessed | tf_op | source)
XLA Modules:
  0.0 244.5 jit_solution(8081212472892602020)
XLA Ops:
  12.9 4.9 %all-to-all-start = ((bf16[8,128,512]{2,1,0:T(8,128)(2,1)}), bf16[8,128,512]{2,1,0:T(8,128)(2,1)S(1)}, u32[]{:S(2)}, u32[]{:S(2)}) async-start(bf16[8,128,512]{2,1,0:T(8,128)(2,1)} %broadcast_in_dim.6), calls=%async_computation | async-start | bytes 2097152 | tf_op jit(solution)/shard_map/all_to_all | solution.py:19
  18.5 13.9 %all-to-all-done = bf16[8,128,512]{2,1,0:T(8,128)(2,1)S(1)} async-done(((bf16[8,128,512]{2,1,0:T(8,128)(2,1)}), bf16[8,128,512]{2,1,0:T(8,128)(2,1)S(1)}, u32[]{:S(2)}, u32[]{:S(2)}) %all-to-all-start) | async-done | bytes 1048608 | tf_op jit(solution)/shard_map/all_to_all | solution.py:19
  33.3 4.1 %head_term.1 = bf16[4,256,896]{2,1,0:T(8,128)(2,1)} custom-call(s32[6]{0:T(128)} %stack.27.order_ref, s32[4]{0:T(128)} %assignment_ref.3, s32[8]{0:T(128)} %lengths_ref.3, bf16[1024,512]{1,0:T(8,128)(2,1)} %bitcast.32, bf16[832,512]{1,0:T(8,128)(2,1)} %w_ref.1), custom_call_target="tpu_custom_call" | custom-call | flops 872415232 | bytes 3735552 | tf_op jit(solution)/shard_map/head_term/pallas_call | solution.py:53
  37.4 30.4 %all_to_all.25 = bf16[4,256,896]{2,1,0:T(8,128)(2,1)S(1)} all-to-all(bf16[4,256,896]{2,1,0:T(8,128)(2,1)} %head_term.1), channel_id=1, replica_groups=mesh['dp'=2,'y'=4,'core'=2,'x'=4,'z'=8] {'x'}, dimensions={0} | all-to-all | bytes 3670016 | tf_op jit(solution)/shard_map/all_to_all | solution.py:24
  69.0 8.6 %all-to-all-start.2 = ((bf16[8,32,896]{2,1,0:T(8,128)(2,1)}), bf16[8,32,896]{2,1,0:T(8,128)(2,1)S(1)}, u32[]{:S(2)}, u32[]{:S(2)}) async-start(bf16[8,32,896]{2,1,0:T(8,128)(2,1)} %bitcast.7), calls=%async_computation.2 | async-start | bytes 917504 | tf_op jit(solution)/shard_map/all_to_all | solution.py:24
  77.6 8.1 %collective-permute-start.8 = (bf16[128,768]{1,0:T(8,128)(2,1)S(1)}, bf16[128,768]{1,0:T(8,128)(2,1)S(1)}, u32[]{:S(2)}, u32[]{:S(2)}) collective-permute-start(bf16[128,768]{1,0:T(8,128)(2,1)S(1)} %pad_maximum_fusion.1), channel_id=1, source_target_pairs={{0,256},{256,0},{1,257},{257,1},{2,258},{258,2},{3,259},{259,3},{4... | collective-permute-start | bytes 589832 | tf_op jit(solution)/shard_map/ppermute | solution.py:14
  85.7 12.4 %collective-permute-done.8 = bf16[128,768]{1,0:T(8,128)(2,1)S(1)} collective-permute-done((bf16[128,768]{1,0:T(8,128)(2,1)S(1)}, bf16[128,768]{1,0:T(8,128)(2,1)S(1)}, u32[]{:S(2)}, u32[]{:S(2)}) %collective-permute-start.8) | collective-permute-done | bytes 196640 | tf_op jit(solution)/shard_map/ppermute | solution.py:14
  98.2 21.5 %all-to-all-done.2 = bf16[8,32,896]{2,1,0:T(8,128)(2,1)S(1)} async-done(((bf16[8,32,896]{2,1,0:T(8,128)(2,1)}), bf16[8,32,896]{2,1,0:T(8,128)(2,1)S(1)}, u32[]{:S(2)}, u32[]{:S(2)}) %all-to-all-start.2) | async-done | bytes 458784 | tf_op jit(solution)/shard_map/all_to_all | solution.py:24
  121.3 5.0 %all-to-all-start.4 = ((bf16[8,128,1024]{2,1,0:T(8,128)(2,1)}), bf16[8,128,1024]{2,1,0:T(8,128)(2,1)S(1)}, u32[]{:S(2)}, u32[]{:S(2)}) async-start(bf16[8,128,1024]{2,1,0:T(8,128)(2,1)} %broadcast_in_dim.8), calls=%async_computation.4 | async-start | bytes 4194304 | tf_op jit(solution)/shard_map/all_to_all | solution.py:19
  126.4 39.6 %all_gather.6 = bf16[512,896]{1,0:T(8,128)(2,1)S(1)} all-gather(bf16[32,896]{1,0:T(8,128)(2,1)S(1)} %reduce_sum.37), channel_id=1, replica_groups=mesh['dp'=2,'y'=4,'core'=2,'x'=4,'z'=8] {'dp','z'}, dimensions={0}, use_global_device_ids=true | all-gather | bytes 974848 | tf_op jit(solution)/shard_map/all_gather | solution.py:280
  166.8 3.1 %collective-permute-start = (bf16[2,128,896]{2,1,0:T(8,128)(2,1)S(1)}, bf16[2,128,896]{2,1,0:T(8,128)(2,1)S(1)}, u32[]{:S(2)}, u32[]{:S(2)}) collective-permute-start(bf16[2,128,896]{2,1,0:T(8,128)(2,1)S(1)} %bitcast.35), channel_id=1, source_target_pairs={{0,8},{8,16},{16,24},{24,0},{1,9},{9,17},{17,25},{25,1},{2,10},{10... | collective-permute-start | bytes 1376264 | tf_op jit(solution)/shard_map/ppermute | solution.py:14
  169.9 2.7 %collective-permute-start.1 = (bf16[2,128,896]{2,1,0:T(8,128)(2,1)S(1)}, bf16[2,128,896]{2,1,0:T(8,128)(2,1)S(1)}, u32[]{:S(2)}, u32[]{:S(2)}) collective-permute-start(bf16[2,128,896]{2,1,0:T(8,128)(2,1)S(1)} %bitcast.36), channel_id=1, source_target_pairs={{0,24},{8,0},{16,8},{24,16},{1,25},{9,1},{17,9},{25,17},{2,26},{10... | collective-permute-start | bytes 1376264 | tf_op jit(solution)/shard_map/ppermute | solution.py:14
  172.6 4.3 %collective-permute-start.4 = (bf16[2,128,896]{2,1,0:T(8,128)(2,1)}, bf16[2,128,896]{2,1,0:T(8,128)(2,1)}, u32[]{:S(2)}, u32[]{:S(2)}) collective-permute-start(bf16[2,128,896]{2,1,0:T(8,128)(2,1)} %bitcast.16.refs_5_), channel_id=1, source_target_pairs={{0,8},{8,16},{16,24},{24,0},{1,9},{9,17},{17,25},{25,1},{2,10},{10... | collective-permute-start | bytes 1376264 | tf_op jit(solution)/shard_map/ppermute | solution.py:14
  177.0 4.3 %collective-permute-done.left.refs_1_ = bf16[2,128,896]{2,1,0:T(8,128)(2,1)S(1)} collective-permute-done((bf16[2,128,896]{2,1,0:T(8,128)(2,1)S(1)}, bf16[2,128,896]{2,1,0:T(8,128)(2,1)S(1)}, u32[]{:S(2)}, u32[]{:S(2)}) %collective-permute-start) | collective-permute-done | bytes 458784 | tf_op jit(solution)/shard_map/ppermute | solution.py:14
  181.3 4.1 %collective-permute-start.2 = (bf16[128,896]{1,0:T(8,128)(2,1)S(1)}, bf16[128,896]{1,0:T(8,128)(2,1)}, u32[]{:S(2)}, u32[]{:S(2)}) collective-permute-start(bf16[128,896]{1,0:T(8,128)(2,1)S(1)} %slice_bitcast_fusion.3), channel_id=1, source_target_pairs={{0,8},{8,16},{16,24},{24,0},{1,9},{9,17},{17,25},{25,1},{2,10},{10... | collective-permute-start | bytes 688136 | tf_op jit(solution)/shard_map/ppermute | solution.py:14
  187.3 3.7 %collective-permute-start.5 = (bf16[2,128,896]{2,1,0:T(8,128)(2,1)}, bf16[2,128,896]{2,1,0:T(8,128)(2,1)}, u32[]{:S(2)}, u32[]{:S(2)}) collective-permute-start(bf16[2,128,896]{2,1,0:T(8,128)(2,1)} %bitcast.16.refs_5_), channel_id=1, source_target_pairs={{0,24},{8,0},{16,8},{24,16},{1,25},{9,1},{17,9},{25,17},{2,26},{10... | collective-permute-start | bytes 1376264 | tf_op jit(solution)/shard_map/ppermute | solution.py:14
  192.0 2.6 %collective-permute-done.3.far_high.refs_4_ = bf16[128,896]{1,0:T(8,128)(2,1)} collective-permute-done((bf16[128,896]{1,0:T(8,128)(2,1)S(1)}, bf16[128,896]{1,0:T(8,128)(2,1)}, u32[]{:S(2)}, u32[]{:S(2)}) %collective-permute-start.3) | collective-permute-done | bytes 229408 | tf_op jit(solution)/shard_map/ppermute | solution.py:14
  194.6 7.4 %input_term.1 = bf16[1024,512]{1,0:T(8,128)(2,1)} custom-call(s32[6]{0:T(128)} %stack.27.order_ref, bf16[2,128,896]{2,1,0:T(8,128)(2,1)} %bitcast.37, bf16[2,128,896]{2,1,0:T(8,128)(2,1)} %copy-done.3, bf16[2,128,896]{2,1,0:T(8,128)(2,1)} %copy-done.4, bf16[128,896]{1,0:T(8,128)(2,1)} %collective-permute-done.2.far_low.refs_3_, ...), custom_call_target="tpu_custom_call" | custom-call | flops 1744830464 | bytes 7864320 | tf_op jit(solution)/shard_map/input_term/pallas_call | solution.py:137
  202.0 5.5 %all-to-all-start.3 = ((bf16[8,128,512]{2,1,0:T(8,128)(2,1)}), bf16[8,128,512]{2,1,0:T(8,128)(2,1)S(1)}, u32[]{:S(2)}, u32[]{:S(2)}) async-start(bf16[8,128,512]{2,1,0:T(8,128)(2,1)} %bitcast.34), calls=%async_computation.3 | async-start | bytes 2097152 | tf_op jit(solution)/shard_map/all_to_all | solution.py:24
  208.5 2.9 %collective-permute-start.6 = (bf16[128,896]{1,0:T(8,128)(2,1)S(1)}, bf16[128,896]{1,0:T(8,128)(2,1)S(1)}, u32[]{:S(2)}, u32[]{:S(2)}) collective-permute-start(bf16[128,896]{1,0:T(8,128)(2,1)S(1)} %slice_bitcast_fusion.1), channel_id=1, source_target_pairs={{0,8},{8,16},{16,24},{24,0},{1,9},{9,17},{17,25},{25,1},{2,10},{10... | collective-permute-start | bytes 688136 | tf_op jit(solution)/shard_map/ppermute | solution.py:14
  212.4 2.9 %collective-permute-start.7 = (bf16[128,896]{1,0:T(8,128)(2,1)S(1)}, bf16[128,896]{1,0:T(8,128)(2,1)}, u32[]{:S(2)}, u32[]{:S(2)}) collective-permute-start(bf16[128,896]{1,0:T(8,128)(2,1)S(1)} %slice_bitcast_fusion), channel_id=1, source_target_pairs={{0,24},{8,0},{16,8},{24,16},{1,25},{9,1},{17,9},{25,17},{2,26},{10... | collective-permute-start | bytes 688136 | tf_op jit(solution)/shard_map/ppermute | solution.py:14
  215.3 2.7 %collective-permute-done.6.refs_8_ = bf16[128,896]{1,0:T(8,128)(2,1)S(1)} collective-permute-done((bf16[128,896]{1,0:T(8,128)(2,1)S(1)}, bf16[128,896]{1,0:T(8,128)(2,1)S(1)}, u32[]{:S(2)}, u32[]{:S(2)}) %collective-permute-start.6) | collective-permute-done | bytes 229408 | tf_op jit(solution)/shard_map/ppermute | solution.py:14
  218.0 4.9 %collective-permute-done.7.refs_9_ = bf16[128,896]{1,0:T(8,128)(2,1)} collective-permute-done((bf16[128,896]{1,0:T(8,128)(2,1)S(1)}, bf16[128,896]{1,0:T(8,128)(2,1)}, u32[]{:S(2)}, u32[]{:S(2)}) %collective-permute-start.7) | collective-permute-done | bytes 229408 | tf_op jit(solution)/shard_map/ppermute | solution.py:14
  222.9 13.9 %weight_grads.1 = (bf16[832,256]{1,0:T(8,128)(2,1)}, bf16[832,256]{1,0:T(8,128)(2,1)}, bf16[416,512]{1,0:T(8,128)(2,1)}) custom-call(s32[6]{0:T(128)} %stack.27.order_ref, s32[4]{0:T(128)} %assignment_ref.3, s32[8]{0:T(128)} %lengths_ref.3, bf16[2,128,896]{2,1,0:T(8,128)(2,1)} %bitcast.38, bf16[2,128,896]{2,1,0:T(8,128)(2,1)} %copy-done.3, ...), custom_call_target="tpu_custom_call" | custom-call | flops 3489660928 | bytes 13369344 | tf_op jit(solution)/shard_map/weight_grads/pallas_call | solution.py:211
  (45 shorter events, 16.8 us)
Async XLA Ops:
  7.2 187.5 %all-gather.3.cloned.1.call-start = ((), (), s32[]{:S(2)}) async-start(), calls=%async_computation.5 | async-start | bytes 6922240 | tf_op jit(solution)/shard_map/all_gather | solution.py:269
  12.9 19.4 %all-to-all-start = ((bf16[8,128,512]{2,1,0:T(8,128)(2,1)}), bf16[8,128,512]{2,1,0:T(8,128)(2,1)S(1)}, u32[]{:S(2)}, u32[]{:S(2)}) async-start(bf16[8,128,512]{2,1,0:T(8,128)(2,1)} %broadcast_in_dim.6), calls=%async_computation | async-start | bytes 2097152 | tf_op jit(solution)/shard_map/all_to_all | solution.py:19
  32.3 1.0 copy-start.1
  67.8 9.7 %copy-start.7 = (bf16[128,512]{1,0:T(8,128)(2,1)S(1)}, bf16[128,512]{1,0:T(8,128)(2,1)}, u32[]{:S(2)}) copy-start(bf16[128,512]{1,0:T(8,128)(2,1)} %param.9) | copy-start | bytes 393220
  67.8 9.8 %copy-start.5 = (bf16[128,512]{1,0:T(8,128)(2,1)S(1)}, bf16[128,512]{1,0:T(8,128)(2,1)}, u32[]{:S(2)}) copy-start(bf16[128,512]{1,0:T(8,128)(2,1)} %param.10) | copy-start | bytes 393220
  69.0 50.7 %all-to-all-start.2 = ((bf16[8,32,896]{2,1,0:T(8,128)(2,1)}), bf16[8,32,896]{2,1,0:T(8,128)(2,1)S(1)}, u32[]{:S(2)}, u32[]{:S(2)}) async-start(bf16[8,32,896]{2,1,0:T(8,128)(2,1)} %bitcast.7), calls=%async_computation.2 | async-start | bytes 917504 | tf_op jit(solution)/shard_map/all_to_all | solution.py:24
  77.6 20.5 %collective-permute-start.8 = (bf16[128,768]{1,0:T(8,128)(2,1)S(1)}, bf16[128,768]{1,0:T(8,128)(2,1)S(1)}, u32[]{:S(2)}, u32[]{:S(2)}) collective-permute-start(bf16[128,768]{1,0:T(8,128)(2,1)S(1)} %pad_maximum_fusion.1), channel_id=1, source_target_pairs={{0,256},{256,0},{1,257},{257,1},{2,258},{258,2},{3,259},{259,3},{4... | collective-permute-start | bytes 589832 | tf_op jit(solution)/shard_map/ppermute | solution.py:14
  121.3 80.7 %all-to-all-start.4 = ((bf16[8,128,1024]{2,1,0:T(8,128)(2,1)}), bf16[8,128,1024]{2,1,0:T(8,128)(2,1)S(1)}, u32[]{:S(2)}, u32[]{:S(2)}) async-start(bf16[8,128,1024]{2,1,0:T(8,128)(2,1)} %broadcast_in_dim.8), calls=%async_computation.4 | async-start | bytes 4194304 | tf_op jit(solution)/shard_map/all_to_all | solution.py:19
  166.8 27.9 %copy-start.2 = (bf16[1,256,896]{2,1,0:T(8,128)(2,1)}, bf16[1,256,896]{2,1,0:T(8,128)(2,1)S(1)}, u32[]{:S(2)}) copy-start(bf16[1,256,896]{2,1,0:T(8,128)(2,1)S(1)} %get-tuple-element.13) | copy-start | bytes 1376260
  166.8 14.5 %collective-permute-start = (bf16[2,128,896]{2,1,0:T(8,128)(2,1)S(1)}, bf16[2,128,896]{2,1,0:T(8,128)(2,1)S(1)}, u32[]{:S(2)}, u32[]{:S(2)}) collective-permute-start(bf16[2,128,896]{2,1,0:T(8,128)(2,1)S(1)} %bitcast.35), channel_id=1, source_target_pairs={{0,8},{8,16},{16,24},{24,0},{1,9},{9,17},{17,25},{25,1},{2,10},{10... | collective-permute-start | bytes 1376264 | tf_op jit(solution)/shard_map/ppermute | solution.py:14
  169.9 15.4 %collective-permute-start.1 = (bf16[2,128,896]{2,1,0:T(8,128)(2,1)S(1)}, bf16[2,128,896]{2,1,0:T(8,128)(2,1)S(1)}, u32[]{:S(2)}, u32[]{:S(2)}) collective-permute-start(bf16[2,128,896]{2,1,0:T(8,128)(2,1)S(1)} %bitcast.36), channel_id=1, source_target_pairs={{0,24},{8,0},{16,8},{24,16},{1,25},{9,1},{17,9},{25,17},{2,26},{10... | collective-permute-start | bytes 1376264 | tf_op jit(solution)/shard_map/ppermute | solution.py:14
  172.6 34.9 %collective-permute-start.4 = (bf16[2,128,896]{2,1,0:T(8,128)(2,1)}, bf16[2,128,896]{2,1,0:T(8,128)(2,1)}, u32[]{:S(2)}, u32[]{:S(2)}) collective-permute-start(bf16[2,128,896]{2,1,0:T(8,128)(2,1)} %bitcast.16.refs_5_), channel_id=1, source_target_pairs={{0,8},{8,16},{16,24},{24,0},{1,9},{9,17},{17,25},{25,1},{2,10},{10... | collective-permute-start | bytes 1376264 | tf_op jit(solution)/shard_map/ppermute | solution.py:14
  181.2 13.4 %copy-start.3 = (bf16[2,128,896]{2,1,0:T(8,128)(2,1)}, bf16[2,128,896]{2,1,0:T(8,128)(2,1)S(1)}, u32[]{:S(2)}) copy-start(bf16[2,128,896]{2,1,0:T(8,128)(2,1)S(1)} %collective-permute-done.left.refs_1_) | copy-start | bytes 1376260
  181.3 10.7 %collective-permute-start.2 = (bf16[128,896]{1,0:T(8,128)(2,1)S(1)}, bf16[128,896]{1,0:T(8,128)(2,1)}, u32[]{:S(2)}, u32[]{:S(2)}) collective-permute-start(bf16[128,896]{1,0:T(8,128)(2,1)S(1)} %slice_bitcast_fusion.3), channel_id=1, source_target_pairs={{0,8},{8,16},{16,24},{24,0},{1,9},{9,17},{17,25},{25,1},{2,10},{10... | collective-permute-start | bytes 688136 | tf_op jit(solution)/shard_map/ppermute | solution.py:14
  185.3 9.3 %copy-start.4 = (bf16[2,128,896]{2,1,0:T(8,128)(2,1)}, bf16[2,128,896]{2,1,0:T(8,128)(2,1)S(1)}, u32[]{:S(2)}) copy-start(bf16[2,128,896]{2,1,0:T(8,128)(2,1)S(1)} %collective-permute-done.1.right.refs_2_) | copy-start | bytes 1376260
  185.4 9.2 %collective-permute-start.3 = (bf16[128,896]{1,0:T(8,128)(2,1)S(1)}, bf16[128,896]{1,0:T(8,128)(2,1)}, u32[]{:S(2)}, u32[]{:S(2)}) collective-permute-start(bf16[128,896]{1,0:T(8,128)(2,1)S(1)} %slice_bitcast_fusion.2), channel_id=1, source_target_pairs={{0,24},{8,0},{16,8},{24,16},{1,25},{9,1},{17,9},{25,17},{2,26},{10... | collective-permute-start | bytes 688136 | tf_op jit(solution)/shard_map/ppermute | solution.py:14
  187.3 24.1 %collective-permute-start.5 = (bf16[2,128,896]{2,1,0:T(8,128)(2,1)}, bf16[2,128,896]{2,1,0:T(8,128)(2,1)}, u32[]{:S(2)}, u32[]{:S(2)}) collective-permute-start(bf16[2,128,896]{2,1,0:T(8,128)(2,1)} %bitcast.16.refs_5_), channel_id=1, source_target_pairs={{0,24},{8,0},{16,8},{24,16},{1,25},{9,1},{17,9},{25,17},{2,26},{10... | collective-permute-start | bytes 1376264 | tf_op jit(solution)/shard_map/ppermute | solution.py:14
  202.0 20.9 %copy-start = (bf16[8,128,1024]{2,1,0:T(8,128)(2,1)}, bf16[8,128,1024]{2,1,0:T(8,128)(2,1)S(1)}, u32[]{:S(2)}) copy-start(bf16[8,128,1024]{2,1,0:T(8,128)(2,1)S(1)} %all-to-all-done.4) | copy-start | bytes 6291460
  202.0 34.8 %all-to-all-start.3 = ((bf16[8,128,512]{2,1,0:T(8,128)(2,1)}), bf16[8,128,512]{2,1,0:T(8,128)(2,1)S(1)}, u32[]{:S(2)}, u32[]{:S(2)}) async-start(bf16[8,128,512]{2,1,0:T(8,128)(2,1)} %bitcast.34), calls=%async_computation.3 | async-start | bytes 2097152 | tf_op jit(solution)/shard_map/all_to_all | solution.py:24
  208.5 9.5 %collective-permute-start.6 = (bf16[128,896]{1,0:T(8,128)(2,1)S(1)}, bf16[128,896]{1,0:T(8,128)(2,1)S(1)}, u32[]{:S(2)}, u32[]{:S(2)}) collective-permute-start(bf16[128,896]{1,0:T(8,128)(2,1)S(1)} %slice_bitcast_fusion.1), channel_id=1, source_target_pairs={{0,8},{8,16},{16,24},{24,0},{1,9},{9,17},{17,25},{25,1},{2,10},{10... | collective-permute-start | bytes 688136 | tf_op jit(solution)/shard_map/ppermute | solution.py:14
  212.4 10.6 %collective-permute-start.7 = (bf16[128,896]{1,0:T(8,128)(2,1)S(1)}, bf16[128,896]{1,0:T(8,128)(2,1)}, u32[]{:S(2)}, u32[]{:S(2)}) collective-permute-start(bf16[128,896]{1,0:T(8,128)(2,1)S(1)} %slice_bitcast_fusion), channel_id=1, source_target_pairs={{0,24},{8,0},{16,8},{24,16},{1,25},{9,1},{17,9},{25,17},{2,26},{10... | collective-permute-start | bytes 688136 | tf_op jit(solution)/shard_map/ppermute | solution.py:14
  218.0 4.9 %copy-start.6 = (bf16[128,896]{1,0:T(8,128)(2,1)}, bf16[128,896]{1,0:T(8,128)(2,1)S(1)}, u32[]{:S(2)}) copy-start(bf16[128,896]{1,0:T(8,128)(2,1)S(1)} %collective-permute-done.6.refs_8_) | copy-start | bytes 688132
Sparse Core Ops, SparseCore 0:
  11.5 173.0 all-gather.2

commit v9 on v8

--- a/solution.py
+++ b/solution.py
@@ -66,19 +66,13 @@
 
 
 def take_part(step, parts, head_ref):
-    here, left, right, far_low, far_high = parts
-    mid = far_low.shape[0]
-    for index, part in enumerate((here, left, right)):
+    mid = parts[0].shape[1]
+    for index, part in enumerate(parts):
         @pl.when(step == index)
         def _(part=part):
             head_ref[:mid, :] = part[0]
             head_ref[mid:, :] = part[1]
 
-    @pl.when(step == 3)
-    def _():
-        head_ref[:mid, :] = far_low[...]
-        head_ref[mid:, :] = far_high[...]
-
 
 def whole(value):
     return pl.BlockSpec(value.shape, lambda i, *_: (0,) * value.ndim)
@@ -90,9 +84,18 @@
     )
 
 
+def pack_kernel(gate_ref, up_ref, out_ref):
+    ffw = gate_ref.shape[1]
+    body = ffw // 128 * 128
+    out_ref[:, :body] = gate_ref[:, :body]
+    out_ref[:, body : 2 * body] = up_ref[:, :body]
+    out_ref[:, 2 * body : body + ffw] = gate_ref[:, body:]
+    out_ref[:, body + ffw :] = up_ref[:, body:]
+
+
 def pack_pair(gate, up):
-    body = gate.shape[1] // 128 * 128
-    return jnp.concatenate([gate[:, :body], up[:, :body], gate[:, body:], up[:, body:]], axis=1)
+    shape = jax.ShapeDtypeStruct((gate.shape[0], 2 * gate.shape[1]), gate.dtype)
+    return pl.pallas_call(pack_kernel, out_shape=shape, name="pack_pair")(gate, up)
 
 
 def swiglu_terms(saved_ref):
@@ -104,9 +107,9 @@
     turned = pltpu.roll(tail, ffw - body, 1)
     gate = jnp.concatenate([pair[:, :body], tail[:, : ffw - body]], axis=1)
     up = jnp.concatenate([pair[:, body : 2 * body], turned[:, : ffw - body]], axis=1)
-    sig = jax.nn.sigmoid(gate)
+    sig = 0.5 * jnp.tanh(0.5 * gate) + 0.5
     silu = gate * sig
-    return up, silu, up * sig * (1.0 + gate * (1.0 - sig))
+    return up, silu, up * (sig + silu * (1.0 - sig))
 
 
 def gradients(head_ref, saved_ref):
@@ -120,10 +123,10 @@
 
 
 def input_kernel(
-    order_ref, here, left, right, far_low, far_high, saved_ref, w_gate_ref, w_up_ref,
+    order_ref, here, left, right, far, saved_ref, w_gate_ref, w_up_ref,
     out_ref, head_ref,
 ):
-    take_part(pl.program_id(0), (here, left, right, far_low, far_high), head_ref)
+    take_part(pl.program_id(0), (here, left, right, far), head_ref)
     grad_gate, grad_up, _ = gradients(head_ref, saved_ref)
     term = jnp.dot(grad_gate, w_gate_ref[...], preferred_element_type=jnp.float32)
     term += jnp.dot(grad_up, w_up_ref[...], preferred_element_type=jnp.float32)
@@ -158,7 +161,7 @@
     scale, order_ref, assignment_ref, lengths_ref,
     *refs,
 ):
-    parts_own, parts_away, refs = refs[:5], refs[5:10], refs[10:]
+    parts_own, parts_away, refs = refs[:4], refs[4:8], refs[8:]
     saved_own, saved_away, act_own, act_away, cot_own, cot_away = refs[:6]
     gate_ref, up_ref, down_ref, gate_acc, up_acc, down_acc, head_own, head_away = refs[6:]
     step = pl.program_id(0)
@@ -235,10 +238,11 @@
     )(*scalars, *head_own, *head_away, saved, saved, rest, rest, cot, rest)
 
 
-def gather_x(block):
-    left, right = shift(block, "x", N_X, 1), shift(block, "x", N_X, -1)
-    far_low, far_high = shift(left[0], "x", N_X, 1), shift(right[1], "x", N_X, -1)
-    return block, left, right, far_low, far_high
+def gather_x(block, onward):
+    left = shift(block, "x", N_X, 1)
+    right = shift(block, "x", N_X, -1)
+    far = shift(left if onward == 1 else right, "x", N_X, onward)
+    return block, left, right, far
 
 
 def on_device(
@@ -280,8 +284,8 @@
     head = lax.all_gather(head, ("dp", "z"), axis=0, tiled=True)
     head = head.reshape(n_dp, N_Z * own, lanes)
     halves = (2, N_Z * own // 2, lanes)
-    head_own = gather_x(pick(head, batch).reshape(halves))
-    head_away = gather_x(pick(head, away).reshape(halves))
+    head_own = gather_x(pick(head, batch).reshape(halves), 1)
+    head_away = gather_x(pick(head, away).reshape(halves), -1)
 
     term = input_term(order, head_own, saved, w_gate.T, w_up.T)
     input_grad = sum_over(term, row_axes, n_row)

time: 246 us -> 243 us (0.988)
  the two profiles are of different devices: /device:TPU:14 before, /device:TPU:46 now
where the time goes in v9:
time: 243 us; the launch traced here: 242 us
  blocking collectives  69.7 us (29%)
  waiting for transfers between devices  66 us (27%)
  starting transfers between devices  56.6 us (23%)
  Pallas kernels  27.3 us (11%)
  between operations  14.2 us (6%)
  local copies, waits for them, and re-layouts  6.11 us (3%)
    all_gather x1, blocking collectives, on_device(): head = lax.all_gather(head, ('dp', 'z'), axis=0, tiled=True)  43.2 us
    ppermute x7, waiting for transfers between devices, shift(): lax.ppermute(value, axis, [(i, (i + step) % size) for i in range(size)])  32.6 us
    ppermute x7, starting transfers between devices, shift(): lax.ppermute(value, axis, [(i, (i + step) % size) for i in range(size)])  29.8 us
    all_to_all x1, blocking collectives, sum_over(): lax.all_to_all(blocks, axis, split_axis=0, concat_axis=0, tiled=True)  26.5 us
    all_to_all x2, waiting for transfers between devices, sum_over(): lax.all_to_all(blocks, axis, split_axis=0, concat_axis=0, tiled=True)  19.5 us
    all_to_all x2, starting transfers between devices, sum_over(): lax.all_to_all(blocks, axis, split_axis=0, concat_axis=0, tiled=True)  16.9 us
    pallas_call x1, Pallas kernels, weight_grads(): pl.pallas_call(functools.partial(weight_kernel, scale), grid_spec=pltpu.P...  14 us
    all_to_all x2, waiting for transfers between devices, spread(): return lax.all_to_all(copies, axis, split_axis=0, concat_axis=0, tiled=True)  13.8 us
  transfers between devices with their start and end apart: 12, of which 7 were waited for; matrix products, arithmetic and copies ran while one was open for 3% of the time, Pallas kernels for 11%

profile of v9, /device:TPU:46, one launch (start us, length us, event | category | flops | bytes accessed | tf_op | source)
XLA Modules:
  0.0 242.0 jit_solution(4325387624143062331)
XLA Ops:
  8.8 2.0 broadcast_in_dim.6
  10.8 4.9 %all-to-all-start = ((bf16[8,128,512]{2,1,0:T(8,128)(2,1)}), bf16[8,128,512]{2,1,0:T(8,128)(2,1)S(1)}, u32[]{:S(2)}, u32[]{:S(2)}) async-start(bf16[8,128,512]{2,1,0:T(8,128)(2,1)} %broadcast_in_dim.6), calls=%async_computation | async-start | bytes 2097152 | tf_op jit(solution)/shard_map/all_to_all | solution.py:19
  16.3 13.8 %all-to-all-done = bf16[8,128,512]{2,1,0:T(8,128)(2,1)S(1)} async-done(((bf16[8,128,512]{2,1,0:T(8,128)(2,1)}), bf16[8,128,512]{2,1,0:T(8,128)(2,1)S(1)}, u32[]{:S(2)}, u32[]{:S(2)}) %all-to-all-start) | async-done | bytes 1048608 | tf_op jit(solution)/shard_map/all_to_all | solution.py:19
  31.1 4.1 %head_term.1 = bf16[4,256,896]{2,1,0:T(8,128)(2,1)} custom-call(s32[6]{0:T(128)} %stack.27.order_ref, s32[4]{0:T(128)} %assignment_ref.3, s32[8]{0:T(128)} %lengths_ref.3, bf16[1024,512]{1,0:T(8,128)(2,1)} %bitcast.24, bf16[832,512]{1,0:T(8,128)(2,1)} %w_ref.1), custom_call_target="tpu_custom_call" | custom-call | flops 872415232 | bytes 3735552 | tf_op jit(solution)/shard_map/head_term/pallas_call | solution.py:53
  35.2 26.5 %all_to_all.25 = bf16[4,256,896]{2,1,0:T(8,128)(2,1)S(1)} all-to-all(bf16[4,256,896]{2,1,0:T(8,128)(2,1)} %head_term.1), channel_id=1, replica_groups=mesh['dp'=2,'y'=4,'core'=2,'x'=4,'z'=8] {'x'}, dimensions={0} | all-to-all | bytes 3670016 | tf_op jit(solution)/shard_map/all_to_all | solution.py:24
  62.9 12.6 %all-to-all-start.2 = ((bf16[8,32,896]{2,1,0:T(8,128)(2,1)}), bf16[8,32,896]{2,1,0:T(8,128)(2,1)S(1)}, u32[]{:S(2)}, u32[]{:S(2)}) async-start(bf16[8,32,896]{2,1,0:T(8,128)(2,1)} %bitcast.7), calls=%async_computation.2 | async-start | bytes 917504 | tf_op jit(solution)/shard_map/all_to_all | solution.py:24
  75.5 8.1 %collective-permute-start.6 = (bf16[128,768]{1,0:T(8,128)(2,1)S(1)}, bf16[128,768]{1,0:T(8,128)(2,1)S(1)}, u32[]{:S(2)}, u32[]{:S(2)}) collective-permute-start(bf16[128,768]{1,0:T(8,128)(2,1)S(1)} %pad_maximum_fusion.1), channel_id=1, source_target_pairs={{0,256},{256,0},{1,257},{257,1},{2,258},{258,2},{3,259},{259,3},{4... | collective-permute-start | bytes 589832 | tf_op jit(solution)/shard_map/ppermute | solution.py:14
  83.7 9.9 %collective-permute-done.6 = bf16[128,768]{1,0:T(8,128)(2,1)S(1)} collective-permute-done((bf16[128,768]{1,0:T(8,128)(2,1)S(1)}, bf16[128,768]{1,0:T(8,128)(2,1)S(1)}, u32[]{:S(2)}, u32[]{:S(2)}) %collective-permute-start.6) | collective-permute-done | bytes 196640 | tf_op jit(solution)/shard_map/ppermute | solution.py:14
  93.6 19.5 %all-to-all-done.2 = bf16[8,32,896]{2,1,0:T(8,128)(2,1)S(1)} async-done(((bf16[8,32,896]{2,1,0:T(8,128)(2,1)}), bf16[8,32,896]{2,1,0:T(8,128)(2,1)S(1)}, u32[]{:S(2)}, u32[]{:S(2)}) %all-to-all-start.2) | async-done | bytes 458784 | tf_op jit(solution)/shard_map/all_to_all | solution.py:24
  114.7 5.0 %all-to-all-start.4 = ((bf16[8,128,1024]{2,1,0:T(8,128)(2,1)}), bf16[8,128,1024]{2,1,0:T(8,128)(2,1)S(1)}, u32[]{:S(2)}, u32[]{:S(2)}) async-start(bf16[8,128,1024]{2,1,0:T(8,128)(2,1)} %broadcast_in_dim.8), calls=%async_computation.4 | async-start | bytes 4194304 | tf_op jit(solution)/shard_map/all_to_all | solution.py:19
  119.8 43.2 %all_gather.6 = bf16[512,896]{1,0:T(8,128)(2,1)S(1)} all-gather(bf16[32,896]{1,0:T(8,128)(2,1)S(1)} %reduce_sum.37), channel_id=1, replica_groups=mesh['dp'=2,'y'=4,'core'=2,'x'=4,'z'=8] {'dp','z'}, dimensions={0}, use_global_device_ids=true | all-gather | bytes 974848 | tf_op jit(solution)/shard_map/all_gather | solution.py:284
  163.9 4.6 %collective-permute-start = (bf16[2,128,896]{2,1,0:T(8,128)(2,1)S(1)}, bf16[2,128,896]{2,1,0:T(8,128)(2,1)S(1)}, u32[]{:S(2)}, u32[]{:S(2)}) collective-permute-start(bf16[2,128,896]{2,1,0:T(8,128)(2,1)S(1)} %bitcast.27), channel_id=1, source_target_pairs={{0,8},{8,16},{16,24},{24,0},{1,9},{9,17},{17,25},{25,1},{2,10},{10... | collective-permute-start | bytes 1376264 | tf_op jit(solution)/shard_map/ppermute | solution.py:14
  168.5 1.9 collective-permute-start.1
  170.5 5.0 %collective-permute-done.left.refs_1_ = bf16[2,128,896]{2,1,0:T(8,128)(2,1)S(1)} collective-permute-done((bf16[2,128,896]{2,1,0:T(8,128)(2,1)S(1)}, bf16[2,128,896]{2,1,0:T(8,128)(2,1)S(1)}, u32[]{:S(2)}, u32[]{:S(2)}) %collective-permute-start) | collective-permute-done | bytes 458784 | tf_op jit(solution)/shard_map/ppermute | solution.py:14
  175.4 5.6 %collective-permute-start.2 = (bf16[2,128,896]{2,1,0:T(8,128)(2,1)S(1)}, bf16[2,128,896]{2,1,0:T(8,128)(2,1)}, u32[]{:S(2)}, u32[]{:S(2)}) collective-permute-start(bf16[2,128,896]{2,1,0:T(8,128)(2,1)S(1)} %collective-permute-done.left.refs_1_), channel_id=1, source_target_pairs={{0,8},{8,16},{16,24},{24,0},{1,9},{9,17},{17,25},{25,1},{2,10},{10... | collective-permute-start | bytes 1376264 | tf_op jit(solution)/shard_map/ppermute | solution.py:14
  181.0 1.9 collective-permute-start.4
  183.0 4.0 %collective-permute-done.2.far.refs_3_ = bf16[2,128,896]{2,1,0:T(8,128)(2,1)} collective-permute-done((bf16[2,128,896]{2,1,0:T(8,128)(2,1)S(1)}, bf16[2,128,896]{2,1,0:T(8,128)(2,1)}, u32[]{:S(2)}, u32[]{:S(2)}) %collective-permute-start.2) | collective-permute-done | bytes 458784 | tf_op jit(solution)/shard_map/ppermute | solution.py:14
  187.0 7.6 %input_term.1 = bf16[1024,512]{1,0:T(8,128)(2,1)} custom-call(s32[6]{0:T(128)} %stack.27.order_ref, bf16[2,128,896]{2,1,0:T(8,128)(2,1)} %bitcast.29, bf16[2,128,896]{2,1,0:T(8,128)(2,1)} %copy-done.3, bf16[2,128,896]{2,1,0:T(8,128)(2,1)} %copy-done.4, bf16[2,128,896]{2,1,0:T(8,128)(2,1)} %collective-permute-done.2.far.refs_3_, ...), custom_call_target="tpu_custom_call" | custom-call | flops 1744830464 | bytes 7864320 | tf_op jit(solution)/shard_map/input_term/pallas_call | solution.py:140
  194.6 4.2 %all-to-all-start.3 = ((bf16[8,128,512]{2,1,0:T(8,128)(2,1)}), bf16[8,128,512]{2,1,0:T(8,128)(2,1)S(1)}, u32[]{:S(2)}, u32[]{:S(2)}) async-start(bf16[8,128,512]{2,1,0:T(8,128)(2,1)} %bitcast.26), calls=%async_computation.3 | async-start | bytes 2097152 | tf_op jit(solution)/shard_map/all_to_all | solution.py:24
  198.9 5.7 %collective-permute-start.3 = (bf16[2,128,896]{2,1,0:T(8,128)(2,1)}, bf16[2,128,896]{2,1,0:T(8,128)(2,1)}, u32[]{:S(2)}, u32[]{:S(2)}) collective-permute-start(bf16[2,128,896]{2,1,0:T(8,128)(2,1)} %bitcast.14.refs_4_), channel_id=1, source_target_pairs={{0,8},{8,16},{16,24},{24,0},{1,9},{9,17},{17,25},{25,1},{2,10},{10... | collective-permute-start | bytes 1376264 | tf_op jit(solution)/shard_map/ppermute | solution.py:14
  204.6 1.9 collective-permute-start.5
  206.5 8.4 %collective-permute-done.3.refs_5_ = bf16[2,128,896]{2,1,0:T(8,128)(2,1)} collective-permute-done((bf16[2,128,896]{2,1,0:T(8,128)(2,1)}, bf16[2,128,896]{2,1,0:T(8,128)(2,1)}, u32[]{:S(2)}, u32[]{:S(2)}) %collective-permute-start.3) | collective-permute-done | bytes 458784 | tf_op jit(solution)/shard_map/ppermute | solution.py:14
  215.0 5.3 %collective-permute-done.5.refs_7_ = bf16[2,128,896]{2,1,0:T(8,128)(2,1)} collective-permute-done((bf16[2,128,896]{2,1,0:T(8,128)(2,1)}, bf16[2,128,896]{2,1,0:T(8,128)(2,1)}, u32[]{:S(2)}, u32[]{:S(2)}) %collective-permute-start.5) | collective-permute-done | bytes 458784 | tf_op jit(solution)/shard_map/ppermute | solution.py:14
  220.3 14.0 %weight_grads.1 = (bf16[832,256]{1,0:T(8,128)(2,1)}, bf16[832,256]{1,0:T(8,128)(2,1)}, bf16[416,512]{1,0:T(8,128)(2,1)}) custom-call(s32[6]{0:T(128)} %stack.27.order_ref, s32[4]{0:T(128)} %assignment_ref.3, s32[8]{0:T(128)} %lengths_ref.3, bf16[2,128,896]{2,1,0:T(8,128)(2,1)} %bitcast.30, bf16[2,128,896]{2,1,0:T(8,128)(2,1)} %copy-done.3, ...), custom_call_target="tpu_custom_call" | custom-call | flops 3489660928 | bytes 13369344 | tf_op jit(solution)/shard_map/weight_grads/pallas_call | solution.py:214
  (31 shorter events, 7.8 us)
Async XLA Ops:
  7.2 179.8 %all-gather.3.cloned.1.call-start = ((), (), s32[]{:S(2)}) async-start(), calls=%async_computation.5 | async-start | bytes 6922240 | tf_op jit(solution)/shard_map/all_gather | solution.py:273
  10.8 19.4 %all-to-all-start = ((bf16[8,128,512]{2,1,0:T(8,128)(2,1)}), bf16[8,128,512]{2,1,0:T(8,128)(2,1)S(1)}, u32[]{:S(2)}, u32[]{:S(2)}) async-start(bf16[8,128,512]{2,1,0:T(8,128)(2,1)} %broadcast_in_dim.6), calls=%async_computation | async-start | bytes 2097152 | tf_op jit(solution)/shard_map/all_to_all | solution.py:19
  30.2 1.0 copy-start.1
  61.7 13.8 %copy-start.6 = (bf16[128,512]{1,0:T(8,128)(2,1)S(1)}, bf16[128,512]{1,0:T(8,128)(2,1)}, u32[]{:S(2)}) copy-start(bf16[128,512]{1,0:T(8,128)(2,1)} %param.9) | copy-start | bytes 393220
  61.7 13.8 %copy-start.5 = (bf16[128,512]{1,0:T(8,128)(2,1)S(1)}, bf16[128,512]{1,0:T(8,128)(2,1)}, u32[]{:S(2)}) copy-start(bf16[128,512]{1,0:T(8,128)(2,1)} %param.10) | copy-start | bytes 393220
  62.9 50.2 %all-to-all-start.2 = ((bf16[8,32,896]{2,1,0:T(8,128)(2,1)}), bf16[8,32,896]{2,1,0:T(8,128)(2,1)S(1)}, u32[]{:S(2)}, u32[]{:S(2)}) async-start(bf16[8,32,896]{2,1,0:T(8,128)(2,1)} %bitcast.7), calls=%async_computation.2 | async-start | bytes 917504 | tf_op jit(solution)/shard_map/all_to_all | solution.py:24
  75.5 18.0 %collective-permute-start.6 = (bf16[128,768]{1,0:T(8,128)(2,1)S(1)}, bf16[128,768]{1,0:T(8,128)(2,1)S(1)}, u32[]{:S(2)}, u32[]{:S(2)}) collective-permute-start(bf16[128,768]{1,0:T(8,128)(2,1)S(1)} %pad_maximum_fusion.1), channel_id=1, source_target_pairs={{0,256},{256,0},{1,257},{257,1},{2,258},{258,2},{3,259},{259,3},{4... | collective-permute-start | bytes 589832 | tf_op jit(solution)/shard_map/ppermute | solution.py:14
  114.7 79.9 %all-to-all-start.4 = ((bf16[8,128,1024]{2,1,0:T(8,128)(2,1)}), bf16[8,128,1024]{2,1,0:T(8,128)(2,1)S(1)}, u32[]{:S(2)}, u32[]{:S(2)}) async-start(bf16[8,128,1024]{2,1,0:T(8,128)(2,1)} %broadcast_in_dim.8), calls=%async_computation.4 | async-start | bytes 4194304 | tf_op jit(solution)/shard_map/all_to_all | solution.py:19
  163.9 23.1 %copy-start.2 = (bf16[1,256,896]{2,1,0:T(8,128)(2,1)}, bf16[1,256,896]{2,1,0:T(8,128)(2,1)S(1)}, u32[]{:S(2)}) copy-start(bf16[1,256,896]{2,1,0:T(8,128)(2,1)S(1)} %get-tuple-element.13) | copy-start | bytes 1376260
  163.9 11.5 %collective-permute-start = (bf16[2,128,896]{2,1,0:T(8,128)(2,1)S(1)}, bf16[2,128,896]{2,1,0:T(8,128)(2,1)S(1)}, u32[]{:S(2)}, u32[]{:S(2)}) collective-permute-start(bf16[2,128,896]{2,1,0:T(8,128)(2,1)S(1)} %bitcast.27), channel_id=1, source_target_pairs={{0,8},{8,16},{16,24},{24,0},{1,9},{9,17},{17,25},{25,1},{2,10},{10... | collective-permute-start | bytes 1376264 | tf_op jit(solution)/shard_map/ppermute | solution.py:14
  168.5 14.4 %collective-permute-start.1 = (bf16[2,128,896]{2,1,0:T(8,128)(2,1)S(1)}, bf16[2,128,896]{2,1,0:T(8,128)(2,1)S(1)}, u32[]{:S(2)}, u32[]{:S(2)}) collective-permute-start(bf16[2,128,896]{2,1,0:T(8,128)(2,1)S(1)} %bitcast.28), channel_id=1, source_target_pairs={{0,24},{8,0},{16,8},{24,16},{1,25},{9,1},{17,9},{25,17},{2,26},{10... | collective-permute-start | bytes 1376264 | tf_op jit(solution)/shard_map/ppermute | solution.py:14
  175.4 11.6 %copy-start.3 = (bf16[2,128,896]{2,1,0:T(8,128)(2,1)}, bf16[2,128,896]{2,1,0:T(8,128)(2,1)S(1)}, u32[]{:S(2)}) copy-start(bf16[2,128,896]{2,1,0:T(8,128)(2,1)S(1)} %collective-permute-done.left.refs_1_) | copy-start | bytes 1376260
  175.4 11.6 %collective-permute-start.2 = (bf16[2,128,896]{2,1,0:T(8,128)(2,1)S(1)}, bf16[2,128,896]{2,1,0:T(8,128)(2,1)}, u32[]{:S(2)}, u32[]{:S(2)}) collective-permute-start(bf16[2,128,896]{2,1,0:T(8,128)(2,1)S(1)} %collective-permute-done.left.refs_1_), channel_id=1, source_target_pairs={{0,8},{8,16},{16,24},{24,0},{1,9},{9,17},{17,25},{25,1},{2,10},{10... | collective-permute-start | bytes 1376264 | tf_op jit(solution)/shard_map/ppermute | solution.py:14
  181.0 23.6 %collective-permute-start.4 = (bf16[2,128,896]{2,1,0:T(8,128)(2,1)}, bf16[2,128,896]{2,1,0:T(8,128)(2,1)}, u32[]{:S(2)}, u32[]{:S(2)}) collective-permute-start(bf16[2,128,896]{2,1,0:T(8,128)(2,1)} %bitcast.14.refs_4_), channel_id=1, source_target_pairs={{0,24},{8,0},{16,8},{24,16},{1,25},{9,1},{17,9},{25,17},{2,26},{10... | collective-permute-start | bytes 1376264 | tf_op jit(solution)/shard_map/ppermute | solution.py:14
  183.0 4.0 %copy-start.4 = (bf16[2,128,896]{2,1,0:T(8,128)(2,1)}, bf16[2,128,896]{2,1,0:T(8,128)(2,1)S(1)}, u32[]{:S(2)}) copy-start(bf16[2,128,896]{2,1,0:T(8,128)(2,1)S(1)} %collective-permute-done.1.right.refs_2_) | copy-start | bytes 1376260
  194.6 25.7 %copy-start = (bf16[8,128,1024]{2,1,0:T(8,128)(2,1)}, bf16[8,128,1024]{2,1,0:T(8,128)(2,1)S(1)}, u32[]{:S(2)}) copy-start(bf16[8,128,1024]{2,1,0:T(8,128)(2,1)S(1)} %all-to-all-done.4) | copy-start | bytes 6291460
  194.6 39.7 %all-to-all-start.3 = ((bf16[8,128,512]{2,1,0:T(8,128)(2,1)}), bf16[8,128,512]{2,1,0:T(8,128)(2,1)S(1)}, u32[]{:S(2)}, u32[]{:S(2)}) async-start(bf16[8,128,512]{2,1,0:T(8,128)(2,1)} %bitcast.26), calls=%async_computation.3 | async-start | bytes 2097152 | tf_op jit(solution)/shard_map/all_to_all | solution.py:24
  198.9 16.1 %collective-permute-start.3 = (bf16[2,128,896]{2,1,0:T(8,128)(2,1)}, bf16[2,128,896]{2,1,0:T(8,128)(2,1)}, u32[]{:S(2)}, u32[]{:S(2)}) collective-permute-start(bf16[2,128,896]{2,1,0:T(8,128)(2,1)} %bitcast.14.refs_4_), channel_id=1, source_target_pairs={{0,8},{8,16},{16,24},{24,0},{1,9},{9,17},{17,25},{25,1},{2,10},{10... | collective-permute-start | bytes 1376264 | tf_op jit(solution)/shard_map/ppermute | solution.py:14
  204.6 15.7 %collective-permute-start.5 = (bf16[2,128,896]{2,1,0:T(8,128)(2,1)}, bf16[2,128,896]{2,1,0:T(8,128)(2,1)}, u32[]{:S(2)}, u32[]{:S(2)}) collective-permute-start(bf16[2,128,896]{2,1,0:T(8,128)(2,1)} %collective-permute-done.4.refs_6_), channel_id=1, source_target_pairs={{0,24},{8,0},{16,8},{24,16},{1,25},{9,1},{17,9},{25,17},{2,26},{10... | collective-permute-start | bytes 1376264 | tf_op jit(solution)/shard_map/ppermute | solution.py:14
Sparse Core Ops, SparseCore 0:
  11.5 171.7 all-gather.2

commit v10 on v8

--- a/solution.py
+++ b/solution.py
@@ -86,17 +86,27 @@
 
 def saved_block(saved, which):
     return pl.BlockSpec(
-        (1, 1) + saved.shape[2:], lambda i, order, *_: (order[2 + i], order[which], 0, 0, 0)
-    )
+        (1, saved.shape[1], 1) + saved.shape[3:],
+        lambda i, order, *_: (order[which], 0, order[2 + i], 0, 0),
+    )
+
+
+def pack_kernel(gate_ref, up_ref, out_ref):
+    ffw = gate_ref.shape[1]
+    body = ffw // 128 * 128
+    out_ref[:, :body] = gate_ref[:, :body]
+    out_ref[:, body : 2 * body] = up_ref[:, :body]
+    out_ref[:, 2 * body : body + ffw] = gate_ref[:, body:]
+    out_ref[:, body + ffw :] = up_ref[:, body:]
 
 
 def pack_pair(gate, up):
-    body = gate.shape[1] // 128 * 128
-    return jnp.concatenate([gate[:, :body], up[:, :body], gate[:, body:], up[:, body:]], axis=1)
+    shape = jax.ShapeDtypeStruct((gate.shape[0], 2 * gate.shape[1]), gate.dtype)
+    return pl.pallas_call(pack_kernel, out_shape=shape, name="pack_pair")(gate, up)
 
 
 def swiglu_terms(saved_ref):
-    pair = saved_ref[0, 0]
+    pair = saved_ref[0, :, 0]
     pair = pair.reshape(pair.shape[0] * pair.shape[1], pair.shape[2]).astype(jnp.float32)
     ffw = pair.shape[1] // 2
     body = ffw // 128 * 128
@@ -266,8 +276,8 @@
     partner = shift(jnp.concatenate([cotangent, act_other], axis=1), "dp", n_dp, 1)
 
     saved = pack_pair(gate_saved, up_saved)[None]
-    saved = lax.all_gather(saved, ("x", "dp", "z"), axis=0, tiled=True)
-    saved = saved.reshape(N_X, n_dp, N_Z, own, 2 * ffw)
+    saved = lax.all_gather(saved, ("dp", "z", "x"), axis=0, tiled=True)
+    saved = saved.reshape(n_dp, N_Z, N_X, own, 2 * ffw)
 
     cot_own = spread(cotangent, row_axes, n_row).reshape(tok, width)
     block_term = head_term(scalars, cot_own, w_down, lanes)

time: 246 us -> 244 us (level)
  local copies, waits for them, and re-layouts: 11.8 us -> 8.01 us
    slice x4 -> x0, local copies, waits for them, and re-layouts: 3.01 us -> none  [the longest x1 0.8 us: pack_pair(): gate[:, :body]]
where the time goes in v10:
time: 244 us; the launch traced here: 243 us
  blocking collectives  70.9 us (29%)
  waiting for transfers between devices  64.2 us (26%)
  starting transfers between devices  56.7 us (23%)
  Pallas kernels  26.8 us (11%)
  between operations  14.2 us (6%)
  local copies, waits for them, and re-layouts  8.01 us (3%)
    all_gather x1, blocking collectives, on_device(): head = lax.all_gather(head, ('dp', 'z'), axis=0, tiled=True)  40.5 us
    ppermute x9, starting transfers between devices, shift(): lax.ppermute(value, axis, [(i, (i + step) % size) for i in range(size)])  34.8 us
    all_to_all x1, blocking collectives, sum_over(): lax.all_to_all(blocks, axis, split_axis=0, concat_axis=0, tiled=True)  30.4 us
    ppermute x9, waiting for transfers between devices, shift(): lax.ppermute(value, axis, [(i, (i + step) % size) for i in range(size)])  29.1 us
    all_to_all x2, waiting for transfers between devices, sum_over(): lax.all_to_all(blocks, axis, split_axis=0, concat_axis=0, tiled=True)  21.2 us
    all_to_all x2, waiting for transfers between devices, spread(): return lax.all_to_all(copies, axis, split_axis=0, concat_axis=0, tiled=True)  13.9 us
    pallas_call x1, Pallas kernels, weight_grads(): pl.pallas_call(functools.partial(weight_kernel, scale), grid_spec=pltpu.P...  13.7 us
    all_to_all x2, starting transfers between devices, sum_over(): lax.all_to_all(blocks, axis, split_axis=0, concat_axis=0, tiled=True)  12.1 us
  transfers between devices with their start and end apart: 14, of which 8 were waited for; matrix products, arithmetic and copies ran while one was open for 3% of the time, Pallas kernels for 10%

profile of v10, /device:TPU:14, one launch (start us, length us, event | category | flops | bytes accessed | tf_op | source)
XLA Modules:
  0.0 242.9 jit_solution(7345175464537860552)
XLA Ops:
  8.8 2.0 broadcast_in_dim.6
  10.8 4.9 %all-to-all-start = ((bf16[8,128,512]{2,1,0:T(8,128)(2,1)}), bf16[8,128,512]{2,1,0:T(8,128)(2,1)S(1)}, u32[]{:S(2)}, u32[]{:S(2)}) async-start(bf16[8,128,512]{2,1,0:T(8,128)(2,1)} %broadcast_in_dim.6), calls=%async_computation | async-start | bytes 2097152 | tf_op jit(solution)/shard_map/all_to_all | solution.py:19
  16.3 13.9 %all-to-all-done = bf16[8,128,512]{2,1,0:T(8,128)(2,1)S(1)} async-done(((bf16[8,128,512]{2,1,0:T(8,128)(2,1)}), bf16[8,128,512]{2,1,0:T(8,128)(2,1)S(1)}, u32[]{:S(2)}, u32[]{:S(2)}) %all-to-all-start) | async-done | bytes 1048608 | tf_op jit(solution)/shard_map/all_to_all | solution.py:19
  31.1 4.1 %head_term.1 = bf16[4,256,896]{2,1,0:T(8,128)(2,1)} custom-call(s32[6]{0:T(128)} %stack.27.order_ref, s32[4]{0:T(128)} %assignment_ref.3, s32[8]{0:T(128)} %lengths_ref.3, bf16[1024,512]{1,0:T(8,128)(2,1)} %bitcast.32, bf16[832,512]{1,0:T(8,128)(2,1)} %w_ref.1), custom_call_target="tpu_custom_call" | custom-call | flops 872415232 | bytes 3735552 | tf_op jit(solution)/shard_map/head_term/pallas_call | solution.py:53
  35.2 30.4 %all_to_all.25 = bf16[4,256,896]{2,1,0:T(8,128)(2,1)S(1)} all-to-all(bf16[4,256,896]{2,1,0:T(8,128)(2,1)} %head_term.1), channel_id=1, replica_groups=mesh['dp'=2,'y'=4,'core'=2,'x'=4,'z'=8] {'x'}, dimensions={0} | all-to-all | bytes 3670016 | tf_op jit(solution)/shard_map/all_to_all | solution.py:24
  66.8 8.6 %all-to-all-start.2 = ((bf16[8,32,896]{2,1,0:T(8,128)(2,1)}), bf16[8,32,896]{2,1,0:T(8,128)(2,1)S(1)}, u32[]{:S(2)}, u32[]{:S(2)}) async-start(bf16[8,32,896]{2,1,0:T(8,128)(2,1)} %bitcast.7), calls=%async_computation.2 | async-start | bytes 917504 | tf_op jit(solution)/shard_map/all_to_all | solution.py:24
  75.4 8.1 %collective-permute-start.8 = (bf16[128,768]{1,0:T(8,128)(2,1)S(1)}, bf16[128,768]{1,0:T(8,128)(2,1)S(1)}, u32[]{:S(2)}, u32[]{:S(2)}) collective-permute-start(bf16[128,768]{1,0:T(8,128)(2,1)S(1)} %pad_maximum_fusion.1), channel_id=1, source_target_pairs={{0,256},{256,0},{1,257},{257,1},{2,258},{258,2},{3,259},{259,3},{4... | collective-permute-start | bytes 589832 | tf_op jit(solution)/shard_map/ppermute | solution.py:14
  83.6 12.6 %collective-permute-done.8 = bf16[128,768]{1,0:T(8,128)(2,1)S(1)} collective-permute-done((bf16[128,768]{1,0:T(8,128)(2,1)S(1)}, bf16[128,768]{1,0:T(8,128)(2,1)S(1)}, u32[]{:S(2)}, u32[]{:S(2)}) %collective-permute-start.8) | collective-permute-done | bytes 196640 | tf_op jit(solution)/shard_map/ppermute | solution.py:14
  96.3 21.1 %all-to-all-done.2 = bf16[8,32,896]{2,1,0:T(8,128)(2,1)S(1)} async-done(((bf16[8,32,896]{2,1,0:T(8,128)(2,1)}), bf16[8,32,896]{2,1,0:T(8,128)(2,1)S(1)}, u32[]{:S(2)}, u32[]{:S(2)}) %all-to-all-start.2) | async-done | bytes 458784 | tf_op jit(solution)/shard_map/all_to_all | solution.py:24
  119.1 4.9 %all-to-all-start.4 = ((bf16[8,128,1024]{2,1,0:T(8,128)(2,1)}), bf16[8,128,1024]{2,1,0:T(8,128)(2,1)S(1)}, u32[]{:S(2)}, u32[]{:S(2)}) async-start(bf16[8,128,1024]{2,1,0:T(8,128)(2,1)} %broadcast_in_dim.8), calls=%async_computation.4 | async-start | bytes 4194304 | tf_op jit(solution)/shard_map/all_to_all | solution.py:19
  124.0 40.5 %all_gather.6 = bf16[512,896]{1,0:T(8,128)(2,1)S(1)} all-gather(bf16[32,896]{1,0:T(8,128)(2,1)S(1)} %reduce_sum.37), channel_id=1, replica_groups=mesh['dp'=2,'y'=4,'core'=2,'x'=4,'z'=8] {'dp','z'}, dimensions={0}, use_global_device_ids=true | all-gather | bytes 974848 | tf_op jit(solution)/shard_map/all_gather | solution.py:290
  165.4 4.2 %collective-permute-start = (bf16[2,128,896]{2,1,0:T(8,128)(2,1)S(1)}, bf16[2,128,896]{2,1,0:T(8,128)(2,1)S(1)}, u32[]{:S(2)}, u32[]{:S(2)}) collective-permute-start(bf16[2,128,896]{2,1,0:T(8,128)(2,1)S(1)} %bitcast.35), channel_id=1, source_target_pairs={{0,8},{8,16},{16,24},{24,0},{1,9},{9,17},{17,25},{25,1},{2,10},{10... | collective-permute-start | bytes 1376264 | tf_op jit(solution)/shard_map/ppermute | solution.py:14
  171.6 5.1 %collective-permute-start.4 = (bf16[2,128,896]{2,1,0:T(8,128)(2,1)}, bf16[2,128,896]{2,1,0:T(8,128)(2,1)}, u32[]{:S(2)}, u32[]{:S(2)}) collective-permute-start(bf16[2,128,896]{2,1,0:T(8,128)(2,1)} %bitcast.16.refs_5_), channel_id=1, source_target_pairs={{0,8},{8,16},{16,24},{24,0},{1,9},{9,17},{17,25},{25,1},{2,10},{10... | collective-permute-start | bytes 1376264 | tf_op jit(solution)/shard_map/ppermute | solution.py:14
  176.7 4.0 %collective-permute-done.left.refs_1_ = bf16[2,128,896]{2,1,0:T(8,128)(2,1)S(1)} collective-permute-done((bf16[2,128,896]{2,1,0:T(8,128)(2,1)S(1)}, bf16[2,128,896]{2,1,0:T(8,128)(2,1)S(1)}, u32[]{:S(2)}, u32[]{:S(2)}) %collective-permute-start) | collective-permute-done | bytes 458784 | tf_op jit(solution)/shard_map/ppermute | solution.py:14
  180.7 5.5 %collective-permute-start.2 = (bf16[128,896]{1,0:T(8,128)(2,1)S(1)}, bf16[128,896]{1,0:T(8,128)(2,1)}, u32[]{:S(2)}, u32[]{:S(2)}) collective-permute-start(bf16[128,896]{1,0:T(8,128)(2,1)S(1)} %slice_bitcast_fusion.3), channel_id=1, source_target_pairs={{0,8},{8,16},{16,24},{24,0},{1,9},{9,17},{17,25},{25,1},{2,10},{10... | collective-permute-start | bytes 688136 | tf_op jit(solution)/shard_map/ppermute | solution.py:14
  188.1 2.1 collective-permute-start.5
  190.6 4.9 %collective-permute-done.3.far_high.refs_4_ = bf16[128,896]{1,0:T(8,128)(2,1)} collective-permute-done((bf16[128,896]{1,0:T(8,128)(2,1)S(1)}, bf16[128,896]{1,0:T(8,128)(2,1)}, u32[]{:S(2)}, u32[]{:S(2)}) %collective-permute-start.3) | collective-permute-done | bytes 229408 | tf_op jit(solution)/shard_map/ppermute | solution.py:14
  195.5 7.4 %input_term.1 = bf16[1024,512]{1,0:T(8,128)(2,1)} custom-call(s32[6]{0:T(128)} %stack.27.order_ref, bf16[2,128,896]{2,1,0:T(8,128)(2,1)} %bitcast.37, bf16[2,128,896]{2,1,0:T(8,128)(2,1)} %copy-done.3, bf16[2,128,896]{2,1,0:T(8,128)(2,1)} %copy-done.4, bf16[128,896]{1,0:T(8,128)(2,1)} %collective-permute-done.2.far_low.refs_3_, ...), custom_call_target="tpu_custom_call" | custom-call | flops 1744830464 | bytes 7864320 | tf_op jit(solution)/shard_map/input_term/pallas_call | solution.py:147
  202.9 3.5 %all-to-all-start.3 = ((bf16[8,128,512]{2,1,0:T(8,128)(2,1)}), bf16[8,128,512]{2,1,0:T(8,128)(2,1)S(1)}, u32[]{:S(2)}, u32[]{:S(2)}) async-start(bf16[8,128,512]{2,1,0:T(8,128)(2,1)} %bitcast.34), calls=%async_computation.3 | async-start | bytes 2097152 | tf_op jit(solution)/shard_map/all_to_all | solution.py:24
  207.4 2.6 %collective-permute-start.6 = (bf16[128,896]{1,0:T(8,128)(2,1)S(1)}, bf16[128,896]{1,0:T(8,128)(2,1)S(1)}, u32[]{:S(2)}, u32[]{:S(2)}) collective-permute-start(bf16[128,896]{1,0:T(8,128)(2,1)S(1)} %slice_bitcast_fusion.1), channel_id=1, source_target_pairs={{0,8},{8,16},{16,24},{24,0},{1,9},{9,17},{17,25},{25,1},{2,10},{10... | collective-permute-start | bytes 688136 | tf_op jit(solution)/shard_map/ppermute | solution.py:14
  210.9 3.2 %collective-permute-start.7 = (bf16[128,896]{1,0:T(8,128)(2,1)S(1)}, bf16[128,896]{1,0:T(8,128)(2,1)}, u32[]{:S(2)}, u32[]{:S(2)}) collective-permute-start(bf16[128,896]{1,0:T(8,128)(2,1)S(1)} %slice_bitcast_fusion), channel_id=1, source_target_pairs={{0,24},{8,0},{16,8},{24,16},{1,25},{9,1},{17,9},{25,17},{2,26},{10... | collective-permute-start | bytes 688136 | tf_op jit(solution)/shard_map/ppermute | solution.py:14
  214.2 2.5 %collective-permute-done.6.refs_8_ = bf16[128,896]{1,0:T(8,128)(2,1)S(1)} collective-permute-done((bf16[128,896]{1,0:T(8,128)(2,1)S(1)}, bf16[128,896]{1,0:T(8,128)(2,1)S(1)}, u32[]{:S(2)}, u32[]{:S(2)}) %collective-permute-start.6) | collective-permute-done | bytes 229408 | tf_op jit(solution)/shard_map/ppermute | solution.py:14
  216.7 4.9 %collective-permute-done.7.refs_9_ = bf16[128,896]{1,0:T(8,128)(2,1)} collective-permute-done((bf16[128,896]{1,0:T(8,128)(2,1)S(1)}, bf16[128,896]{1,0:T(8,128)(2,1)}, u32[]{:S(2)}, u32[]{:S(2)}) %collective-permute-start.7) | collective-permute-done | bytes 229408 | tf_op jit(solution)/shard_map/ppermute | solution.py:14
  221.5 13.7 %weight_grads.1 = (bf16[832,256]{1,0:T(8,128)(2,1)}, bf16[832,256]{1,0:T(8,128)(2,1)}, bf16[416,512]{1,0:T(8,128)(2,1)}) custom-call(s32[6]{0:T(128)} %stack.27.order_ref, s32[4]{0:T(128)} %assignment_ref.3, s32[8]{0:T(128)} %lengths_ref.3, bf16[2,128,896]{2,1,0:T(8,128)(2,1)} %bitcast.38, bf16[2,128,896]{2,1,0:T(8,128)(2,1)} %copy-done.3, ...), custom_call_target="tpu_custom_call" | custom-call | flops 3489660928 | bytes 13369344 | tf_op jit(solution)/shard_map/weight_grads/pallas_call | solution.py:221
  (41 shorter events, 13.9 us)
Async XLA Ops:
  7.2 188.3 %all-gather.3.cloned.1.call-start = ((), (), s32[]{:S(2)}) async-start(), calls=%async_computation.5 | async-start | bytes 6922240 | tf_op jit(solution)/shard_map/all_gather | solution.py:279
  10.8 19.4 %all-to-all-start = ((bf16[8,128,512]{2,1,0:T(8,128)(2,1)}), bf16[8,128,512]{2,1,0:T(8,128)(2,1)S(1)}, u32[]{:S(2)}, u32[]{:S(2)}) async-start(bf16[8,128,512]{2,1,0:T(8,128)(2,1)} %broadcast_in_dim.6), calls=%async_computation | async-start | bytes 2097152 | tf_op jit(solution)/shard_map/all_to_all | solution.py:19
  30.1 1.0 copy-start.1
  65.6 9.8 %copy-start.7 = (bf16[128,512]{1,0:T(8,128)(2,1)S(1)}, bf16[128,512]{1,0:T(8,128)(2,1)}, u32[]{:S(2)}) copy-start(bf16[128,512]{1,0:T(8,128)(2,1)} %param.9) | copy-start | bytes 393220
  65.6 9.8 %copy-start.5 = (bf16[128,512]{1,0:T(8,128)(2,1)S(1)}, bf16[128,512]{1,0:T(8,128)(2,1)}, u32[]{:S(2)}) copy-start(bf16[128,512]{1,0:T(8,128)(2,1)} %param.10) | copy-start | bytes 393220
  66.8 50.6 %all-to-all-start.2 = ((bf16[8,32,896]{2,1,0:T(8,128)(2,1)}), bf16[8,32,896]{2,1,0:T(8,128)(2,1)S(1)}, u32[]{:S(2)}, u32[]{:S(2)}) async-start(bf16[8,32,896]{2,1,0:T(8,128)(2,1)} %bitcast.7), calls=%async_computation.2 | async-start | bytes 917504 | tf_op jit(solution)/shard_map/all_to_all | solution.py:24
  75.4 20.8 %collective-permute-start.8 = (bf16[128,768]{1,0:T(8,128)(2,1)S(1)}, bf16[128,768]{1,0:T(8,128)(2,1)S(1)}, u32[]{:S(2)}, u32[]{:S(2)}) collective-permute-start(bf16[128,768]{1,0:T(8,128)(2,1)S(1)} %pad_maximum_fusion.1), channel_id=1, source_target_pairs={{0,256},{256,0},{1,257},{257,1},{2,258},{258,2},{3,259},{259,3},{4... | collective-permute-start | bytes 589832 | tf_op jit(solution)/shard_map/ppermute | solution.py:14
  119.1 83.8 %all-to-all-start.4 = ((bf16[8,128,1024]{2,1,0:T(8,128)(2,1)}), bf16[8,128,1024]{2,1,0:T(8,128)(2,1)S(1)}, u32[]{:S(2)}, u32[]{:S(2)}) async-start(bf16[8,128,1024]{2,1,0:T(8,128)(2,1)} %broadcast_in_dim.8), calls=%async_computation.4 | async-start | bytes 4194304 | tf_op jit(solution)/shard_map/all_to_all | solution.py:19
  165.4 30.1 %copy-start.2 = (bf16[1,256,896]{2,1,0:T(8,128)(2,1)}, bf16[1,256,896]{2,1,0:T(8,128)(2,1)S(1)}, u32[]{:S(2)}) copy-start(bf16[1,256,896]{2,1,0:T(8,128)(2,1)S(1)} %get-tuple-element.13) | copy-start | bytes 1376260
  165.4 15.3 %collective-permute-start = (bf16[2,128,896]{2,1,0:T(8,128)(2,1)S(1)}, bf16[2,128,896]{2,1,0:T(8,128)(2,1)S(1)}, u32[]{:S(2)}, u32[]{:S(2)}) collective-permute-start(bf16[2,128,896]{2,1,0:T(8,128)(2,1)S(1)} %bitcast.35), channel_id=1, source_target_pairs={{0,8},{8,16},{16,24},{24,0},{1,9},{9,17},{17,25},{25,1},{2,10},{10... | collective-permute-start | bytes 1376264 | tf_op jit(solution)/shard_map/ppermute | solution.py:14
  169.6 16.5 %collective-permute-start.1 = (bf16[2,128,896]{2,1,0:T(8,128)(2,1)S(1)}, bf16[2,128,896]{2,1,0:T(8,128)(2,1)S(1)}, u32[]{:S(2)}, u32[]{:S(2)}) collective-permute-start(bf16[2,128,896]{2,1,0:T(8,128)(2,1)S(1)} %bitcast.36), channel_id=1, source_target_pairs={{0,24},{8,0},{16,8},{24,16},{1,25},{9,1},{17,9},{25,17},{2,26},{10... | collective-permute-start | bytes 1376264 | tf_op jit(solution)/shard_map/ppermute | solution.py:14
  171.6 34.8 %collective-permute-start.4 = (bf16[2,128,896]{2,1,0:T(8,128)(2,1)}, bf16[2,128,896]{2,1,0:T(8,128)(2,1)}, u32[]{:S(2)}, u32[]{:S(2)}) collective-permute-start(bf16[2,128,896]{2,1,0:T(8,128)(2,1)} %bitcast.16.refs_5_), channel_id=1, source_target_pairs={{0,8},{8,16},{16,24},{24,0},{1,9},{9,17},{17,25},{25,1},{2,10},{10... | collective-permute-start | bytes 1376264 | tf_op jit(solution)/shard_map/ppermute | solution.py:14
  180.7 14.8 %copy-start.3 = (bf16[2,128,896]{2,1,0:T(8,128)(2,1)}, bf16[2,128,896]{2,1,0:T(8,128)(2,1)S(1)}, u32[]{:S(2)}) copy-start(bf16[2,128,896]{2,1,0:T(8,128)(2,1)S(1)} %collective-permute-done.left.refs_1_) | copy-start | bytes 1376260
  180.7 9.9 %collective-permute-start.2 = (bf16[128,896]{1,0:T(8,128)(2,1)S(1)}, bf16[128,896]{1,0:T(8,128)(2,1)}, u32[]{:S(2)}, u32[]{:S(2)}) collective-permute-start(bf16[128,896]{1,0:T(8,128)(2,1)S(1)} %slice_bitcast_fusion.3), channel_id=1, source_target_pairs={{0,8},{8,16},{16,24},{24,0},{1,9},{9,17},{17,25},{25,1},{2,10},{10... | collective-permute-start | bytes 688136 | tf_op jit(solution)/shard_map/ppermute | solution.py:14
  186.2 9.3 %copy-start.4 = (bf16[2,128,896]{2,1,0:T(8,128)(2,1)}, bf16[2,128,896]{2,1,0:T(8,128)(2,1)S(1)}, u32[]{:S(2)}) copy-start(bf16[2,128,896]{2,1,0:T(8,128)(2,1)S(1)} %collective-permute-done.1.right.refs_2_) | copy-start | bytes 1376260
  186.2 9.2 %collective-permute-start.3 = (bf16[128,896]{1,0:T(8,128)(2,1)S(1)}, bf16[128,896]{1,0:T(8,128)(2,1)}, u32[]{:S(2)}, u32[]{:S(2)}) collective-permute-start(bf16[128,896]{1,0:T(8,128)(2,1)S(1)} %slice_bitcast_fusion.2), channel_id=1, source_target_pairs={{0,24},{8,0},{16,8},{24,16},{1,25},{9,1},{17,9},{25,17},{2,26},{10... | collective-permute-start | bytes 688136 | tf_op jit(solution)/shard_map/ppermute | solution.py:14
  188.1 21.8 %collective-permute-start.5 = (bf16[2,128,896]{2,1,0:T(8,128)(2,1)}, bf16[2,128,896]{2,1,0:T(8,128)(2,1)}, u32[]{:S(2)}, u32[]{:S(2)}) collective-permute-start(bf16[2,128,896]{2,1,0:T(8,128)(2,1)} %bitcast.16.refs_5_), channel_id=1, source_target_pairs={{0,24},{8,0},{16,8},{24,16},{1,25},{9,1},{17,9},{25,17},{2,26},{10... | collective-permute-start | bytes 1376264 | tf_op jit(solution)/shard_map/ppermute | solution.py:14
  202.9 18.7 %copy-start = (bf16[8,128,1024]{2,1,0:T(8,128)(2,1)}, bf16[8,128,1024]{2,1,0:T(8,128)(2,1)S(1)}, u32[]{:S(2)}) copy-start(bf16[8,128,1024]{2,1,0:T(8,128)(2,1)S(1)} %all-to-all-done.4) | copy-start | bytes 6291460
  202.9 32.4 %all-to-all-start.3 = ((bf16[8,128,512]{2,1,0:T(8,128)(2,1)}), bf16[8,128,512]{2,1,0:T(8,128)(2,1)S(1)}, u32[]{:S(2)}, u32[]{:S(2)}) async-start(bf16[8,128,512]{2,1,0:T(8,128)(2,1)} %bitcast.34), calls=%async_computation.3 | async-start | bytes 2097152 | tf_op jit(solution)/shard_map/all_to_all | solution.py:24
  207.4 9.3 %collective-permute-start.6 = (bf16[128,896]{1,0:T(8,128)(2,1)S(1)}, bf16[128,896]{1,0:T(8,128)(2,1)S(1)}, u32[]{:S(2)}, u32[]{:S(2)}) collective-permute-start(bf16[128,896]{1,0:T(8,128)(2,1)S(1)} %slice_bitcast_fusion.1), channel_id=1, source_target_pairs={{0,8},{8,16},{16,24},{24,0},{1,9},{9,17},{17,25},{25,1},{2,10},{10... | collective-permute-start | bytes 688136 | tf_op jit(solution)/shard_map/ppermute | solution.py:14
  210.9 10.6 %collective-permute-start.7 = (bf16[128,896]{1,0:T(8,128)(2,1)S(1)}, bf16[128,896]{1,0:T(8,128)(2,1)}, u32[]{:S(2)}, u32[]{:S(2)}) collective-permute-start(bf16[128,896]{1,0:T(8,128)(2,1)S(1)} %slice_bitcast_fusion), channel_id=1, source_target_pairs={{0,24},{8,0},{16,8},{24,16},{1,25},{9,1},{17,9},{25,17},{2,26},{10... | collective-permute-start | bytes 688136 | tf_op jit(solution)/shard_map/ppermute | solution.py:14
  216.7 4.9 %copy-start.6 = (bf16[128,896]{1,0:T(8,128)(2,1)}, bf16[128,896]{1,0:T(8,128)(2,1)S(1)}, u32[]{:S(2)}) copy-start(bf16[128,896]{1,0:T(8,128)(2,1)S(1)} %collective-permute-done.6.refs_8_) | copy-start | bytes 688132
Sparse Core Ops, SparseCore 0:
  11.5 172.9 all-gather.2
